TPU v7x, 128 devices: a whole 4x4x4 slice. The times are simulated.
128 devices in a mesh: row: 16 (over y, x), col: 8 (over z, core).
Axes of the slice: x: 4, y: 4, z: 4, core: 2. Of those that a mesh axis runs over, the one named last changes fastest.
Arguments:
- owned_rows: bfloat16 [3072, 8192], P(('row', 'col')), may hold values from -6 to 6
- suffix_lengths: int32 [128], replicated, may hold values from 1 to 24, 1024 in all
- owner_map: int32 [128], replicated, may hold values from 0 to 127, each once
- prefix_lengths: int32 [128], replicated, may hold values from 0 to 4095
- gate_weight: bfloat16 [8192, 29568], P('row', 'col'), may hold values from -0.0625 to 0.0625
- up_weight: bfloat16 [8192, 29568], P('row', 'col'), may hold values from -0.0625 to 0.0625
- down_weight: bfloat16 [29568, 8192], P('col', 'row'), may hold values from -0.03125 to 0.03125
Outputs:
- mixed: bfloat16 [1024, 8192], P('col', 'row')
Inputs may be any that keep to these rules, and one draw needn't show every extreme that they name: `suffix_lengths`: the lengths add up to 1024; the largest is exactly 24. `owner_map`: each device owns one request; request r's suffix rows fill, in order, the first suffix_lengths[r] of the 24 slots of its owner in owned_rows, and the other slots are not used.
All inputs are finite; a program needn't handle non-finite values.
Results may differ from a plain program's by a relative error of at most 0.0049.
Values may be sent and summed in bfloat16 or wider, within the bound.
No kernel may reach another device: no remote copies, remote signals or barrier semaphores. Data moves between devices by JAX's collectives and lax.ppermute only.
A program may use at most 128 MiB of HBM per device.

v0:
```python
import jax
import jax.numpy as jnp
from jax import lax
from jax.sharding import PartitionSpec as P

TOK_DEV = 8


def source_rows(suffix_lengths, owner_map, prefix_lengths, row_count, slot_size):
    request_ids = jnp.arange(suffix_lengths.shape[0], dtype=jnp.int32)
    longer = prefix_lengths[None, :] > prefix_lengths[:, None]
    earlier = (prefix_lengths[None, :] == prefix_lengths[:, None]) & (
        request_ids[None, :] < request_ids[:, None]
    )
    starts = jnp.sum(jnp.where(longer | earlier, suffix_lengths[None, :], 0), axis=1)
    positions = jnp.arange(row_count, dtype=jnp.int32)
    ends = starts + suffix_lengths
    inside = (positions[:, None] >= starts[None, :]) & (positions[:, None] < ends[None, :])
    offsets = owner_map * slot_size - starts
    shifted = jnp.sum(jnp.where(inside, offsets[None, :], 0), axis=1)
    return positions + shifted


def on_device(
    owned_rows, suffix_lengths, owner_map, prefix_lengths, gate_weight, up_weight, down_weight
):
    slot_size = owned_rows.shape[0]
    total_rows = TOK_DEV * suffix_lengths.shape[0]
    source = source_rows(suffix_lengths, owner_map, prefix_lengths, total_rows, slot_size)
    gathered = lax.all_gather(owned_rows, "col", axis=0, tiled=True)
    feature_rows = lax.all_to_all(gathered, "row", split_axis=1, concat_axis=0, tiled=True)
    suffix_rows = jnp.take(feature_rows, source, axis=0)
    block_rows = suffix_rows
    gate_share = lax.psum_scatter(
        jnp.dot(block_rows, gate_weight, preferred_element_type=jnp.float32),
        "row",
        scatter_dimension=0,
        tiled=True,
    )
    block_rows = suffix_rows
    up_share = lax.psum_scatter(
        jnp.dot(block_rows, up_weight, preferred_element_type=jnp.float32),
        "row",
        scatter_dimension=0,
        tiled=True,
    )
    hidden_share = (jax.nn.silu(gate_share) * up_share).astype(jnp.bfloat16)
    partial_sums = jnp.dot(
        lax.all_gather(hidden_share, "row", axis=0, tiled=True),
        down_weight,
        preferred_element_type=jnp.float32,
    )
    return lax.psum_scatter(partial_sums, "col", scatter_dimension=0, tiled=True).astype(
        jnp.bfloat16
    )


def solution(mesh):
    return jax.shard_map(
        on_device,
        mesh=mesh,
        in_specs=(
            P(("row", "col"), None),
            P(),
            P(),
            P(),
            P("row", "col"),
            P("row", "col"),
            P("col", "row"),
        ),
        out_specs=P("col", "row"),
        check_vma=False,
    )
```

profile of v0, /device:TPU:0, one launch (start us, length us, event | category | flops | bytes accessed | tf_op | source)
XLA Modules:
  0.0 444.5 jit_solution(16864953255005129052)
XLA Ops:
  6.5 0.0 all-gather.3.cloned.1.call-start
  6.5 0.7 all-gather.3.cloned.1.call-update
  7.3 32.2 %all-gather.3.cloned.1.call-done = bf16[192,8192]{1,0:T(8,128)(2,1)} async-done(((bf16[24,8192]{1,0:T(8,128)(2,1)}), bf16[192,8192]{1,0:T(8,128)(2,1)}) %all-gather.3.cloned.1.call-update) | async-done | bytes 3145744 | tf_op jit(solution)/shard_map/all_gather | solution.py:30
  39.5 3.9 copy.13
  43.4 0.0 copy-start.1
  43.4 0.0 copy-start.2
  43.4 0.0 copy-start.3
  43.4 6.9 %all-to-all-start = ((bf16[192,16,512]{2,0,1:T(8,128)(2,1)}), bf16[192,16,512]{2,0,1:T(8,128)(2,1)S(1)}, u32[]{:S(2)}, u32[]{:S(2)}) async-start(bf16[192,16,512]{2,0,1:T(8,128)(2,1)} %bitcast.14), calls=%async_computation | async-start | bytes 6291456 | tf_op jit(solution)/shard_map/all_to_all | solution.py:31
  50.3 0.0 reduce-scatter.6.cloned.1.call-start
  50.4 0.0 copy-done.1
  50.4 0.0 copy-done.2
  50.4 0.2 select_reduce_fusion.1
  50.6 0.0 copy-done.3
  50.6 0.2 select_reduce_fusion
  50.8 48.1 %all-to-all-done = bf16[192,16,512]{2,0,1:T(8,128)(2,1)S(1)} async-done(((bf16[192,16,512]{2,0,1:T(8,128)(2,1)}), bf16[192,16,512]{2,0,1:T(8,128)(2,1)S(1)}, u32[]{:S(2)}, u32[]{:S(2)}) %all-to-all-start) | async-done | bytes 3145760 | tf_op jit(solution)/shard_map/all_to_all | solution.py:31
  98.9 5.0 %gather_fusion = bf16[1024,512]{1,0:T(8,128)(2,1)} fusion(bf16[3072,512]{1,0:T(8,128)(2,1)S(1)} %bitcast.13, s32[1024]{0:T(1024)S(1)} %broadcast_clamp_fusion), kind=kCustom, calls=%fused_computation | custom fusion | bytes 2101248 | tf_op jit(solution)/shard_map/jit(_take)/gather | solution.py:32
  104.0 12.0 %fusion.1 = f32[1024,3696]{1,0:T(8,128)} fusion(bf16[512,3696]{0,1:T(8,128)(2,1)} %param.12, bf16[1024,512]{1,0:T(8,128)(2,1)} %gather_fusion, pred[1024]{0:T(1024)(128)(4,1)S(1)} %compare_and_fusion), kind=kOutput, calls=%fused_computation.8 | convolution fusion | flops 3876061184 | bytes 19973120 | tf_op jit(solution)/shard_map/dot_general | solution.py:42
  116.0 0.0 copy-start
  116.0 0.0 reduce-scatter.6.cloned.1.call-update
  116.0 0.0 reduce-scatter.4.cloned.1.call-start
  116.1 1.1 copy-done
  117.2 10.0 %fusion.2 = f32[1024,3696]{1,0:T(8,128)} fusion(bf16[512,3696]{0,1:T(8,128)(2,1)} %param.11, bf16[1024,512]{1,0:T(8,128)(2,1)S(1)} %copy-done, pred[1024]{0:T(1024)(128)(4,1)S(1)} %compare_and_fusion), kind=kOutput, calls=%fused_computation.9 | convolution fusion | flops 3876061184 | bytes 19973120 | tf_op jit(solution)/shard_map/dot_general | solution.py:35
  127.2 0.0 reduce-scatter.4.cloned.1.call-update
  127.2 0.0 all-gather.5.cloned.1.call-start
  127.3 90.2 %reduce-scatter.6.cloned.1.call-done = f32[64,3696]{1,0:T(8,128)} async-done(((f32[1024,3696]{1,0:T(8,128)}), f32[64,3696]{1,0:T(8,128)}) %reduce-scatter.6.cloned.1.call-update) | async-done | bytes 946192 | tf_op jit(solution)/shard_map/reduce_scatter | solution.py:41
  217.5 106.2 %reduce-scatter.4.cloned.1.call-done = f32[64,3696]{1,0:T(8,128)} async-done(((f32[1024,3696]{1,0:T(8,128)}), f32[64,3696]{1,0:T(8,128)}) %reduce-scatter.4.cloned.1.call-update) | async-done | bytes 946192 | tf_op jit(solution)/shard_map/reduce_scatter | solution.py:34
  323.7 2.5 multiply_convert_fusion
  326.2 0.0 all-gather.5.cloned.1.call-update
  326.2 0.0 reduce-scatter.8.cloned.1.call-start
  326.3 66.2 %all-gather.5.cloned.1.call-done = bf16[1024,3696]{1,0:T(8,128)(2,1)} async-done(((bf16[64,3696]{1,0:T(8,128)(2,1)}), bf16[1024,3696]{1,0:T(8,128)(2,1)}) %all-gather.5.cloned.1.call-update) | async-done | bytes 7569424 | tf_op jit(solution)/shard_map/all_gather | solution.py:49
  392.5 9.8 %fusion.8 = f32[1024,512]{1,0:T(8,128)} fusion(bf16[1024,3696]{1,0:T(8,128)(2,1)} %all-gather.5.cloned.1.call-done, bf16[3696,512]{1,0:T(8,128)(2,1)} %param.13), kind=kOutput, calls=%fused_computation.22 | convolution fusion | flops 3875536896 | bytes 13451264 | tf_op jit(solution)/shard_map/dot_general | solution.py:48
  402.3 0.0 reduce-scatter.8.cloned.1.call-update
  402.3 34.0 %reduce-scatter.8.cloned.1.call-done = f32[128,512]{1,0:T(8,128)} async-done(((f32[1024,512]{1,0:T(8,128)}), f32[128,512]{1,0:T(8,128)}) %reduce-scatter.8.cloned.1.call-update) | async-done | bytes 262160 | tf_op jit(solution)/shard_map/reduce_scatter | solution.py:53
  436.3 1.6 convert_element_type.7
  (4 shorter events, 0.0 us)
Async XLA Ops:
  6.5 32.9 %all-gather.3.cloned.1.call-start = ((), (), s32[]{:S(2)}) async-start(), calls=%async_computation.4 | async-start | bytes 3538944 | tf_op jit(solution)/shard_map/all_gather | solution.py:30
  43.4 7.0 %copy-start.1 = (s32[128]{0:T(128)S(1)}, s32[128]{0:T(128)}, u32[]{:S(2)}) copy-start(s32[128]{0:T(128)} %param.10) | copy-start | bytes 1540
  43.4 7.0 %copy-start.2 = (s32[128]{0:T(128)S(1)}, s32[128]{0:T(128)}, u32[]{:S(2)}) copy-start(s32[128]{0:T(128)} %param.8) | copy-start | bytes 1540
  43.4 7.2 %copy-start.3 = (s32[128]{0:T(128)S(1)}, s32[128]{0:T(128)}, u32[]{:S(2)}) copy-start(s32[128]{0:T(128)} %param.9) | copy-start | bytes 1540
  43.4 55.6 %all-to-all-start = ((bf16[192,16,512]{2,0,1:T(8,128)(2,1)}), bf16[192,16,512]{2,0,1:T(8,128)(2,1)S(1)}, u32[]{:S(2)}, u32[]{:S(2)}) async-start(bf16[192,16,512]{2,0,1:T(8,128)(2,1)} %bitcast.14), calls=%async_computation | async-start | bytes 6291456 | tf_op jit(solution)/shard_map/all_to_all | solution.py:31
  50.3 167.1 %reduce-scatter.6.cloned.1.call-start = ((), (), s32[]{:S(2)}) async-start(), calls=%async_computation.6 | async-start | bytes 16154624 | tf_op jit(solution)/shard_map/reduce_scatter | solution.py:41
  116.0 1.2 copy-start
  116.0 207.6 %reduce-scatter.4.cloned.1.call-start = ((), (), s32[]{:S(2)}) async-start(), calls=%async_computation.5 | async-start | bytes 16154624 | tf_op jit(solution)/shard_map/reduce_scatter | solution.py:34
  127.2 265.2 %all-gather.5.cloned.1.call-start = ((), (), s32[]{:S(2)}) async-start(), calls=%async_computation.7 | async-start | bytes 8077312 | tf_op jit(solution)/shard_map/all_gather | solution.py:49
  326.2 110.1 %reduce-scatter.8.cloned.1.call-start = ((), (), s32[]{:S(2)}) async-start(), calls=%async_computation.8 | async-start | bytes 2359296 | tf_op jit(solution)/shard_map/reduce_scatter | solution.py:53
Sparse Core Ops, SparseCore 0:
  9.0 30.3 all-gather.2
  116.2 101.2 reduce-scatter.5
  220.9 102.7 reduce-scatter.3
  326.4 66.0 all-gather.4
  402.5 33.8 reduce-scatter.7
where the time goes:
time: 445 us; the launch traced here: 444 us
  waiting for transfers between devices  378 us (85%)
  matrix products  31.9 us (7%)
  between operations  13.2 us (3%)
  local copies, waits for them, and re-layouts  10.1 us (2%)
  starting transfers between devices  7.11 us (2%)
  other arithmetic  4.55 us (1%)
    reduce_scatter x1, waiting for transfers between devices, on_device(): lax.psum_scatter(jnp.dot(block_rows, gate_weight, preferred_element_type=...  106 us
    reduce_scatter x1, waiting for transfers between devices, on_device(): lax.psum_scatter(jnp.dot(block_rows, up_weight, preferred_element_type=jn...  90.2 us
    all_gather x1, waiting for transfers between devices, on_device(): lax.all_gather(hidden_share, 'row', axis=0, tiled=True)  66.2 us
    all_to_all x1, waiting for transfers between devices, on_device(): lax.all_to_all(gathered, 'row', split_axis=1, concat_axis=0, tiled=True)  48.1 us
    reduce_scatter x1, waiting for transfers between devices, on_device(): lax.psum_scatter(partial_sums, 'col', scatter_dimension=0, tiled=True)  34 us
    all_gather x1, waiting for transfers between devices, on_device(): gathered = lax.all_gather(owned_rows, 'col', axis=0, tiled=True)  32.2 us
    dot_general x1, matrix products, on_device(): jnp.dot(block_rows, up_weight, preferred_element_type=jnp.float32)  12 us
    dot_general x1, matrix products, on_device(): jnp.dot(block_rows, gate_weight, preferred_element_type=jnp.float32)  9.97 us
  transfers between devices with their start and end apart: 6, of which 6 were waited for; matrix products, arithmetic and copies ran while one was open for 2% of the time, Pallas kernels for 0%

commit v1 on v0

v1 whole, which is shorter than its diff:
```python
import jax
import jax.numpy as jnp
from jax import lax
from jax.experimental import pallas as pl
from jax.experimental.pallas import tpu as pltpu
from jax.sharding import Mesh, PartitionSpec as P

SIDE = 4
CORES = 2
SUB = 232
BLOCK = 2 * SUB
HALF = SIDE * BLOCK
TOK_DEV = 8
BF16 = jnp.bfloat16
F32 = jnp.float32


def shift(value, axis, by, size=SIDE):
    return lax.ppermute(value, axis, [(i, (i + by) % size) for i in range(size)])


def around(value, axis):
    return [value] + [shift(value, axis, by) for by in range(1, SIDE)]


def exchange(value, axis):
    return lax.all_to_all(value, axis, split_axis=0, concat_axis=0, tiled=True)


def source_rows(suffix_lengths, owner_map, prefix_lengths, positions):
    request_ids = jnp.arange(suffix_lengths.shape[0], dtype=jnp.int32)
    longer = prefix_lengths[None, :] > prefix_lengths[:, None]
    earlier = (prefix_lengths[None, :] == prefix_lengths[:, None]) & (
        request_ids[None, :] < request_ids[:, None]
    )
    starts = jnp.sum(jnp.where(longer | earlier, suffix_lengths[None, :], 0), axis=1)
    ends = starts + suffix_lengths
    inside = (positions[:, None] >= starts[None, :]) & (positions[:, None] < ends[None, :])
    row, col = owner_map // (SIDE * CORES), owner_map % (SIDE * CORES)
    z_behind = (lax.axis_index("z") - col // CORES) % SIDE
    other_core = (lax.axis_index("core") + col) % CORES
    slot = ((other_core * SIDE + z_behind) * SIDE * SIDE + row) * 24
    shifted = jnp.sum(jnp.where(inside, (slot - starts)[None, :], 0), axis=1)
    return positions + shifted


def partial_kernel(order_ref, own_ref, other_ref, x0, x1, x2, x3, out_ref):
    def products(weight_ref):
        total = None
        for behind, rows in enumerate((x0, x1, x2, x3)):
            term = lax.dot_general(
                weight_ref[order_ref[behind], 0],
                rows[...],
                (((1,), (1,)), ((), ())),
                preferred_element_type=F32,
            )
            total = term if total is None else total + term
        out_ref[0] = total.astype(BF16)

    @pl.when(pl.program_id(0) == 0)
    def _():
        products(own_ref)

    @pl.when(pl.program_id(0) == 1)
    def _():
        products(other_ref)


def partial_products(order, own, other, rows):
    features = own.shape[-1]
    whole = pl.BlockSpec(rows[0].shape, lambda c, s, order: (0, 0))
    return pl.pallas_call(
        partial_kernel,
        grid_spec=pltpu.PrefetchScalarGridSpec(
            num_scalar_prefetch=1,
            grid=(2, 2),
            in_specs=[
                pl.BlockSpec((SIDE, 1, BLOCK, features), lambda c, s, order: (0, s * (1 - c) + c, 0, 0)),
                pl.BlockSpec((SIDE, 1, BLOCK, features), lambda c, s, order: (0, s * c, 0, 0)),
            ]
            + [whole] * SIDE,
            out_specs=pl.BlockSpec((1, BLOCK, rows[0].shape[0]), lambda c, s, order: (2 * c + s, 0, 0)),
        ),
        out_shape=jax.ShapeDtypeStruct((SIDE, BLOCK, rows[0].shape[0]), BF16),
    )(order, own, other, *rows)


def hidden_kernel(parts_ref, out_ref):
    total = parts_ref[0].astype(F32)
    for i in range(1, SIDE):
        total = total + parts_ref[i].astype(F32)
    gate, up = total[:SUB], total[SUB:]
    out_ref[...] = (gate / (1.0 + jnp.exp(-gate)) * up).astype(BF16)


def hidden_rows(parts):
    return pl.pallas_call(
        hidden_kernel,
        out_shape=jax.ShapeDtypeStruct((SUB, parts.shape[-1]), BF16),
    )(parts)


def down_kernel(*refs):
    out_ref, weights, hiddens = refs[-1], refs[:2], refs[2:-1]
    total = None
    for half in range(2):
        for behind in range(SIDE):
            hidden = hiddens[half * SIDE + behind]
            for i in range(SIDE):
                term = lax.dot_general(
                    hidden[i],
                    weights[half][behind, i],
                    (((0,), (0,)), ((), ())),
                    preferred_element_type=F32,
                )
                total = term if total is None else total + term
    out_ref[...] = total


def down_products(weights, hiddens):
    tokens, features = hiddens[0].shape[-1], weights[0].shape[-1]
    return pl.pallas_call(
        down_kernel,
        out_shape=jax.ShapeDtypeStruct((tokens, features), F32),
    )(*weights, *hiddens)


def on_device(
    owned_rows, suffix_lengths, owner_map, prefix_lengths, gate_weight, up_weight, down_weight
):
    slots = owned_rows.shape[0]
    features = gate_weight.shape[0]
    x, y = lax.axis_index("x"), lax.axis_index("y")
    core = lax.axis_index("core")
    behind = jnp.arange(SIDE, dtype=jnp.int32)
    x_order, y_order = (x - behind) % SIDE, (y - behind) % SIDE

    pad = ((0, 2 * HALF - gate_weight.shape[1]), (0, 0))
    gate, up = jnp.pad(gate_weight.T, pad), jnp.pad(up_weight.T, pad)

    def halves(weight):
        return weight.reshape(2, SIDE, 2, SUB, features)

    both = jnp.concatenate([halves(gate), halves(up)], axis=3)
    own_x, own_y = exchange(both[0], "x"), exchange(both[1], "y")
    other_x, other_y = shift(own_x, "core", 1, 2), shift(own_y, "core", 1, 2)

    down = jnp.pad(down_weight, pad).reshape(2, SIDE, 2, SUB, features)
    down = jnp.concatenate([down, shift(down, "core", 1, 2)], axis=2)
    down_x = jnp.take(jnp.take(down[0], x_order, axis=0), y_order, axis=1)
    down_y = jnp.take(jnp.take(down[1], y_order, axis=0), x_order, axis=1)

    blocks = owned_rows.reshape(slots, SIDE * SIDE, features).transpose(1, 0, 2)
    feature_rows = exchange(blocks, ("y", "x")).reshape(-1, features)
    near = jnp.concatenate(around(feature_rows, "z"), axis=0)
    every = jnp.concatenate([near, shift(near, "core", 1, 2)], axis=0)
    place = jnp.arange(TOK_DEV * suffix_lengths.shape[0] // CORES, dtype=jnp.int32)
    positions = (place // 128 * CORES + core) * 128 + place % 128
    source = source_rows(suffix_lengths, owner_map, prefix_lengths, positions)
    rows = every.at[source].get(mode="promise_in_bounds")

    part_x = partial_products(x_order, own_x, other_x, around(rows, "x"))
    part_y = partial_products(y_order, own_y, other_y, around(rows, "y"))
    hidden_x = hidden_rows(exchange(part_x, "y"))
    hidden_y = hidden_rows(exchange(part_y, "x"))

    all_x = around(jnp.stack(around(hidden_x, "y")), "x")
    all_y = around(jnp.stack(around(hidden_y, "x")), "y")
    partial_sums = down_products([down_x, down_y], all_x + all_y)
    parts = exchange(partial_sums.reshape(SIDE, -1, features), "z")
    return jnp.sum(parts, axis=0).astype(BF16)


def solution(mesh):
    torus = Mesh(mesh.devices.reshape(SIDE, SIDE, SIDE, CORES), ("y", "x", "z", "core"))
    row, col = ("y", "x"), ("z", "core")
    return jax.shard_map(
        on_device,
        mesh=torus,
        in_specs=(P(row + col, None), P(), P(), P(), P(row, col), P(row, col), P(col, row)),
        out_specs=P(col, row),
        check_vma=False,
    )
```

time: 445 us -> 367 us (0.82)
  waiting for transfers between devices: 378 us -> 142 us
  blocking collectives: 0 us -> 65.6 us
  starting transfers between devices: 7.11 us -> 52.8 us
  Pallas kernels: 0 us -> 35.1 us
  matrix products: 31.9 us -> 0 us
  local copies, waits for them, and re-layouts: 10.1 us -> 39.9 us
  other arithmetic: 4.55 us -> 27.1 us
  between operations: 13.2 us -> 0.29 us
    reduce_scatter x3 -> x0, waiting for transfers between devices: 230 us -> none  [the longest x1 106 us: on_device(): lax.psum_scatter(jnp.dot(block_rows, gate_weight, preferred_element_type=...]
    ppermute x0 -> x25, waiting for transfers between devices: none -> 126 us  [shift(): lax.ppermute(value, axis, [(i, (i + by) % size) for i in range(size)])]
    all_gather x2 -> x0, waiting for transfers between devices: 98.4 us -> none  [the longest x1 66.2 us: on_device(): lax.all_gather(hidden_share, 'row', axis=0, tiled=True)]
    all_to_all x0 -> x2, blocking collectives: none -> 65.6 us  [exchange(): return lax.all_to_all(value, axis, split_axis=0, concat_axis=0, tiled=True)]
    pallas_call x0 -> x5, Pallas kernels: none -> 35.1 us  [the longest x2 19 us: partial_products(): pl.pallas_call(partial_kernel, grid_spec=pltpu.PrefetchScalarGridSpec(num...]
    ppermute x0 -> x25, starting transfers between devices: none -> 33.5 us  [shift(): lax.ppermute(value, axis, [(i, (i + by) % size) for i in range(size)])]
    dot_general x3 -> x0, matrix products: 31.9 us -> none  [the longest x1 12 us: on_device(): jnp.dot(block_rows, up_weight, preferred_element_type=jnp.float32)]
    all_to_all x1 -> x4, waiting for transfers between devices: 48.1 us -> 16.2 us  [exchange(): return lax.all_to_all(value, axis, split_axis=0, concat_axis=0, tiled=True)]
  transfers between devices with their start and end apart: 6 -> 29, of which waited for: 6 -> 15; matrix products, arithmetic and copies ran while one was open for 2% -> 16% of each run, Pallas kernels for 0% -> 7%
where the time goes in v1:
time: 367 us; the launch traced here: 363 us
  waiting for transfers between devices  142 us (39%)
  blocking collectives  65.6 us (18%)
  starting transfers between devices  52.8 us (14%)
  local copies, waits for them, and re-layouts  39.9 us (11%)
  Pallas kernels  35.1 us (10%)
  other arithmetic  27.1 us (7%)
    ppermute x25, waiting for transfers between devices, shift(): lax.ppermute(value, axis, [(i, (i + by) % size) for i in range(size)])  126 us
    all_to_all x2, blocking collectives, exchange(): return lax.all_to_all(value, axis, split_axis=0, concat_axis=0, tiled=True)  65.6 us
    ppermute x25, starting transfers between devices, shift(): lax.ppermute(value, axis, [(i, (i + by) % size) for i in range(size)])  33.5 us
    all_to_all x4, starting transfers between devices, exchange(): return lax.all_to_all(value, axis, split_axis=0, concat_axis=0, tiled=True)  19.3 us
    pallas_call x2, Pallas kernels, partial_products(): pl.pallas_call(partial_kernel, grid_spec=pltpu.PrefetchScalarGridSpec(num...  19 us
    all_to_all x4, waiting for transfers between devices, exchange(): return lax.all_to_all(value, axis, split_axis=0, concat_axis=0, tiled=True)  16.2 us
    pallas_call x1, Pallas kernels, down_products(): pl.pallas_call(down_kernel, out_shape=jax.ShapeDtypeStruct((tokens, featu...  11 us
    gather x2, local copies, waits for them, and re-layouts, on_device(): down_y = jnp.take(jnp.take(down[1], y_order, axis=0), x_order, axis=1)  9.46 us
  transfers between devices with their start and end apart: 29, of which 15 were waited for; matrix products, arithmetic and copies ran while one was open for 16% of the time, Pallas kernels for 7%

profile of v1, /device:TPU:0, one launch (start us, length us, event | category | flops | bytes accessed | tf_op | source)
XLA Modules:
  0.0 363.1 jit_solution(7771060146872239441)
XLA Ops:
  0.0 1.8 copy.23
  1.8 7.1 %all-to-all-start.1 = ((bf16[16,24,512]{2,1,0:T(8,128)(2,1)}), bf16[16,24,512]{2,1,0:T(8,128)(2,1)S(1)}, u32[]{:S(2)}, u32[]{:S(2)}) async-start(bf16[16,24,512]{2,1,0:T(8,128)(2,1)} %bitcast.35), calls=%async_computation.1 | async-start | bytes 786432 | tf_op jit(solution)/shard_map/all_to_all | solution.py:27
  8.9 2.5 pad.11
  12.4 3.4 fusion.4
  15.8 3.2 all-to-all-done.1
  19.0 49.3 %all_to_all.30.own_ref = bf16[4,2,464,512]{3,2,1,0:T(8,128)(2,1)} all-to-all(bf16[4,2,464,512]{3,2,1,0:T(8,128)(2,1)} %get-tuple-element.6), channel_id=1, replica_groups=mesh['y'=4,'x'=4,'z'=4,'core'=2] {'y'}, dimensions={0} | all-to-all | bytes 7602176 | tf_op jit(solution)/shard_map/all_to_all | solution.py:27
  68.4 4.8 %all-to-all-start = ((bf16[4,2,464,512]{3,2,1,0:T(8,128)(2,1)}), bf16[4,2,464,512]{3,2,1,0:T(8,128)(2,1)}, u32[]{:S(2)}, u32[]{:S(2)}) async-start(bf16[4,2,464,512]{3,2,1,0:T(8,128)(2,1)} %get-tuple-element.8), calls=%async_computation | async-start | bytes 7602176 | tf_op jit(solution)/shard_map/all_to_all | solution.py:27
  73.3 2.0 collective-permute-start.2
  75.3 3.6 collective-permute-start.3
  78.9 1.0 collective-permute-start.4
  79.9 7.2 %collective-permute-done.2 = bf16[384,512]{1,0:T(8,128)(2,1)S(1)} collective-permute-done((bf16[384,512]{1,0:T(8,128)(2,1)S(1)}, bf16[384,512]{1,0:T(8,128)(2,1)S(1)}, u32[]{:S(2)}, u32[]{:S(2)}) %collective-permute-start.2) | collective-permute-done | bytes 393248 | tf_op jit(solution)/shard_map/ppermute | solution.py:19
  87.1 9.6 %collective-permute-done.3 = bf16[384,512]{1,0:T(8,128)(2,1)S(1)} collective-permute-done((bf16[384,512]{1,0:T(8,128)(2,1)S(1)}, bf16[384,512]{1,0:T(8,128)(2,1)S(1)}, u32[]{:S(2)}, u32[]{:S(2)}) %collective-permute-start.3) | collective-permute-done | bytes 393248 | tf_op jit(solution)/shard_map/ppermute | solution.py:19
  96.7 1.3 pad_maximum_fusion.2
  98.2 4.1 %pad.10 = bf16[3712,512]{1,0:T(8,128)(2,1)} pad(bf16[3696,512]{1,0:T(8,128)(2,1)} %param.17, bf16[]{:T(256)} %constant.130.clone.1), padding=0_16x0_0 | pad | bytes 7585794 | tf_op jit(solution)/shard_map/jit(_pad)/pad | solution.py:148
  103.1 13.1 %all-to-all-done.own_ref = bf16[4,2,464,512]{3,2,1,0:T(8,128)(2,1)} async-done(((bf16[4,2,464,512]{3,2,1,0:T(8,128)(2,1)}), bf16[4,2,464,512]{3,2,1,0:T(8,128)(2,1)}, u32[]{:S(2)}, u32[]{:S(2)}) %all-to-all-start) | async-done | bytes 3801120 | tf_op jit(solution)/shard_map/all_to_all | solution.py:27
  116.5 1.0 constant_dynamic-update-slice_fusion.3
  117.5 1.0 constant_dynamic-update-slice_fusion.2
  118.5 1.0 constant_dynamic-update-slice_fusion.1
  119.5 1.5 constant_dynamic-update-slice_fusion
  121.1 2.6 gather_fusion
  124.3 2.1 collective-permute-start.17
  126.3 24.4 %collective-permute-done.16.x1 = bf16[512,512]{1,0:T(8,128)(2,1)S(1)} collective-permute-done((bf16[512,512]{1,0:T(8,128)(2,1)}, bf16[512,512]{1,0:T(8,128)(2,1)S(1)}, u32[]{:S(2)}, u32[]{:S(2)}) %collective-permute-start.16) | collective-permute-done | bytes 524320 | tf_op jit(solution)/shard_map/ppermute | solution.py:19
  151.3 13.1 %collective-permute-done.18.x3 = bf16[512,512]{1,0:T(8,128)(2,1)S(1)} collective-permute-done((bf16[512,512]{1,0:T(8,128)(2,1)}, bf16[512,512]{1,0:T(8,128)(2,1)S(1)}, u32[]{:S(2)}, u32[]{:S(2)}) %collective-permute-start.18) | collective-permute-done | bytes 524320 | tf_op jit(solution)/shard_map/ppermute | solution.py:19
  164.4 0.8 copy-done.17
  165.2 9.5 %shard_map.75 = bf16[4,464,512]{2,1,0:T(8,128)(2,1)} custom-call(s32[4]{0:T(128)} %and_select_fusion.7.order_ref, bf16[4,2,464,512]{3,2,1,0:T(8,128)(2,1)} %all_to_all.30.own_ref, bf16[4,2,464,512]{3,2,1,0:T(8,128)(2,1)} %collective-permute-done.15.other_ref, bf16[512,512]{1,0:T(8,128)(2,1)} %gather_fusion, bf16[512,512]{1,0:T(8,128)(2,1)} %copy-done.14, ...), custom_call_target="tpu_custom_call" | custom-call | tf_op jit(solution)/shard_map/pallas_call | solution.py:72
  174.7 3.7 %all-to-all-start.4 = ((bf16[4,464,512]{2,1,0:T(8,128)(2,1)}), bf16[4,464,512]{2,1,0:T(8,128)(2,1)S(1)}, u32[]{:S(2)}, u32[]{:S(2)}) async-start(bf16[4,464,512]{2,1,0:T(8,128)(2,1)} %shard_map.75), calls=%async_computation.4 | async-start | bytes 3801088 | tf_op jit(solution)/shard_map/all_to_all | solution.py:27
  178.5 2.0 collective-permute-start.6
  180.4 2.7 collective-permute-start.7
  183.1 1.5 collective-permute-start.8
  185.1 29.6 %collective-permute-done.6.x1 = bf16[512,512]{1,0:T(8,128)(2,1)S(1)} collective-permute-done((bf16[512,512]{1,0:T(8,128)(2,1)S(1)}, bf16[512,512]{1,0:T(8,128)(2,1)S(1)}, u32[]{:S(2)}, u32[]{:S(2)}) %collective-permute-start.6) | collective-permute-done | bytes 524320 | tf_op jit(solution)/shard_map/ppermute | solution.py:19
  214.7 9.7 %collective-permute-done.7.x2 = bf16[512,512]{1,0:T(8,128)(2,1)S(1)} collective-permute-done((bf16[512,512]{1,0:T(8,128)(2,1)S(1)}, bf16[512,512]{1,0:T(8,128)(2,1)S(1)}, u32[]{:S(2)}, u32[]{:S(2)}) %collective-permute-start.7) | collective-permute-done | bytes 524320 | tf_op jit(solution)/shard_map/ppermute | solution.py:19
  224.4 0.8 copy-done.15
  225.2 9.5 %shard_map.73 = bf16[4,464,512]{2,1,0:T(8,128)(2,1)} custom-call(s32[4]{0:T(128)} %and_select_fusion.8.order_ref, bf16[4,2,464,512]{3,2,1,0:T(8,128)(2,1)} %all-to-all-done.own_ref, bf16[4,2,464,512]{3,2,1,0:T(8,128)(2,1)} %collective-permute-done.1.other_ref, bf16[512,512]{1,0:T(8,128)(2,1)} %gather_fusion, bf16[512,512]{1,0:T(8,128)(2,1)} %copy-done.13, ...), custom_call_target="tpu_custom_call" | custom-call | tf_op jit(solution)/shard_map/pallas_call | solution.py:72
  234.8 1.3 copy-done.3
  236.1 3.6 all-to-all-start.2
  239.7 2.5 shard_map.76
  243.0 2.6 collective-permute-start.21
  245.6 8.8 %collective-permute-done.19 = bf16[232,512]{1,0:T(8,128)(2,1)S(1)} collective-permute-done((bf16[232,512]{1,0:T(8,128)(2,1)}, bf16[232,512]{1,0:T(8,128)(2,1)S(1)}, u32[]{:S(2)}, u32[]{:S(2)}) %collective-permute-start.19) | collective-permute-done | bytes 237600 | tf_op jit(solution)/shard_map/ppermute | solution.py:19
  255.0 1.1 pad_maximum_fusion.4.refs_6_
  256.1 1.8 collective-permute-start.22
  257.9 5.4 %fusion.5 = (bf16[4,4,232,512]{3,2,1,0:T(8,128)(2,1)}, bf16[4,4,232,512]{3,2,1,0:T(8,128)(2,1)}) fusion(bf16[2,4,2,232,512]{4,3,2,1,0:T(8,128)(2,1)} %collective-permute-done, bf16[2,4,2,232,512]{4,3,2,1,0:T(8,128)(2,1)} %bitcast), kind=kLoop, calls=%fused_computation.16 | loop fusion | flops 3801088 | bytes 15204352 | tf_op jit(solution)/shard_map/squeeze | solution.py:151
  263.2 4.7 %gather_fusion.3 = bf16[4,4,232,512]{3,2,1,0:T(8,128)(2,1)} fusion(bf16[4,4,232,512]{3,2,1,0:T(8,128)(2,1)} %get-tuple-element.9, s32[1024]{0:T(1024)S(1)} %pad_clamp_fusion.1), kind=kCustom, calls=%fused_computation.2.clone | custom fusion | bytes 7602192 | tf_op jit(solution)/shard_map/jit(_take)/gather | solution.py:151
  267.9 4.7 %gather_fusion.1 = bf16[4,4,232,512]{3,2,1,0:T(8,128)(2,1)} fusion(bf16[4,4,232,512]{3,2,1,0:T(8,128)(2,1)} %get-tuple-element.10, s32[1024]{0:T(1024)S(1)} %pad_clamp_fusion.2), kind=kCustom, calls=%fused_computation.clone | custom fusion | bytes 7602192 | tf_op jit(solution)/shard_map/jit(_take)/gather | solution.py:150
  272.6 1.3 copy-done.2
  274.0 2.5 shard_map.74
  276.5 1.5 collective-permute-start.9
  278.0 1.5 collective-permute-start.10
  279.5 2.3 collective-permute-start.11
  281.8 4.3 %broadcast_select_fusion = bf16[4,4,232,512]{3,2,1,0:T(8,128)(2,1)} fusion(bf16[4,4,232,512]{3,2,1,0:T(8,128)(2,1)} %gather_fusion.3, pred[4]{0:T(512)(128)(4,1)S(1)} %compare_and_fusion), kind=kLoop, calls=%fused_computation.21 | loop fusion | flops 1900544 | bytes 7602180 | tf_op jit(solution)/shard_map/jit(_take)/select_n | solution.py:151
  286.2 0.9 collective-permute-start.23
  287.0 3.7 %collective-permute-done.9 = bf16[232,512]{1,0:T(8,128)(2,1)S(1)} collective-permute-done((bf16[232,512]{1,0:T(8,128)(2,1)}, bf16[232,512]{1,0:T(8,128)(2,1)S(1)}, u32[]{:S(2)}, u32[]{:S(2)}) %collective-permute-start.9) | collective-permute-done | bytes 237600 | tf_op jit(solution)/shard_map/ppermute | solution.py:19
  291.3 4.5 %collective-permute-done.10 = bf16[232,512]{1,0:T(8,128)(2,1)S(1)} collective-permute-done((bf16[232,512]{1,0:T(8,128)(2,1)}, bf16[232,512]{1,0:T(8,128)(2,1)S(1)}, u32[]{:S(2)}, u32[]{:S(2)}) %collective-permute-start.10) | collective-permute-done | bytes 237600 | tf_op jit(solution)/shard_map/ppermute | solution.py:19
  295.8 10.5 %collective-permute-done.11 = bf16[232,512]{1,0:T(8,128)(2,1)S(1)} collective-permute-done((bf16[232,512]{1,0:T(8,128)(2,1)}, bf16[232,512]{1,0:T(8,128)(2,1)S(1)}, u32[]{:S(2)}, u32[]{:S(2)}) %collective-permute-start.11) | collective-permute-done | bytes 237600 | tf_op jit(solution)/shard_map/ppermute | solution.py:19
  306.5 2.2 collective-permute-start.12
  308.7 3.5 collective-permute-start.13
  312.2 2.3 broadcast_select_fusion.1
  314.5 4.7 %gather_fusion.4 = bf16[4,4,232,512]{3,2,1,0:T(8,128)(2,1)} fusion(bf16[4,4,232,512]{3,2,1,0:T(8,128)(2,1)} %broadcast_select_fusion, s32[1024]{0:T(1024)S(1)} %pad_clamp_fusion.2), kind=kCustom, calls=%fused_computation.3.clone | custom fusion | bytes 7602192 | tf_op jit(solution)/shard_map/jit(_take)/gather | solution.py:151
  319.2 4.7 %gather_fusion.2 = bf16[4,4,232,512]{3,2,1,0:T(8,128)(2,1)} fusion(bf16[4,4,232,512]{3,2,1,0:T(8,128)(2,1)} %broadcast_select_fusion.1, s32[1024]{0:T(1024)S(1)} %pad_clamp_fusion.1), kind=kCustom, calls=%fused_computation.1.clone | custom fusion | bytes 7602192 | tf_op jit(solution)/shard_map/jit(_take)/gather | solution.py:150
  323.9 4.5 %fusion.6.refs_1_ = bf16[4,4,232,512]{3,2,1,0:T(8,128)(2,1)} fusion(bf16[4,4,232,512]{3,2,1,0:T(8,128)(2,1)} %gather_fusion.4, pred[4]{0:T(512)(128)(4,1)S(1)} %compare_and_fusion.1), kind=kLoop, calls=%fused_computation.18 | loop fusion | flops 1900544 | bytes 7602180 | tf_op jit(solution)/shard_map/jit(_take)/select_n | solution.py:151
  328.4 2.3 fusion.7.refs_0_
  330.7 4.3 %collective-permute-done.13.refs_4_ = bf16[4,232,512]{2,1,0:T(8,128)(2,1)} collective-permute-done((bf16[4,232,512]{2,1,0:T(8,128)(2,1)S(1)}, bf16[4,232,512]{2,1,0:T(8,128)(2,1)}, u32[]{:S(2)}, u32[]{:S(2)}) %collective-permute-start.13) | collective-permute-done | bytes 950304 | tf_op jit(solution)/shard_map/ppermute | solution.py:19
  335.1 11.0 %shard_map.77 = f32[512,512]{1,0:T(8,128)} custom-call(bf16[4,4,232,512]{3,2,1,0:T(8,128)(2,1)} %fusion.7.refs_0_, bf16[4,4,232,512]{3,2,1,0:T(8,128)(2,1)} %fusion.6.refs_1_, bf16[4,232,512]{2,1,0:T(8,128)(2,1)} %copy-done.6, bf16[4,232,512]{2,1,0:T(8,128)(2,1)} %collective-permute-done.12.refs_3_, bf16[4,232,512]{2,1,0:T(8,128)(2,1)} %collective-permute-done.13.refs_4_, ...), custom_call_target="tpu_custom_call" | custom-call | tf_op jit(solution)/shard_map/pallas_call | solution.py:122
  346.1 16.2 %all_to_all.31 = f32[4,128,512]{2,1,0:T(8,128)S(1)} all-to-all(f32[4,128,512]{2,1,0:T(8,128)} %bitcast.38), channel_id=1, replica_groups=mesh['y'=4,'x'=4,'z'=4,'core'=2] {'z'}, dimensions={0} | all-to-all | bytes 2097152 | tf_op jit(solution)/shard_map/all_to_all | solution.py:27
  362.3 0.8 reduce_sum.32
  (81 shorter events, 6.1 us)
Async XLA Ops:
  1.8 17.2 %all-to-all-start.1 = ((bf16[16,24,512]{2,1,0:T(8,128)(2,1)}), bf16[16,24,512]{2,1,0:T(8,128)(2,1)S(1)}, u32[]{:S(2)}, u32[]{:S(2)}) async-start(bf16[16,24,512]{2,1,0:T(8,128)(2,1)} %bitcast.35), calls=%async_computation.1 | async-start | bytes 786432 | tf_op jit(solution)/shard_map/all_to_all | solution.py:27
  8.9 3.2 copy-start.7
  68.4 47.8 %all-to-all-start = ((bf16[4,2,464,512]{3,2,1,0:T(8,128)(2,1)}), bf16[4,2,464,512]{3,2,1,0:T(8,128)(2,1)}, u32[]{:S(2)}, u32[]{:S(2)}) async-start(bf16[4,2,464,512]{3,2,1,0:T(8,128)(2,1)} %get-tuple-element.8), calls=%async_computation | async-start | bytes 7602176 | tf_op jit(solution)/shard_map/all_to_all | solution.py:27
  73.2 91.2 %collective-permute-start.15 = (bf16[4,2,464,512]{3,2,1,0:T(8,128)(2,1)}, bf16[4,2,464,512]{3,2,1,0:T(8,128)(2,1)}, u32[]{:S(2)}, u32[]{:S(2)}) collective-permute-start(bf16[4,2,464,512]{3,2,1,0:T(8,128)(2,1)} %all_to_all.30.own_ref), channel_id=1, source_target_pairs={{0,1},{1,0},{2,3},{3,2},{4,5},{5,4},{6,7},{7,6},{8,9},{9,8},{10,11... | collective-permute-start | bytes 11403272 | tf_op jit(solution)/shard_map/ppermute | solution.py:19
  73.3 13.8 %collective-permute-start.2 = (bf16[384,512]{1,0:T(8,128)(2,1)S(1)}, bf16[384,512]{1,0:T(8,128)(2,1)S(1)}, u32[]{:S(2)}, u32[]{:S(2)}) collective-permute-start(bf16[384,512]{1,0:T(8,128)(2,1)S(1)} %bitcast.41), channel_id=1, source_target_pairs={{0,2},{2,4},{4,6},{6,0},{1,3},{3,5},{5,7},{7,1},{8,10},{10,12},{12... | collective-permute-start | bytes 1179656 | tf_op jit(solution)/shard_map/ppermute | solution.py:19
  75.3 21.4 %collective-permute-start.3 = (bf16[384,512]{1,0:T(8,128)(2,1)S(1)}, bf16[384,512]{1,0:T(8,128)(2,1)S(1)}, u32[]{:S(2)}, u32[]{:S(2)}) collective-permute-start(bf16[384,512]{1,0:T(8,128)(2,1)S(1)} %bitcast.42), channel_id=1, source_target_pairs={{0,4},{2,6},{4,0},{6,2},{1,5},{3,7},{5,1},{7,3},{8,12},{10,14},{12... | collective-permute-start | bytes 1179656 | tf_op jit(solution)/shard_map/ppermute | solution.py:19
  78.9 17.9 %collective-permute-start.4 = (bf16[384,512]{1,0:T(8,128)(2,1)S(1)}, bf16[384,512]{1,0:T(8,128)(2,1)S(1)}, u32[]{:S(2)}, u32[]{:S(2)}) collective-permute-start(bf16[384,512]{1,0:T(8,128)(2,1)S(1)} %bitcast.43), channel_id=1, source_target_pairs={{0,6},{2,0},{4,2},{6,4},{1,7},{3,1},{5,3},{7,5},{8,14},{10,8},{12,... | collective-permute-start | bytes 1179656 | tf_op jit(solution)/shard_map/ppermute | solution.py:19
  87.1 9.6 %copy-start.8 = (bf16[384,512]{1,0:T(8,128)(2,1)}, bf16[384,512]{1,0:T(8,128)(2,1)S(1)}, u32[]{:S(2)}) copy-start(bf16[384,512]{1,0:T(8,128)(2,1)S(1)} %collective-permute-done.2) | copy-start | bytes 1179652
  96.7 1.4 copy-start.9
  96.7 1.4 copy-start.10
  98.2 4.7 %copy-start.18 = (s32[128]{0:T(128)S(1)}, s32[128]{0:T(128)}, u32[]{:S(2)}) copy-start(s32[128]{0:T(128)} %param.14) | copy-start | bytes 1540
  98.2 4.7 %copy-start.19 = (s32[128]{0:T(128)S(1)}, s32[128]{0:T(128)}, u32[]{:S(2)}) copy-start(s32[128]{0:T(128)} %param.12) | copy-start | bytes 1540
  98.2 4.9 %copy-start.20 = (s32[128]{0:T(128)S(1)}, s32[128]{0:T(128)}, u32[]{:S(2)}) copy-start(s32[128]{0:T(128)} %param.13) | copy-start | bytes 1540
  98.2 21.4 %collective-permute-start.5 = (bf16[1536,512]{1,0:T(8,128)(2,1)}, bf16[1536,512]{1,0:T(8,128)(2,1)}, u32[]{:S(2)}, u32[]{:S(2)}) collective-permute-start(bf16[1536,512]{1,0:T(8,128)(2,1)} %pad_maximum_fusion.2), channel_id=1, source_target_pairs={{0,1},{1,0},{2,3},{3,2},{4,5},{5,4},{6,7},{7,6},{8,9},{9,8},{10,11... | collective-permute-start | bytes 4718600 | tf_op jit(solution)/shard_map/ppermute | solution.py:19
  102.4 155.5 %collective-permute-start = (bf16[2,4,2,232,512]{4,3,2,1,0:T(8,128)(2,1)}, bf16[2,4,2,232,512]{4,3,2,1,0:T(8,128)(2,1)}, u32[]{:S(2)}, u32[]{:S(2)}) collective-permute-start(bf16[2,4,2,232,512]{4,3,2,1,0:T(8,128)(2,1)} %bitcast), channel_id=1, source_target_pairs={{0,1},{1,0},{2,3},{3,2},{4,5},{5,4},{6,7},{7,6},{8,9},{9,8},{10,11... | collective-permute-start | bytes 11403272 | tf_op jit(solution)/shard_map/ppermute | solution.py:19
  116.1 108.3 %collective-permute-start.1 = (bf16[4,2,464,512]{3,2,1,0:T(8,128)(2,1)}, bf16[4,2,464,512]{3,2,1,0:T(8,128)(2,1)}, u32[]{:S(2)}, u32[]{:S(2)}) collective-permute-start(bf16[4,2,464,512]{3,2,1,0:T(8,128)(2,1)} %all-to-all-done.own_ref), channel_id=1, source_target_pairs={{0,1},{1,0},{2,3},{3,2},{4,5},{5,4},{6,7},{7,6},{8,9},{9,8},{10,11... | collective-permute-start | bytes 11403272 | tf_op jit(solution)/shard_map/ppermute | solution.py:19
  123.7 27.0 %collective-permute-start.16 = (bf16[512,512]{1,0:T(8,128)(2,1)}, bf16[512,512]{1,0:T(8,128)(2,1)S(1)}, u32[]{:S(2)}, u32[]{:S(2)}) collective-permute-start(bf16[512,512]{1,0:T(8,128)(2,1)} %gather_fusion), channel_id=1, source_target_pairs={{0,32},{32,64},{64,96},{96,0},{1,33},{33,65},{65,97},{97,1},{2,34}... | collective-permute-start | bytes 1572872 | tf_op jit(solution)/shard_map/ppermute | solution.py:19
  124.3 27.0 %collective-permute-start.17 = (bf16[512,512]{1,0:T(8,128)(2,1)}, bf16[512,512]{1,0:T(8,128)(2,1)S(1)}, u32[]{:S(2)}, u32[]{:S(2)}) collective-permute-start(bf16[512,512]{1,0:T(8,128)(2,1)} %gather_fusion), channel_id=1, source_target_pairs={{0,64},{32,96},{64,0},{96,32},{1,65},{33,97},{65,1},{97,33},{2,66}... | collective-permute-start | bytes 1572872 | tf_op jit(solution)/shard_map/ppermute | solution.py:19
  150.7 13.7 %copy-start.14 = (bf16[512,512]{1,0:T(8,128)(2,1)}, bf16[512,512]{1,0:T(8,128)(2,1)S(1)}, u32[]{:S(2)}) copy-start(bf16[512,512]{1,0:T(8,128)(2,1)S(1)} %collective-permute-done.16.x1) | copy-start | bytes 1572868
  150.7 13.7 %collective-permute-start.18 = (bf16[512,512]{1,0:T(8,128)(2,1)}, bf16[512,512]{1,0:T(8,128)(2,1)S(1)}, u32[]{:S(2)}, u32[]{:S(2)}) collective-permute-start(bf16[512,512]{1,0:T(8,128)(2,1)} %gather_fusion), channel_id=1, source_target_pairs={{0,96},{32,0},{64,32},{96,64},{1,97},{33,1},{65,33},{97,65},{2,98}... | collective-permute-start | bytes 1572872 | tf_op jit(solution)/shard_map/ppermute | solution.py:19
  151.3 13.1 %copy-start.16 = (bf16[512,512]{1,0:T(8,128)(2,1)}, bf16[512,512]{1,0:T(8,128)(2,1)S(1)}, u32[]{:S(2)}) copy-start(bf16[512,512]{1,0:T(8,128)(2,1)S(1)} %collective-permute-done.17.x2) | copy-start | bytes 1572868
  164.4 0.8 copy-start.17
  174.7 3.7 %copy-start.4 = (bf16[512,512]{1,0:T(8,128)(2,1)S(1)}, bf16[512,512]{1,0:T(8,128)(2,1)}, u32[]{:S(2)}) copy-start(bf16[512,512]{1,0:T(8,128)(2,1)} %gather_fusion) | copy-start | bytes 1572868
  174.7 60.0 %all-to-all-start.4 = ((bf16[4,464,512]{2,1,0:T(8,128)(2,1)}), bf16[4,464,512]{2,1,0:T(8,128)(2,1)S(1)}, u32[]{:S(2)}, u32[]{:S(2)}) async-start(bf16[4,464,512]{2,1,0:T(8,128)(2,1)} %shard_map.75), calls=%async_computation.4 | async-start | bytes 3801088 | tf_op jit(solution)/shard_map/all_to_all | solution.py:27
  178.5 36.2 %collective-permute-start.6 = (bf16[512,512]{1,0:T(8,128)(2,1)S(1)}, bf16[512,512]{1,0:T(8,128)(2,1)S(1)}, u32[]{:S(2)}, u32[]{:S(2)}) collective-permute-start(bf16[512,512]{1,0:T(8,128)(2,1)S(1)} %copy-done.4), channel_id=1, source_target_pairs={{0,8},{8,16},{16,24},{24,0},{1,9},{9,17},{17,25},{25,1},{2,10},{10... | collective-permute-start | bytes 1572872 | tf_op jit(solution)/shard_map/ppermute | solution.py:19
  180.4 44.0 %collective-permute-start.7 = (bf16[512,512]{1,0:T(8,128)(2,1)S(1)}, bf16[512,512]{1,0:T(8,128)(2,1)S(1)}, u32[]{:S(2)}, u32[]{:S(2)}) collective-permute-start(bf16[512,512]{1,0:T(8,128)(2,1)S(1)} %copy-done.4), channel_id=1, source_target_pairs={{0,16},{8,24},{16,0},{24,8},{1,17},{9,25},{17,1},{25,9},{2,18},{10... | collective-permute-start | bytes 1572872 | tf_op jit(solution)/shard_map/ppermute | solution.py:19
  183.1 41.3 %collective-permute-start.8 = (bf16[512,512]{1,0:T(8,128)(2,1)S(1)}, bf16[512,512]{1,0:T(8,128)(2,1)}, u32[]{:S(2)}, u32[]{:S(2)}) collective-permute-start(bf16[512,512]{1,0:T(8,128)(2,1)S(1)} %copy-done.4), channel_id=1, source_target_pairs={{0,24},{8,0},{16,8},{24,16},{1,25},{9,1},{17,9},{25,17},{2,26},{10... | collective-permute-start | bytes 1572872 | tf_op jit(solution)/shard_map/ppermute | solution.py:19
  214.7 9.8 %copy-start.13 = (bf16[512,512]{1,0:T(8,128)(2,1)}, bf16[512,512]{1,0:T(8,128)(2,1)S(1)}, u32[]{:S(2)}) copy-start(bf16[512,512]{1,0:T(8,128)(2,1)S(1)} %collective-permute-done.6.x1) | copy-start | bytes 1572868
  224.4 0.8 copy-start.15
  234.7 1.3 copy-start.3
  236.1 36.6 %all-to-all-start.2 = ((bf16[4,464,512]{2,1,0:T(8,128)(2,1)}), bf16[4,464,512]{2,1,0:T(8,128)(2,1)S(1)}, u32[]{:S(2)}, u32[]{:S(2)}) async-start(bf16[4,464,512]{2,1,0:T(8,128)(2,1)} %shard_map.73), calls=%async_computation.2 | async-start | bytes 3801088 | tf_op jit(solution)/shard_map/all_to_all | solution.py:27
  242.3 12.1 %collective-permute-start.19 = (bf16[232,512]{1,0:T(8,128)(2,1)}, bf16[232,512]{1,0:T(8,128)(2,1)S(1)}, u32[]{:S(2)}, u32[]{:S(2)}) collective-permute-start(bf16[232,512]{1,0:T(8,128)(2,1)} %shard_map.76), channel_id=1, source_target_pairs={{0,8},{8,16},{16,24},{24,0},{1,9},{9,17},{17,25},{25,1},{2,10},{10... | collective-permute-start | bytes 712712 | tf_op jit(solution)/shard_map/ppermute | solution.py:19
  242.3 12.1 %collective-permute-start.20 = (bf16[232,512]{1,0:T(8,128)(2,1)}, bf16[232,512]{1,0:T(8,128)(2,1)S(1)}, u32[]{:S(2)}, u32[]{:S(2)}) collective-permute-start(bf16[232,512]{1,0:T(8,128)(2,1)} %shard_map.76), channel_id=1, source_target_pairs={{0,16},{8,24},{16,0},{24,8},{1,17},{9,25},{17,1},{25,9},{2,18},{10... | collective-permute-start | bytes 712712 | tf_op jit(solution)/shard_map/ppermute | solution.py:19
  243.0 12.1 %collective-permute-start.21 = (bf16[232,512]{1,0:T(8,128)(2,1)}, bf16[232,512]{1,0:T(8,128)(2,1)S(1)}, u32[]{:S(2)}, u32[]{:S(2)}) collective-permute-start(bf16[232,512]{1,0:T(8,128)(2,1)} %shard_map.76), channel_id=1, source_target_pairs={{0,24},{8,0},{16,8},{24,16},{1,25},{9,1},{17,9},{25,17},{2,26},{10... | collective-permute-start | bytes 712712 | tf_op jit(solution)/shard_map/ppermute | solution.py:19
  256.1 34.6 %copy-start.5 = (bf16[4,232,512]{2,1,0:T(8,128)(2,1)}, bf16[4,232,512]{2,1,0:T(8,128)(2,1)S(1)}, u32[]{:S(2)}) copy-start(bf16[4,232,512]{2,1,0:T(8,128)(2,1)S(1)} %pad_maximum_fusion.4.refs_6_) | copy-start | bytes 2850820
  256.1 56.1 %collective-permute-start.22 = (bf16[4,232,512]{2,1,0:T(8,128)(2,1)S(1)}, bf16[4,232,512]{2,1,0:T(8,128)(2,1)}, u32[]{:S(2)}, u32[]{:S(2)}) collective-permute-start(bf16[4,232,512]{2,1,0:T(8,128)(2,1)S(1)} %pad_maximum_fusion.4.refs_6_), channel_id=1, source_target_pairs={{0,32},{32,64},{64,96},{96,0},{1,33},{33,65},{65,97},{97,1},{2,34}... | collective-permute-start | bytes 2850824 | tf_op jit(solution)/shard_map/ppermute | solution.py:19
  272.6 1.3 copy-start.2
  276.5 29.8 %copy-start.12 = (bf16[232,512]{1,0:T(8,128)(2,1)S(1)}, bf16[232,512]{1,0:T(8,128)(2,1)}, u32[]{:S(2)}) copy-start(bf16[232,512]{1,0:T(8,128)(2,1)} %shard_map.74) | copy-start | bytes 712708
  276.5 35.7 %copy-start = (bf16[4,4,232,512]{3,2,1,0:T(8,128)(2,1)S(1)}, bf16[4,4,232,512]{3,2,1,0:T(8,128)(2,1)}, u32[]{:S(2)}) copy-start(bf16[4,4,232,512]{3,2,1,0:T(8,128)(2,1)} %gather_fusion.1) | copy-start | bytes 11403268
  276.5 14.2 %collective-permute-start.9 = (bf16[232,512]{1,0:T(8,128)(2,1)}, bf16[232,512]{1,0:T(8,128)(2,1)S(1)}, u32[]{:S(2)}, u32[]{:S(2)}) collective-permute-start(bf16[232,512]{1,0:T(8,128)(2,1)} %shard_map.74), channel_id=1, source_target_pairs={{0,32},{32,64},{64,96},{96,0},{1,33},{33,65},{65,97},{97,1},{2,34}... | collective-permute-start | bytes 712712 | tf_op jit(solution)/shard_map/ppermute | solution.py:19
  278.0 17.8 %collective-permute-start.10 = (bf16[232,512]{1,0:T(8,128)(2,1)}, bf16[232,512]{1,0:T(8,128)(2,1)S(1)}, u32[]{:S(2)}, u32[]{:S(2)}) collective-permute-start(bf16[232,512]{1,0:T(8,128)(2,1)} %shard_map.74), channel_id=1, source_target_pairs={{0,64},{32,96},{64,0},{96,32},{1,65},{33,97},{65,1},{97,33},{2,66}... | collective-permute-start | bytes 712712 | tf_op jit(solution)/shard_map/ppermute | solution.py:19
  279.5 26.8 %collective-permute-start.11 = (bf16[232,512]{1,0:T(8,128)(2,1)}, bf16[232,512]{1,0:T(8,128)(2,1)S(1)}, u32[]{:S(2)}, u32[]{:S(2)}) collective-permute-start(bf16[232,512]{1,0:T(8,128)(2,1)} %shard_map.74), channel_id=1, source_target_pairs={{0,96},{32,0},{64,32},{96,64},{1,97},{33,1},{65,33},{97,65},{2,98}... | collective-permute-start | bytes 712712 | tf_op jit(solution)/shard_map/ppermute | solution.py:19
  286.2 44.5 %collective-permute-start.23 = (bf16[4,232,512]{2,1,0:T(8,128)(2,1)S(1)}, bf16[4,232,512]{2,1,0:T(8,128)(2,1)S(1)}, u32[]{:S(2)}, u32[]{:S(2)}) collective-permute-start(bf16[4,232,512]{2,1,0:T(8,128)(2,1)S(1)} %pad_maximum_fusion.4.refs_6_), channel_id=1, source_target_pairs={{0,64},{32,96},{64,0},{96,32},{1,65},{33,97},{65,1},{97,33},{2,66}... | collective-permute-start | bytes 2850824 | tf_op jit(solution)/shard_map/ppermute | solution.py:19
  290.7 40.0 %collective-permute-start.24 = (bf16[4,232,512]{2,1,0:T(8,128)(2,1)S(1)}, bf16[4,232,512]{2,1,0:T(8,128)(2,1)}, u32[]{:S(2)}, u32[]{:S(2)}) collective-permute-start(bf16[4,232,512]{2,1,0:T(8,128)(2,1)S(1)} %pad_maximum_fusion.4.refs_6_), channel_id=1, source_target_pairs={{0,96},{32,0},{64,32},{96,64},{1,97},{33,1},{65,33},{97,65},{2,98}... | collective-permute-start | bytes 2850824 | tf_op jit(solution)/shard_map/ppermute | solution.py:19
  306.5 8.0 %copy-start.6 = (bf16[4,232,512]{2,1,0:T(8,128)(2,1)}, bf16[4,232,512]{2,1,0:T(8,128)(2,1)S(1)}, u32[]{:S(2)}) copy-start(bf16[4,232,512]{2,1,0:T(8,128)(2,1)S(1)} %pad_maximum_fusion.3.refs_2_) | copy-start | bytes 2850820
  306.5 24.2 %collective-permute-start.12 = (bf16[4,232,512]{2,1,0:T(8,128)(2,1)S(1)}, bf16[4,232,512]{2,1,0:T(8,128)(2,1)}, u32[]{:S(2)}, u32[]{:S(2)}) collective-permute-start(bf16[4,232,512]{2,1,0:T(8,128)(2,1)S(1)} %pad_maximum_fusion.3.refs_2_), channel_id=1, source_target_pairs={{0,8},{8,16},{16,24},{24,0},{1,9},{9,17},{17,25},{25,1},{2,10},{10... | collective-permute-start | bytes 2850824 | tf_op jit(solution)/shard_map/ppermute | solution.py:19
  308.7 26.4 %collective-permute-start.13 = (bf16[4,232,512]{2,1,0:T(8,128)(2,1)S(1)}, bf16[4,232,512]{2,1,0:T(8,128)(2,1)}, u32[]{:S(2)}, u32[]{:S(2)}) collective-permute-start(bf16[4,232,512]{2,1,0:T(8,128)(2,1)S(1)} %pad_maximum_fusion.3.refs_2_), channel_id=1, source_target_pairs={{0,16},{8,24},{16,0},{24,8},{1,17},{9,25},{17,1},{25,9},{2,18},{10... | collective-permute-start | bytes 2850824 | tf_op jit(solution)/shard_map/ppermute | solution.py:19
  312.2 22.9 %collective-permute-start.14 = (bf16[4,232,512]{2,1,0:T(8,128)(2,1)S(1)}, bf16[4,232,512]{2,1,0:T(8,128)(2,1)}, u32[]{:S(2)}, u32[]{:S(2)}) collective-permute-start(bf16[4,232,512]{2,1,0:T(8,128)(2,1)S(1)} %pad_maximum_fusion.3.refs_2_), channel_id=1, source_target_pairs={{0,24},{8,0},{16,8},{24,16},{1,25},{9,1},{17,9},{25,17},{2,26},{10... | collective-permute-start | bytes 2850824 | tf_op jit(solution)/shard_map/ppermute | solution.py:19
  323.9 4.5 %copy-start.1 = (bf16[4,4,232,512]{3,2,1,0:T(8,128)(2,1)S(1)}, bf16[4,4,232,512]{3,2,1,0:T(8,128)(2,1)}, u32[]{:S(2)}) copy-start(bf16[4,4,232,512]{3,2,1,0:T(8,128)(2,1)} %gather_fusion.2) | copy-start | bytes 11403268
  330.7 4.4 %copy-start.11 = (bf16[4,232,512]{2,1,0:T(8,128)(2,1)}, bf16[4,232,512]{2,1,0:T(8,128)(2,1)S(1)}, u32[]{:S(2)}) copy-start(bf16[4,232,512]{2,1,0:T(8,128)(2,1)S(1)} %collective-permute-done.23.refs_8_) | copy-start | bytes 2850820

commit v2 on v0

v2 whole, which is shorter than its diff:
```python
import functools

import jax
import jax.numpy as jnp
from jax import lax
from jax.experimental import pallas as pl
from jax.experimental.pallas import tpu as pltpu
from jax.sharding import Mesh, PartitionSpec as P

SIDE = 4
CORES = 2
SUB = 232
BLOCK = 2 * SUB
HALF = SIDE * BLOCK
TOK_DEV = 8
BF16 = jnp.bfloat16
F32 = jnp.float32


def shift(value, axis, by, size=SIDE):
    return lax.ppermute(value, axis, [(i, (i + by) % size) for i in range(size)])


def around(value, axis):
    near = {by: shift(value, axis, by) for by in (1, 3, 2)}
    return [value] + [near[by] for by in range(1, SIDE)]


def around_halves(low, high, axis):
    low1, high3 = shift(low, axis, 1), shift(high, axis, 3)
    high1, low3 = shift(high, axis, 1), shift(low, axis, 3)
    low2, high2 = shift(low1, axis, 1), shift(high3, axis, 3)
    return [(low, high), (low1, high1), (low2, high2), (low3, high3)]


def exchange(value, axis):
    return lax.all_to_all(value, axis, split_axis=0, concat_axis=0, tiled=True)


def source_rows(suffix_lengths, owner_map, prefix_lengths, positions):
    request_ids = jnp.arange(suffix_lengths.shape[0], dtype=jnp.int32)
    longer = prefix_lengths[None, :] > prefix_lengths[:, None]
    earlier = (prefix_lengths[None, :] == prefix_lengths[:, None]) & (
        request_ids[None, :] < request_ids[:, None]
    )
    starts = jnp.sum(jnp.where(longer | earlier, suffix_lengths[None, :], 0), axis=1)
    ends = starts + suffix_lengths
    inside = (positions[:, None] >= starts[None, :]) & (positions[:, None] < ends[None, :])
    row, col = owner_map // (SIDE * CORES), owner_map % (SIDE * CORES)
    z_behind = (lax.axis_index("z") - col // CORES) % SIDE
    other_core = (lax.axis_index("core") + col) % CORES
    slot = ((other_core * SIDE + z_behind) * SIDE * SIDE + row) * 24
    shifted = jnp.sum(jnp.where(inside, (slot - starts)[None, :], 0), axis=1)
    return positions + shifted


ANY = pl.BlockSpec(memory_space=pl.ANY)
SMEM = pl.BlockSpec(memory_space=pltpu.SMEM)
VMEM = pl.BlockSpec(memory_space=pltpu.VMEM)


def pieces_kernel(place_ref, gate_ref, up_ref, *refs, axis, base):
    outs, sem = refs[:-1], refs[-1]
    copies = []
    for n, out_ref in enumerate(outs):
        to = lax.rem(place_ref[axis] + (n + 1) % SIDE, SIDE)
        for half in range(2):
            first = pl.multiple_of(base + to * BLOCK + half * SUB, 8)
            for kind, ref in enumerate((gate_ref, up_ref)):
                copies.append(
                    pltpu.make_async_copy(
                        ref.at[pl.ds(first, SUB)],
                        out_ref.at[half, pl.ds(kind * SUB, SUB)],
                        sem.at[n, 2 * half + kind],
                    )
                )
    for copy in copies:
        copy.start()
    for copy in copies:
        copy.wait()


def pieces_for(place, gate, up, axis, base):
    shape = jax.ShapeDtypeStruct((2, BLOCK, gate.shape[1]), BF16)
    return pl.pallas_call(
        functools.partial(pieces_kernel, axis=axis, base=base),
        in_specs=[SMEM] + [ANY] * 2,
        out_specs=[VMEM] * SIDE,
        out_shape=[shape] * SIDE,
        scratch_shapes=[pltpu.SemaphoreType.DMA((SIDE, 4))],
    )(place, gate, up)


def products_kernel(place_ref, *refs, aheads):
    weights, rows = refs[: 4 * SIDE], refs[4 * SIDE : 6 * SIDE]
    outs, (weight_buf, rows_buf, sem) = refs[6 * SIDE : -3], refs[-3:]
    features = rows[0].shape[1]
    shares = [(axis, ahead) for ahead in aheads for axis in range(2)]

    def copy(source, target, n, b):
        return pltpu.make_async_copy(source, target.at[:, pl.ds(b * features, features)], sem.at[n, b])

    def rows_copy(axis, b):
        return copy(rows[axis * SIDE + b], rows_buf.at[axis], len(shares) + axis, b)

    def weight_copy(other, n, b):
        axis, ahead = shares[n]
        at = lax.rem(place_ref[axis] + ahead, SIDE)
        source = weights[(2 * axis + other) * SIDE + b].at[lax.rem(at, 2)]
        return copy(source, weight_buf.at[n], n, b)

    for n, (axis, ahead) in enumerate(shares):
        at = lax.rem(place_ref[axis] + ahead, SIDE)
        if n < 2:
            for b in range(SIDE):
                rows_copy(axis, b).start()

        @pl.when(at < 2)
        def _(n=n):
            for b in range(SIDE):
                weight_copy(0, n, b).start()

        @pl.when(at >= 2)
        def _(n=n):
            for b in range(SIDE):
                weight_copy(1, n, b).start()

    for n, (axis, _) in enumerate(shares):
        for b in range(SIDE):
            if n < 2:
                rows_copy(axis, b).wait()
            weight_copy(0, n, b).wait()
        outs[n][...] = lax.dot_general(
            weight_buf[n], rows_buf[axis], (((1,), (1,)), ((), ())), preferred_element_type=F32
        ).astype(outs[n].dtype)


def products(place, weights, rows, aheads):
    tokens, features = rows[0].shape
    count = 2 * len(aheads)
    return pl.pallas_call(
        functools.partial(products_kernel, aheads=aheads),
        in_specs=[SMEM] + [ANY] * (6 * SIDE),
        out_specs=[VMEM] * count,
        out_shape=[
            jax.ShapeDtypeStruct((BLOCK, tokens), BF16 if ahead else F32)
            for ahead in aheads
            for _ in range(2)
        ],
        scratch_shapes=[
            pltpu.VMEM((count, BLOCK, SIDE * features), BF16),
            pltpu.VMEM((2, tokens, SIDE * features), BF16),
            pltpu.SemaphoreType.DMA((count + 2, SIDE)),
        ],
    )(place, *weights, *rows)


def hidden_kernel(repeated_ref, *refs):
    for axis in range(2):
        parts, out_ref = refs[axis * SIDE : (axis + 1) * SIDE], refs[2 * SIDE + axis]
        total = parts[0][...]
        for part in parts[1:]:
            total = total + part[...].astype(F32)
        gate, up = total[:SUB], total[SUB:]
        hidden = gate / (1.0 + jnp.exp(-gate)) * up
        if axis:
            unit = lax.broadcasted_iota(jnp.int32, hidden.shape, 0)
            hidden = jnp.where(unit < repeated_ref[0], 0.0, hidden)
        out_ref[...] = hidden.astype(BF16)


def hidden_rows(repeated, parts):
    return pl.pallas_call(
        hidden_kernel,
        in_specs=[SMEM] + [VMEM] * len(parts),
        out_specs=[VMEM] * 2,
        out_shape=[jax.ShapeDtypeStruct((SUB, parts[0].shape[-1]), BF16)] * 2,
    )(repeated, *parts)


def down_kernel(place_ref, own_ref, other_ref, *refs, which, extra, last):
    blocks = 2 * len(which)
    second = own_ref.shape[0] - HALF
    hiddens, refs = refs[: 2 * blocks], refs[2 * blocks :]
    sums, outs, (weight_buf, hidden_buf, total_ref, sem) = refs[:extra], refs[extra:-4], refs[-4:]

    def unit(n, i):
        far_axis = 1 - n % 2
        far = lax.rem(place_ref[far_axis] + SIDE - which[n // 2], SIDE)
        near = lax.rem(place_ref[1 - far_axis] + SIDE - i, SIDE)
        return n % 2 * second + far * BLOCK + lax.rem(near, 2) * SUB, near

    def weight_copy(core_ref, n, i):
        first = pl.multiple_of(unit(n, i)[0], 8)
        return pltpu.make_async_copy(core_ref.at[pl.ds(first, SUB)], weight_buf.at[n, i], sem.at[n, i])

    def hidden_copy(n, i):
        source = hiddens[2 * n + i // 2].at[i % 2]
        return pltpu.make_async_copy(source, hidden_buf.at[n, i], sem.at[n, SIDE + i])

    for n in range(blocks):
        for i in range(SIDE):
            hidden_copy(n, i).start()

            @pl.when(unit(n, i)[1] < 2)
            def _(n=n, i=i):
                weight_copy(own_ref, n, i).start()

            @pl.when(unit(n, i)[1] >= 2)
            def _(n=n, i=i):
                weight_copy(other_ref, n, i).start()

    for n in range(blocks):
        for i in range(SIDE):
            hidden_copy(n, i).wait()
            weight_copy(own_ref, n, i).wait()
        term = lax.dot_general(
            jnp.concatenate([hidden_buf[n, i] for i in range(SIDE)], axis=0),
            jnp.concatenate([weight_buf[n, i] for i in range(SIDE)], axis=0),
            (((0,), (0,)), ((), ())),
            preferred_element_type=F32,
        )
        if n:
            term = term + total_ref[...]
        elif extra:
            term = term + sums[0][...]
        if last or n + 1 < blocks:
            total_ref[...] = term
        else:
            outs[0][...] = term
    if last:
        for ahead, out_ref in enumerate(outs):
            tokens = out_ref.shape[0]
            at = lax.rem(place_ref[2] + ahead, SIDE) * tokens
            out_ref[...] = total_ref[pl.ds(pl.multiple_of(at, tokens), tokens), :].astype(out_ref.dtype)


def down_products(place, own, other, which, hiddens, sums=None, last=False):
    blocks = len(hiddens) // 2
    features, tokens = own.shape[1], hiddens[0].shape[-1]
    extra = [] if sums is None else [sums]
    if last:
        part = (tokens // SIDE, features)
        out_shape = [jax.ShapeDtypeStruct(part, BF16 if ahead else F32) for ahead in range(SIDE)]
    else:
        out_shape = [jax.ShapeDtypeStruct((tokens, features), F32)]
    outs = pl.pallas_call(
        functools.partial(down_kernel, which=which, extra=len(extra), last=last),
        in_specs=[SMEM] + [ANY] * (2 + len(hiddens)) + [VMEM] * len(extra),
        out_specs=[VMEM] * len(out_shape),
        out_shape=out_shape,
        scratch_shapes=[
            pltpu.VMEM((blocks, SIDE, SUB, features), BF16),
            pltpu.VMEM((blocks, SIDE, SUB, tokens), BF16),
            pltpu.VMEM((tokens, features), F32),
            pltpu.SemaphoreType.DMA((blocks, 2 * SIDE)),
        ],
    )(place, own, other, *hiddens, *extra)
    return outs if last else outs[0]


def on_device(
    owned_rows, suffix_lengths, owner_map, prefix_lengths, gate_weight, up_weight, down_weight
):
    slots = owned_rows.shape[0]
    features, units = gate_weight.shape
    second = units - HALF
    x, y = lax.axis_index("x"), lax.axis_index("y")
    core = lax.axis_index("core")
    place = jnp.stack([y, x, lax.axis_index("z")])

    blocks = owned_rows.reshape(slots, SIDE * SIDE, features).transpose(1, 0, 2)
    blocks, gate_weight, up_weight = lax.optimization_barrier((blocks, gate_weight, up_weight))
    feature_rows = exchange(blocks, ("y", "x")).reshape(-1, features)

    def pieces(axis, base):
        cut = pieces_for(place, gate_weight.T, up_weight.T, "yx".index(axis), base)
        return [cut[-1]] + [shift(cut[ahead - 1], axis, ahead) for ahead in range(1, SIDE)]

    own_x, own_y = pieces("x", 0), pieces("y", second)
    other_down = shift(down_weight, "core", 1, 2)
    near = around(feature_rows, "z")
    every = jnp.concatenate(near + [shift(r, "core", 1, 2) for r in near], axis=0)
    at = jnp.arange(TOK_DEV * suffix_lengths.shape[0] // CORES, dtype=jnp.int32)
    positions = (at // 128 * CORES + core) * 128 + at % 128
    source = source_rows(suffix_lengths, owner_map, prefix_lengths, positions)
    rows = every.at[source].get(mode="promise_in_bounds")

    rows_x, rows_y = around(rows, "x"), around(rows, "y")
    other_x = [shift(w, "core", 1, 2) for w in own_x]
    other_y = [shift(w, "core", 1, 2) for w in own_y]

    shares_x, shares_y = {}, {}
    for aheads in ((2,), (1, 3, 0)):
        shares = products(
            place, own_x + other_x + own_y + other_y, rows_x + rows_y, aheads
        )
        shares_x.update(zip(aheads, shares[::2]))
        shares_y.update(zip(aheads, shares[1::2]))

    def swap(shares, axis):
        return [shares[0]] + [shift(shares[d], axis, d) for d in (1, 3, 2)]

    repeated = jnp.where((y == 0) & (x % 2 == 0), HALF - second, 0)
    hidden_x, hidden_y = hidden_rows(repeated[None], swap(shares_x, "y") + swap(shares_y, "x"))
    hidden_x, hidden_y = around(hidden_x, "y"), around(hidden_y, "x")
    all_x = around_halves(jnp.stack(hidden_x[:2]), jnp.stack(hidden_x[2:]), "x")
    all_y = around_halves(jnp.stack(hidden_y[:2]), jnp.stack(hidden_y[2:]), "y")

    def step(which, sums=None, last=False):
        halves = [half for i in which for pair in (all_x[i], all_y[i]) for half in pair]
        return down_products(place, down_weight, other_down, which, halves, sums, last)

    parts = step([1, 3, 2], step([0]), last=True)
    parts = swap(dict(enumerate(parts)), "z")
    return sum(part.astype(F32) for part in parts).astype(BF16)


def solution(mesh):
    torus = Mesh(mesh.devices.reshape(SIDE, SIDE, SIDE, CORES), ("y", "x", "z", "core"))
    row, col = ("y", "x"), ("z", "core")
    return jax.shard_map(
        on_device,
        mesh=torus,
        in_specs=(P(row + col, None), P(), P(), P(), P(row, col), P(row, col), P(col, row)),
        out_specs=P(col, row),
        check_vma=False,
    )
```

time: 445 us -> 303 us (0.68)
  waiting for transfers between devices: 378 us -> 161 us
  starting transfers between devices: 7.11 us -> 71.9 us
  Pallas kernels: 0 us -> 43.7 us
  matrix products: 31.9 us -> 0 us
  between operations: 13.2 us -> 0.52 us
  local copies, waits for them, and re-layouts: 10.1 us -> 20.2 us
    reduce_scatter x3 -> x0, waiting for transfers between devices: 230 us -> none  [the longest x1 106 us: on_device(): lax.psum_scatter(jnp.dot(block_rows, gate_weight, preferred_element_type=...]
    ppermute x0 -> x55, waiting for transfers between devices: none -> 151 us  [shift(): lax.ppermute(value, axis, [(i, (i + by) % size) for i in range(size)])]
    all_gather x2 -> x0, waiting for transfers between devices: 98.4 us -> none  [the longest x1 66.2 us: on_device(): lax.all_gather(hidden_share, 'row', axis=0, tiled=True)]
    ppermute x0 -> x55, starting transfers between devices: none -> 64.8 us  [shift(): lax.ppermute(value, axis, [(i, (i + by) % size) for i in range(size)])]
    pallas_call x0 -> x7, Pallas kernels: none -> 43.7 us  [the longest x2 17.4 us: products(): pl.pallas_call(functools.partial(products_kernel, aheads=aheads), in_spec...]
    all_to_all x1, waiting for transfers between devices: 48.1 us -> 10.1 us  [exchange(): return lax.all_to_all(value, axis, split_axis=0, concat_axis=0, tiled=True)]
    dot_general x3 -> x0, matrix products: 31.9 us -> none  [the longest x1 12 us: on_device(): jnp.dot(block_rows, up_weight, preferred_element_type=jnp.float32)]
    unnamed x8 -> x69, local copies, waits for them, and re-layouts: 1.16 us -> 13.4 us
  transfers between devices with their start and end apart: 6 -> 56, of which waited for: 6 -> 28; matrix products, arithmetic and copies ran while one was open for 2% -> 6% of each run, Pallas kernels for 0% -> 12%
where the time goes in v2:
time: 303 us; the launch traced here: 302 us
  waiting for transfers between devices  161 us (53%)
  starting transfers between devices  71.9 us (24%)
  Pallas kernels  43.7 us (14%)
  local copies, waits for them, and re-layouts  20.2 us (7%)
  other arithmetic  4.87 us (2%)
    ppermute x55, waiting for transfers between devices, shift(): lax.ppermute(value, axis, [(i, (i + by) % size) for i in range(size)])  151 us
    ppermute x55, starting transfers between devices, shift(): lax.ppermute(value, axis, [(i, (i + by) % size) for i in range(size)])  64.8 us
    pallas_call x2, Pallas kernels, products(): pl.pallas_call(functools.partial(products_kernel, aheads=aheads), in_spec...  17.4 us
    unnamed x69, local copies, waits for them, and re-layouts  13.4 us
    pallas_call x2, Pallas kernels, down_products(): pl.pallas_call(functools.partial(down_kernel, which=which, extra=len(extr...  12.9 us
    all_to_all x1, waiting for transfers between devices, exchange(): return lax.all_to_all(value, axis, split_axis=0, concat_axis=0, tiled=True)  10.1 us
    pallas_call x2, Pallas kernels, pieces_for(): pl.pallas_call(functools.partial(pieces_kernel, axis=axis, base=base), in...  9.77 us
    all_to_all x1, starting transfers between devices, exchange(): return lax.all_to_all(value, axis, split_axis=0, concat_axis=0, tiled=True)  7.15 us
  transfers between devices with their start and end apart: 56, of which 28 were waited for; matrix products, arithmetic and copies ran while one was open for 6% of the time, Pallas kernels for 12%

profile of v2, /device:TPU:0, one launch (start us, length us, event | category | flops | bytes accessed | tf_op | source)
XLA Modules:
  0.0 302.2 jit_solution(10095809976106421033)
XLA Ops:
  0.0 1.8 copy.13
  1.8 7.1 %all-to-all-start = ((bf16[16,24,512]{2,1,0:T(8,128)(2,1)}), bf16[16,24,512]{2,1,0:T(8,128)(2,1)S(1)}, u32[]{:S(2)}, u32[]{:S(2)}) async-start(bf16[16,24,512]{2,1,0:T(8,128)(2,1)} %bitcast.23), calls=%async_computation | async-start | bytes 786432 | tf_op jit(solution)/shard_map/all_to_all | solution.py:37
  8.9 10.1 %all-to-all-done = bf16[16,24,512]{2,1,0:T(8,128)(2,1)S(1)} async-done(((bf16[16,24,512]{2,1,0:T(8,128)(2,1)}), bf16[16,24,512]{2,1,0:T(8,128)(2,1)S(1)}, u32[]{:S(2)}, u32[]{:S(2)}) %all-to-all-start) | async-done | bytes 393248 | tf_op jit(solution)/shard_map/all_to_all | solution.py:37
  19.0 1.9 collective-permute-start.15
  21.6 5.0 %shard_map.74 = (bf16[2,464,512]{2,1,0:T(8,128)(2,1)}, bf16[2,464,512]{2,1,0:T(8,128)(2,1)}, bf16[2,464,512]{2,1,0:T(8,128)(2,1)}, bf16[2,464,512]{2,1,0:T(8,128)(2,1)}) custom-call(s32[3]{0:T(128)} %pad_add_fusion.place_ref, bf16[3696,512]{1,0:T(8,128)(2,1)} %bitcast.24, bf16[3696,512]{1,0:T(8,128)(2,1)} %bitcast.26), custom_call_target="tpu_custom_call" | custom-call | tf_op jit(solution)/shard_map/pallas_call | solution.py:85
  26.7 2.3 collective-permute-start.9
  29.0 1.2 collective-permute-start.10
  30.2 3.6 %collective-permute-start.16 = (bf16[384,512]{1,0:T(8,128)(2,1)S(1)}, bf16[384,512]{1,0:T(8,128)(2,1)}, u32[]{:S(2)}, u32[]{:S(2)}) collective-permute-start(bf16[384,512]{1,0:T(8,128)(2,1)S(1)} %bitcast.29), channel_id=1, source_target_pairs={{0,4},{2,6},{4,0},{6,2},{1,5},{3,7},{5,1},{7,3},{8,12},{10,14},{12... | collective-permute-start | bytes 1179656 | tf_op jit(solution)/shard_map/ppermute | solution.py:21
  34.0 1.1 collective-permute-start.17
  35.1 5.9 %collective-permute-done.16 = bf16[384,512]{1,0:T(8,128)(2,1)} collective-permute-done((bf16[384,512]{1,0:T(8,128)(2,1)S(1)}, bf16[384,512]{1,0:T(8,128)(2,1)}, u32[]{:S(2)}, u32[]{:S(2)}) %collective-permute-start.16) | collective-permute-done | bytes 393248 | tf_op jit(solution)/shard_map/ppermute | solution.py:21
  41.2 7.6 %collective-permute-done.17 = bf16[384,512]{1,0:T(8,128)(2,1)} collective-permute-done((bf16[384,512]{1,0:T(8,128)(2,1)S(1)}, bf16[384,512]{1,0:T(8,128)(2,1)}, u32[]{:S(2)}, u32[]{:S(2)}) %collective-permute-start.17) | collective-permute-done | bytes 393248 | tf_op jit(solution)/shard_map/ppermute | solution.py:21
  48.8 4.8 %shard_map.73 = (bf16[2,464,512]{2,1,0:T(8,128)(2,1)}, bf16[2,464,512]{2,1,0:T(8,128)(2,1)}, bf16[2,464,512]{2,1,0:T(8,128)(2,1)}, bf16[2,464,512]{2,1,0:T(8,128)(2,1)}) custom-call(s32[3]{0:T(128)} %pad_add_fusion.place_ref, bf16[3696,512]{1,0:T(8,128)(2,1)} %bitcast.25, bf16[3696,512]{1,0:T(8,128)(2,1)} %bitcast.27), custom_call_target="tpu_custom_call" | custom-call | tf_op jit(solution)/shard_map/pallas_call | solution.py:85
  54.0 15.8 %collective-permute-done.8.refs_9_ = bf16[2,464,512]{2,1,0:T(8,128)(2,1)S(1)} collective-permute-done((bf16[2,464,512]{2,1,0:T(8,128)(2,1)}, bf16[2,464,512]{2,1,0:T(8,128)(2,1)S(1)}, u32[]{:S(2)}, u32[]{:S(2)}) %collective-permute-start.8) | collective-permute-done | bytes 950304 | tf_op jit(solution)/shard_map/ppermute | solution.py:21
  71.2 1.8 constant_dynamic-update-slice_fusion.6
  73.0 1.8 constant_dynamic-update-slice_fusion.5
  75.1 2.9 collective-permute-start.3
  78.0 1.8 constant_dynamic-update-slice_fusion.4
  80.3 1.8 constant_dynamic-update-slice_fusion.3
  82.1 1.8 constant_dynamic-update-slice_fusion.2
  85.4 4.3 %gather_fusion = bf16[512,512]{1,0:T(8,128)(2,1)S(1)} fusion(bf16[3072,512]{1,0:T(8,128)(2,1)} %constant_dynamic-update-slice_fusion, s32[1024]{0:T(1024)S(1)} %pad_clamp_fusion), kind=kCustom, calls=%fused_computation | custom fusion | bytes 1050624 | tf_op jit(solution)/shard_map/gather | solution.py:287
  89.8 10.8 %collective-permute-done.2.refs_2_ = bf16[2,464,512]{2,1,0:T(8,128)(2,1)} collective-permute-done((bf16[2,464,512]{2,1,0:T(8,128)(2,1)}, bf16[2,464,512]{2,1,0:T(8,128)(2,1)}, u32[]{:S(2)}, u32[]{:S(2)}) %collective-permute-start.2) | collective-permute-done | bytes 950304 | tf_op jit(solution)/shard_map/ppermute | solution.py:21
  100.9 18.2 %collective-permute-done.3.refs_3_ = bf16[2,464,512]{2,1,0:T(8,128)(2,1)} collective-permute-done((bf16[2,464,512]{2,1,0:T(8,128)(2,1)}, bf16[2,464,512]{2,1,0:T(8,128)(2,1)}, u32[]{:S(2)}, u32[]{:S(2)}) %collective-permute-start.3) | collective-permute-done | bytes 950304 | tf_op jit(solution)/shard_map/ppermute | solution.py:21
  119.1 2.6 collective-permute-start.24
  122.3 5.3 %collective-permute-start.26 = (bf16[512,512]{1,0:T(8,128)(2,1)S(1)}, bf16[512,512]{1,0:T(8,128)(2,1)S(1)}, u32[]{:S(2)}, u32[]{:S(2)}) collective-permute-start(bf16[512,512]{1,0:T(8,128)(2,1)S(1)} %gather_fusion), channel_id=1, source_target_pairs={{0,64},{32,96},{64,0},{96,32},{1,65},{33,97},{65,1},{97,33},{2,66}... | collective-permute-start | bytes 1572872 | tf_op jit(solution)/shard_map/ppermute | solution.py:21
  127.6 13.0 %collective-permute-done.24.refs_19_ = bf16[512,512]{1,0:T(8,128)(2,1)S(1)} collective-permute-done((bf16[512,512]{1,0:T(8,128)(2,1)S(1)}, bf16[512,512]{1,0:T(8,128)(2,1)S(1)}, u32[]{:S(2)}, u32[]{:S(2)}) %collective-permute-start.24) | collective-permute-done | bytes 524320 | tf_op jit(solution)/shard_map/ppermute | solution.py:21
  140.6 6.9 %collective-permute-done.25.refs_21_ = bf16[512,512]{1,0:T(8,128)(2,1)S(1)} collective-permute-done((bf16[512,512]{1,0:T(8,128)(2,1)S(1)}, bf16[512,512]{1,0:T(8,128)(2,1)S(1)}, u32[]{:S(2)}, u32[]{:S(2)}) %collective-permute-start.25) | collective-permute-done | bytes 524320 | tf_op jit(solution)/shard_map/ppermute | solution.py:21
  148.1 5.6 %collective-permute-done.27.refs_23_ = bf16[512,512]{1,0:T(8,128)(2,1)S(1)} collective-permute-done((bf16[512,512]{1,0:T(8,128)(2,1)S(1)}, bf16[512,512]{1,0:T(8,128)(2,1)S(1)}, u32[]{:S(2)}, u32[]{:S(2)}) %collective-permute-start.27) | collective-permute-done | bytes 524320 | tf_op jit(solution)/shard_map/ppermute | solution.py:21
  155.8 1.4 collective-permute-done.5.refs_5_
  157.2 1.2 collective-permute-done.6.refs_6_
  158.5 1.3 collective-permute-done.7.refs_7_
  160.8 6.0 %shard_map.76 = (bf16[464,512]{1,0:T(8,128)(2,1)}, bf16[464,512]{1,0:T(8,128)(2,1)}) custom-call(s32[3]{0:T(128)} %pad_add_fusion.place_ref, bf16[2,464,512]{2,1,0:T(8,128)(2,1)} %get-tuple-element.32.refs_0_, bf16[2,464,512]{2,1,0:T(8,128)(2,1)} %collective-permute-done.1.refs_1_, bf16[2,464,512]{2,1,0:T(8,128)(2,1)} %collective-permute-done.2.refs_2_, ...), custom_call_target="tpu_custom_call" | custom-call | tf_op jit(solution)/shard_map/pallas_call | solution.py:141
  167.0 3.0 collective-permute-start.33
  170.0 11.3 %shard_map.75 = (bf16[464,512]{1,0:T(8,128)(2,1)}, bf16[464,512]{1,0:T(8,128)(2,1)}, bf16[464,512]{1,0:T(8,128)(2,1)}, bf16[464,512]{1,0:T(8,128)(2,1)}, f32[464,512]{1,0:T(8,128)}, /*index=5*/f32[464,512]{1,0:T(8,128)}) custom-call(s32[3]{0:T(128)} %pad_add_fusion.place_ref, bf16[2,464,512]{2,1,0:T(8,128)(2,1)} %get-tuple-element.32.refs_0_, ...), custom_call_target="tpu_custom_call" | custom-call | tf_op jit(solution)/shard_map/pallas_call | solution.py:141
  181.3 1.8 collective-permute-start.28
  183.1 1.5 collective-permute-start.29
  185.5 2.3 collective-permute-start.32
  187.8 7.3 %collective-permute-done.28.refs_1_ = bf16[464,512]{1,0:T(8,128)(2,1)S(1)} collective-permute-done((bf16[464,512]{1,0:T(8,128)(2,1)}, bf16[464,512]{1,0:T(8,128)(2,1)S(1)}, u32[]{:S(2)}, u32[]{:S(2)}) %collective-permute-start.28) | collective-permute-done | bytes 475168 | tf_op jit(solution)/shard_map/ppermute | solution.py:21
  195.4 2.4 collective-permute-done.31.refs_5_
  198.7 3.6 %shard_map.77 = (bf16[232,512]{1,0:T(8,128)(2,1)}, bf16[232,512]{1,0:T(8,128)(2,1)}) custom-call(s32[1]{0:T(128)} %bitcast.3.repeated_ref, f32[464,512]{1,0:T(8,128)} %get-tuple-element.41.refs_0_, bf16[464,512]{1,0:T(8,128)(2,1)} %copy-done.23, bf16[464,512]{1,0:T(8,128)(2,1)} %copy-done.24, bf16[464,512]{1,0:T(8,128)(2,1)} %copy-done.18, ...), custom_call_target="tpu_custom_call" | custom-call | tf_op jit(solution)/shard_map/pallas_call | solution.py:173
  202.4 2.3 collective-permute-start.41
  205.5 1.1 collective-permute-start.39
  206.7 1.7 collective-permute-start.36
  208.4 4.1 %collective-permute-done.41 = bf16[232,512]{1,0:T(8,128)(2,1)S(1)} collective-permute-done((bf16[232,512]{1,0:T(8,128)(2,1)}, bf16[232,512]{1,0:T(8,128)(2,1)S(1)}, u32[]{:S(2)}, u32[]{:S(2)}) %collective-permute-start.41) | collective-permute-done | bytes 237600 | tf_op jit(solution)/shard_map/ppermute | solution.py:21
  213.2 1.7 collective-permute-done.42
  216.0 1.4 collective-permute-start.43
  218.9 2.2 collective-permute-done.37
  222.1 21.5 %collective-permute-done.34 = bf16[232,512]{1,0:T(8,128)(2,1)S(1)} collective-permute-done((bf16[232,512]{1,0:T(8,128)(2,1)}, bf16[232,512]{1,0:T(8,128)(2,1)S(1)}, u32[]{:S(2)}, u32[]{:S(2)}) %collective-permute-start.34) | collective-permute-done | bytes 237600 | tf_op jit(solution)/shard_map/ppermute | solution.py:21
  244.6 3.7 %collective-permute-start.45 = (bf16[2,232,512]{2,1,0:T(8,128)(2,1)S(1)}, bf16[2,232,512]{2,1,0:T(8,128)(2,1)}, u32[]{:S(2)}, u32[]{:S(2)}) collective-permute-start(bf16[2,232,512]{2,1,0:T(8,128)(2,1)S(1)} %pad_maximum_fusion.1.refs_1_), channel_id=1, source_target_pairs={{0,24},{8,0},{16,8},{24,16},{1,25},{9,1},{17,9},{25,17},{2,26},{10... | collective-permute-start | bytes 1425416 | tf_op jit(solution)/shard_map/ppermute | solution.py:21
  248.7 5.1 %collective-permute-done.46.refs_6_ = bf16[2,232,512]{2,1,0:T(8,128)(2,1)S(1)} collective-permute-done((bf16[2,232,512]{2,1,0:T(8,128)(2,1)S(1)}, bf16[2,232,512]{2,1,0:T(8,128)(2,1)S(1)}, u32[]{:S(2)}, u32[]{:S(2)}) %collective-permute-start.46) | collective-permute-done | bytes 475168 | tf_op jit(solution)/shard_map/ppermute | solution.py:21
  253.8 4.5 %collective-permute-start.44 = (bf16[2,232,512]{2,1,0:T(8,128)(2,1)S(1)}, bf16[2,232,512]{2,1,0:T(8,128)(2,1)}, u32[]{:S(2)}, u32[]{:S(2)}) collective-permute-start(bf16[2,232,512]{2,1,0:T(8,128)(2,1)S(1)} %pad_maximum_fusion.refs_0_), channel_id=1, source_target_pairs={{0,24},{8,0},{16,8},{24,16},{1,25},{9,1},{17,9},{25,17},{2,26},{10... | collective-permute-start | bytes 1425416 | tf_op jit(solution)/shard_map/ppermute | solution.py:21
  258.4 1.5 collective-permute-start.51
  259.9 3.3 %collective-permute-done.38.refs_1_ = bf16[2,232,512]{2,1,0:T(8,128)(2,1)S(1)} collective-permute-done((bf16[2,232,512]{2,1,0:T(8,128)(2,1)S(1)}, bf16[2,232,512]{2,1,0:T(8,128)(2,1)S(1)}, u32[]{:S(2)}, u32[]{:S(2)}) %collective-permute-start.38) | collective-permute-done | bytes 475168 | tf_op jit(solution)/shard_map/ppermute | solution.py:21
  263.2 2.0 collective-permute-start.50
  265.2 5.5 %collective-permute-done.35.refs_0_ = bf16[2,232,512]{2,1,0:T(8,128)(2,1)} collective-permute-done((bf16[2,232,512]{2,1,0:T(8,128)(2,1)S(1)}, bf16[2,232,512]{2,1,0:T(8,128)(2,1)}, u32[]{:S(2)}, u32[]{:S(2)}) %collective-permute-start.35) | collective-permute-done | bytes 475168 | tf_op jit(solution)/shard_map/ppermute | solution.py:21
  270.7 2.0 collective-permute-start.48
  272.7 4.8 %shard_map.78.refs_12_ = f32[512,512]{1,0:T(8,128)} custom-call(s32[3]{0:T(128)} %pad_add_fusion.place_ref, bf16[3696,512]{1,0:T(8,128)(2,1)} %own_ref.3, bf16[3696,512]{1,0:T(8,128)(2,1)} %collective-permute-done.other_ref, bf16[2,232,512]{2,1,0:T(8,128)(2,1)} %copy-done.16, bf16[2,232,512]{2,1,0:T(8,128)(2,1)} %copy-done.15, ...), custom_call_target="tpu_custom_call" | custom-call | tf_op jit(solution)/shard_map/pallas_call | solution.py:247
  277.6 3.5 %collective-permute-done.49.refs_9_ = bf16[2,232,512]{2,1,0:T(8,128)(2,1)} collective-permute-done((bf16[2,232,512]{2,1,0:T(8,128)(2,1)}, bf16[2,232,512]{2,1,0:T(8,128)(2,1)}, u32[]{:S(2)}, u32[]{:S(2)}) %collective-permute-start.49) | collective-permute-done | bytes 475168 | tf_op jit(solution)/shard_map/ppermute | solution.py:21
  281.1 1.3 collective-permute-done.48.refs_8_
  282.4 8.1 %shard_map.79 = (f32[128,512]{1,0:T(8,128)}, bf16[128,512]{1,0:T(8,128)(2,1)}, bf16[128,512]{1,0:T(8,128)(2,1)}, bf16[128,512]{1,0:T(8,128)(2,1)}) custom-call(s32[3]{0:T(128)} %pad_add_fusion.place_ref, bf16[3696,512]{1,0:T(8,128)(2,1)} %own_ref.3, bf16[3696,512]{1,0:T(8,128)(2,1)} %collective-permute-done.other_ref, ...), custom_call_target="tpu_custom_call" | custom-call | tf_op jit(solution)/shard_map/pallas_call | solution.py:247
  290.6 2.0 collective-permute-start.52
  292.5 1.3 collective-permute-start.53
  293.9 2.4 collective-permute-start.54
  297.7 2.8 collective-permute-done.54
  300.5 1.7 add_convert_fusion
  (139 shorter events, 20.2 us)
Async XLA Ops:
  1.8 17.2 %all-to-all-start = ((bf16[16,24,512]{2,1,0:T(8,128)(2,1)}), bf16[16,24,512]{2,1,0:T(8,128)(2,1)S(1)}, u32[]{:S(2)}, u32[]{:S(2)}) async-start(bf16[16,24,512]{2,1,0:T(8,128)(2,1)} %bitcast.23), calls=%async_computation | async-start | bytes 786432 | tf_op jit(solution)/shard_map/all_to_all | solution.py:37
  19.0 15.0 %collective-permute-start.15 = (bf16[384,512]{1,0:T(8,128)(2,1)S(1)}, bf16[384,512]{1,0:T(8,128)(2,1)}, u32[]{:S(2)}, u32[]{:S(2)}) collective-permute-start(bf16[384,512]{1,0:T(8,128)(2,1)S(1)} %bitcast.28), channel_id=1, source_target_pairs={{0,2},{2,4},{4,6},{6,0},{1,3},{3,5},{5,7},{7,1},{8,10},{10,12},{12... | collective-permute-start | bytes 1179656 | tf_op jit(solution)/shard_map/ppermute | solution.py:21
  26.6 43.2 %collective-permute-start.8 = (bf16[2,464,512]{2,1,0:T(8,128)(2,1)}, bf16[2,464,512]{2,1,0:T(8,128)(2,1)S(1)}, u32[]{:S(2)}, u32[]{:S(2)}) collective-permute-start(bf16[2,464,512]{2,1,0:T(8,128)(2,1)} %get-tuple-element.37), channel_id=1, source_target_pairs={{0,32},{32,64},{64,96},{96,0},{1,33},{33,65},{65,97},{97,1},{2,34}... | collective-permute-start | bytes 2850824 | tf_op jit(solution)/shard_map/ppermute | solution.py:21
  26.7 43.2 %collective-permute-start.9 = (bf16[2,464,512]{2,1,0:T(8,128)(2,1)}, bf16[2,464,512]{2,1,0:T(8,128)(2,1)S(1)}, u32[]{:S(2)}, u32[]{:S(2)}) collective-permute-start(bf16[2,464,512]{2,1,0:T(8,128)(2,1)} %get-tuple-element.38), channel_id=1, source_target_pairs={{0,64},{32,96},{64,0},{96,32},{1,65},{33,97},{65,1},{97,33},{2,66}... | collective-permute-start | bytes 2850824 | tf_op jit(solution)/shard_map/ppermute | solution.py:21
  29.0 45.8 %collective-permute-start.10 = (bf16[2,464,512]{2,1,0:T(8,128)(2,1)}, bf16[2,464,512]{2,1,0:T(8,128)(2,1)}, u32[]{:S(2)}, u32[]{:S(2)}) collective-permute-start(bf16[2,464,512]{2,1,0:T(8,128)(2,1)} %get-tuple-element.39), channel_id=1, source_target_pairs={{0,96},{32,0},{64,32},{96,64},{1,97},{33,1},{65,33},{97,65},{2,98}... | collective-permute-start | bytes 2850824 | tf_op jit(solution)/shard_map/ppermute | solution.py:21
  30.2 10.8 %collective-permute-start.16 = (bf16[384,512]{1,0:T(8,128)(2,1)S(1)}, bf16[384,512]{1,0:T(8,128)(2,1)}, u32[]{:S(2)}, u32[]{:S(2)}) collective-permute-start(bf16[384,512]{1,0:T(8,128)(2,1)S(1)} %bitcast.29), channel_id=1, source_target_pairs={{0,4},{2,6},{4,0},{6,2},{1,5},{3,7},{5,1},{7,3},{8,12},{10,14},{12... | collective-permute-start | bytes 1179656 | tf_op jit(solution)/shard_map/ppermute | solution.py:21
  34.0 14.8 %collective-permute-start.17 = (bf16[384,512]{1,0:T(8,128)(2,1)S(1)}, bf16[384,512]{1,0:T(8,128)(2,1)}, u32[]{:S(2)}, u32[]{:S(2)}) collective-permute-start(bf16[384,512]{1,0:T(8,128)(2,1)S(1)} %bitcast.30), channel_id=1, source_target_pairs={{0,6},{2,0},{4,2},{6,4},{1,7},{3,1},{5,3},{7,5},{8,14},{10,8},{12,... | collective-permute-start | bytes 1179656 | tf_op jit(solution)/shard_map/ppermute | solution.py:21
  40.9 12.7 %collective-permute-start.18 = (bf16[384,512]{1,0:T(8,128)(2,1)S(1)}, bf16[384,512]{1,0:T(8,128)(2,1)}, u32[]{:S(2)}, u32[]{:S(2)}) collective-permute-start(bf16[384,512]{1,0:T(8,128)(2,1)S(1)} %bitcast.31), channel_id=1, source_target_pairs={{0,1},{1,0},{2,3},{3,2},{4,5},{5,4},{6,7},{7,6},{8,9},{9,8},{10,11... | collective-permute-start | bytes 1179656 | tf_op jit(solution)/shard_map/ppermute | solution.py:21
  48.8 26.3 %collective-permute-start.19 = (bf16[384,512]{1,0:T(8,128)(2,1)}, bf16[384,512]{1,0:T(8,128)(2,1)}, u32[]{:S(2)}, u32[]{:S(2)}) collective-permute-start(bf16[384,512]{1,0:T(8,128)(2,1)} %collective-permute-done.15), channel_id=1, source_target_pairs={{0,1},{1,0},{2,3},{3,2},{4,5},{5,4},{6,7},{7,6},{8,9},{9,8},{10,11... | collective-permute-start | bytes 1179656 | tf_op jit(solution)/shard_map/ppermute | solution.py:21
  53.6 36.1 %collective-permute-start.1 = (bf16[2,464,512]{2,1,0:T(8,128)(2,1)}, bf16[2,464,512]{2,1,0:T(8,128)(2,1)}, u32[]{:S(2)}, u32[]{:S(2)}) collective-permute-start(bf16[2,464,512]{2,1,0:T(8,128)(2,1)} %get-tuple-element.33), channel_id=1, source_target_pairs={{0,8},{8,16},{16,24},{24,0},{1,9},{9,17},{17,25},{25,1},{2,10},{10... | collective-permute-start | bytes 2850824 | tf_op jit(solution)/shard_map/ppermute | solution.py:21
  69.8 51.8 %copy-start.2 = (bf16[2,464,512]{2,1,0:T(8,128)(2,1)}, bf16[2,464,512]{2,1,0:T(8,128)(2,1)S(1)}, u32[]{:S(2)}) copy-start(bf16[2,464,512]{2,1,0:T(8,128)(2,1)S(1)} %collective-permute-done.8.refs_9_) | copy-start | bytes 2850820
  69.8 9.9 %collective-permute-start.20 = (bf16[384,512]{1,0:T(8,128)(2,1)}, bf16[384,512]{1,0:T(8,128)(2,1)S(1)}, u32[]{:S(2)}, u32[]{:S(2)}) collective-permute-start(bf16[384,512]{1,0:T(8,128)(2,1)} %collective-permute-done.16), channel_id=1, source_target_pairs={{0,1},{1,0},{2,3},{3,2},{4,5},{5,4},{6,7},{7,6},{8,9},{9,8},{10,11... | collective-permute-start | bytes 1179656 | tf_op jit(solution)/shard_map/ppermute | solution.py:21
  69.8 51.9 %copy-start.3 = (bf16[2,464,512]{2,1,0:T(8,128)(2,1)}, bf16[2,464,512]{2,1,0:T(8,128)(2,1)S(1)}, u32[]{:S(2)}) copy-start(bf16[2,464,512]{2,1,0:T(8,128)(2,1)S(1)} %collective-permute-done.9.refs_10_) | copy-start | bytes 2850820
  69.9 9.9 %collective-permute-start.21 = (bf16[384,512]{1,0:T(8,128)(2,1)}, bf16[384,512]{1,0:T(8,128)(2,1)S(1)}, u32[]{:S(2)}, u32[]{:S(2)}) collective-permute-start(bf16[384,512]{1,0:T(8,128)(2,1)} %collective-permute-done.17), channel_id=1, source_target_pairs={{0,1},{1,0},{2,3},{3,2},{4,5},{5,4},{6,7},{7,6},{8,9},{9,8},{10,11... | collective-permute-start | bytes 1179656 | tf_op jit(solution)/shard_map/ppermute | solution.py:21
  74.8 25.8 %collective-permute-start.2 = (bf16[2,464,512]{2,1,0:T(8,128)(2,1)}, bf16[2,464,512]{2,1,0:T(8,128)(2,1)}, u32[]{:S(2)}, u32[]{:S(2)}) collective-permute-start(bf16[2,464,512]{2,1,0:T(8,128)(2,1)} %get-tuple-element.34), channel_id=1, source_target_pairs={{0,16},{8,24},{16,0},{24,8},{1,17},{9,25},{17,1},{25,9},{2,18},{10... | collective-permute-start | bytes 2850824 | tf_op jit(solution)/shard_map/ppermute | solution.py:21
  75.1 44.0 %collective-permute-start.3 = (bf16[2,464,512]{2,1,0:T(8,128)(2,1)}, bf16[2,464,512]{2,1,0:T(8,128)(2,1)}, u32[]{:S(2)}, u32[]{:S(2)}) collective-permute-start(bf16[2,464,512]{2,1,0:T(8,128)(2,1)} %get-tuple-element.35), channel_id=1, source_target_pairs={{0,24},{8,0},{16,8},{24,16},{1,25},{9,1},{17,9},{25,17},{2,26},{10... | collective-permute-start | bytes 2850824 | tf_op jit(solution)/shard_map/ppermute | solution.py:21
  79.8 41.9 %collective-permute-start.11 = (bf16[2,464,512]{2,1,0:T(8,128)(2,1)S(1)}, bf16[2,464,512]{2,1,0:T(8,128)(2,1)}, u32[]{:S(2)}, u32[]{:S(2)}) collective-permute-start(bf16[2,464,512]{2,1,0:T(8,128)(2,1)S(1)} %copy-done.1), channel_id=1, source_target_pairs={{0,1},{1,0},{2,3},{3,2},{4,5},{5,4},{6,7},{7,6},{8,9},{9,8},{10,11... | collective-permute-start | bytes 2850824 | tf_op jit(solution)/shard_map/ppermute | solution.py:21
  79.8 41.9 %collective-permute-start.4 = (bf16[2,464,512]{2,1,0:T(8,128)(2,1)}, bf16[2,464,512]{2,1,0:T(8,128)(2,1)}, u32[]{:S(2)}, u32[]{:S(2)}) collective-permute-start(bf16[2,464,512]{2,1,0:T(8,128)(2,1)} %get-tuple-element.32.refs_0_), channel_id=1, source_target_pairs={{0,1},{1,0},{2,3},{3,2},{4,5},{5,4},{6,7},{7,6},{8,9},{9,8},{10,11... | collective-permute-start | bytes 2850824 | tf_op jit(solution)/shard_map/ppermute | solution.py:21
  89.7 70.1 %copy-start = (bf16[512,512]{1,0:T(8,128)(2,1)}, bf16[512,512]{1,0:T(8,128)(2,1)S(1)}, u32[]{:S(2)}) copy-start(bf16[512,512]{1,0:T(8,128)(2,1)S(1)} %gather_fusion) | copy-start | bytes 1572868
  89.7 32.1 %collective-permute-start.22 = (bf16[512,512]{1,0:T(8,128)(2,1)S(1)}, bf16[512,512]{1,0:T(8,128)(2,1)}, u32[]{:S(2)}, u32[]{:S(2)}) collective-permute-start(bf16[512,512]{1,0:T(8,128)(2,1)S(1)} %gather_fusion), channel_id=1, source_target_pairs={{0,8},{8,16},{16,24},{24,0},{1,9},{9,17},{17,25},{25,1},{2,10},{10... | collective-permute-start | bytes 1572872 | tf_op jit(solution)/shard_map/ppermute | solution.py:21
  100.6 21.7 %collective-permute-start.23 = (bf16[512,512]{1,0:T(8,128)(2,1)S(1)}, bf16[512,512]{1,0:T(8,128)(2,1)S(1)}, u32[]{:S(2)}, u32[]{:S(2)}) collective-permute-start(bf16[512,512]{1,0:T(8,128)(2,1)S(1)} %gather_fusion), channel_id=1, source_target_pairs={{0,16},{8,24},{16,0},{24,8},{1,17},{9,25},{17,1},{25,9},{2,18},{10... | collective-permute-start | bytes 1572872 | tf_op jit(solution)/shard_map/ppermute | solution.py:21
  119.1 21.6 %collective-permute-start.24 = (bf16[512,512]{1,0:T(8,128)(2,1)S(1)}, bf16[512,512]{1,0:T(8,128)(2,1)S(1)}, u32[]{:S(2)}, u32[]{:S(2)}) collective-permute-start(bf16[512,512]{1,0:T(8,128)(2,1)S(1)} %gather_fusion), channel_id=1, source_target_pairs={{0,24},{8,0},{16,8},{24,16},{1,25},{9,1},{17,9},{25,17},{2,26},{10... | collective-permute-start | bytes 1572872 | tf_op jit(solution)/shard_map/ppermute | solution.py:21
  121.7 25.9 %collective-permute-start.25 = (bf16[512,512]{1,0:T(8,128)(2,1)S(1)}, bf16[512,512]{1,0:T(8,128)(2,1)S(1)}, u32[]{:S(2)}, u32[]{:S(2)}) collective-permute-start(bf16[512,512]{1,0:T(8,128)(2,1)S(1)} %gather_fusion), channel_id=1, source_target_pairs={{0,32},{32,64},{64,96},{96,0},{1,33},{33,65},{65,97},{97,1},{2,34}... | collective-permute-start | bytes 1572872 | tf_op jit(solution)/shard_map/ppermute | solution.py:21
  121.7 32.0 %collective-permute-start.12 = (bf16[2,464,512]{2,1,0:T(8,128)(2,1)S(1)}, bf16[2,464,512]{2,1,0:T(8,128)(2,1)S(1)}, u32[]{:S(2)}, u32[]{:S(2)}) collective-permute-start(bf16[2,464,512]{2,1,0:T(8,128)(2,1)S(1)} %collective-permute-done.8.refs_9_), channel_id=1, source_target_pairs={{0,1},{1,0},{2,3},{3,2},{4,5},{5,4},{6,7},{7,6},{8,9},{9,8},{10,11... | collective-permute-start | bytes 2850824 | tf_op jit(solution)/shard_map/ppermute | solution.py:21
  121.8 32.4 %collective-permute-start.13 = (bf16[2,464,512]{2,1,0:T(8,128)(2,1)S(1)}, bf16[2,464,512]{2,1,0:T(8,128)(2,1)S(1)}, u32[]{:S(2)}, u32[]{:S(2)}) collective-permute-start(bf16[2,464,512]{2,1,0:T(8,128)(2,1)S(1)} %collective-permute-done.9.refs_10_), channel_id=1, source_target_pairs={{0,1},{1,0},{2,3},{3,2},{4,5},{5,4},{6,7},{7,6},{8,9},{9,8},{10,11... | collective-permute-start | bytes 2850824 | tf_op jit(solution)/shard_map/ppermute | solution.py:21
  122.3 36.2 %copy-start.8 = (bf16[512,512]{1,0:T(8,128)(2,1)}, bf16[512,512]{1,0:T(8,128)(2,1)S(1)}, u32[]{:S(2)}) copy-start(bf16[512,512]{1,0:T(8,128)(2,1)S(1)} %collective-permute-done.23.refs_18_) | copy-start | bytes 1572868
  122.3 25.3 %collective-permute-start.26 = (bf16[512,512]{1,0:T(8,128)(2,1)S(1)}, bf16[512,512]{1,0:T(8,128)(2,1)S(1)}, u32[]{:S(2)}, u32[]{:S(2)}) collective-permute-start(bf16[512,512]{1,0:T(8,128)(2,1)S(1)} %gather_fusion), channel_id=1, source_target_pairs={{0,64},{32,96},{64,0},{96,32},{1,65},{33,97},{65,1},{97,33},{2,66}... | collective-permute-start | bytes 1572872 | tf_op jit(solution)/shard_map/ppermute | solution.py:21
  140.6 13.1 %collective-permute-start.27 = (bf16[512,512]{1,0:T(8,128)(2,1)S(1)}, bf16[512,512]{1,0:T(8,128)(2,1)S(1)}, u32[]{:S(2)}, u32[]{:S(2)}) collective-permute-start(bf16[512,512]{1,0:T(8,128)(2,1)S(1)} %gather_fusion), channel_id=1, source_target_pairs={{0,96},{32,0},{64,32},{96,64},{1,97},{33,1},{65,33},{97,65},{2,98}... | collective-permute-start | bytes 1572872 | tf_op jit(solution)/shard_map/ppermute | solution.py:21
  147.6 123.1 %collective-permute-start = (bf16[3696,512]{1,0:T(8,128)(2,1)}, bf16[3696,512]{1,0:T(8,128)(2,1)}, u32[]{:S(2)}, u32[]{:S(2)}) collective-permute-start(bf16[3696,512]{1,0:T(8,128)(2,1)} %own_ref.3), channel_id=1, source_target_pairs={{0,1},{1,0},{2,3},{3,2},{4,5},{5,4},{6,7},{7,6},{8,9},{9,8},{10,11... | collective-permute-start | bytes 11354120 | tf_op jit(solution)/shard_map/ppermute | solution.py:21
  147.6 8.3 %collective-permute-start.14 = (bf16[2,464,512]{2,1,0:T(8,128)(2,1)}, bf16[2,464,512]{2,1,0:T(8,128)(2,1)}, u32[]{:S(2)}, u32[]{:S(2)}) collective-permute-start(bf16[2,464,512]{2,1,0:T(8,128)(2,1)} %collective-permute-done.10.refs_11_), channel_id=1, source_target_pairs={{0,1},{1,0},{2,3},{3,2},{4,5},{5,4},{6,7},{7,6},{8,9},{9,8},{10,11... | collective-permute-start | bytes 2850824 | tf_op jit(solution)/shard_map/ppermute | solution.py:21
  153.7 3.5 %collective-permute-start.5 = (bf16[2,464,512]{2,1,0:T(8,128)(2,1)}, bf16[2,464,512]{2,1,0:T(8,128)(2,1)}, u32[]{:S(2)}, u32[]{:S(2)}) collective-permute-start(bf16[2,464,512]{2,1,0:T(8,128)(2,1)} %collective-permute-done.1.refs_1_), channel_id=1, source_target_pairs={{0,1},{1,0},{2,3},{3,2},{4,5},{5,4},{6,7},{7,6},{8,9},{9,8},{10,11... | collective-permute-start | bytes 2850824 | tf_op jit(solution)/shard_map/ppermute | solution.py:21
  153.7 4.7 %collective-permute-start.6 = (bf16[2,464,512]{2,1,0:T(8,128)(2,1)}, bf16[2,464,512]{2,1,0:T(8,128)(2,1)S(1)}, u32[]{:S(2)}, u32[]{:S(2)}) collective-permute-start(bf16[2,464,512]{2,1,0:T(8,128)(2,1)} %collective-permute-done.2.refs_2_), channel_id=1, source_target_pairs={{0,1},{1,0},{2,3},{3,2},{4,5},{5,4},{6,7},{7,6},{8,9},{9,8},{10,11... | collective-permute-start | bytes 2850824 | tf_op jit(solution)/shard_map/ppermute | solution.py:21
  155.2 4.6 %collective-permute-start.7 = (bf16[2,464,512]{2,1,0:T(8,128)(2,1)}, bf16[2,464,512]{2,1,0:T(8,128)(2,1)S(1)}, u32[]{:S(2)}, u32[]{:S(2)}) collective-permute-start(bf16[2,464,512]{2,1,0:T(8,128)(2,1)} %collective-permute-done.3.refs_3_), channel_id=1, source_target_pairs={{0,1},{1,0},{2,3},{3,2},{4,5},{5,4},{6,7},{7,6},{8,9},{9,8},{10,11... | collective-permute-start | bytes 2850824 | tf_op jit(solution)/shard_map/ppermute | solution.py:21
  166.8 17.8 %collective-permute-start.30 = (bf16[464,512]{1,0:T(8,128)(2,1)}, bf16[464,512]{1,0:T(8,128)(2,1)S(1)}, u32[]{:S(2)}, u32[]{:S(2)}) collective-permute-start(bf16[464,512]{1,0:T(8,128)(2,1)} %get-tuple-element.44), channel_id=1, source_target_pairs={{0,64},{32,96},{64,0},{96,32},{1,65},{33,97},{65,1},{97,33},{2,66}... | collective-permute-start | bytes 1425416 | tf_op jit(solution)/shard_map/ppermute | solution.py:21
  167.0 18.5 %collective-permute-start.33 = (bf16[464,512]{1,0:T(8,128)(2,1)}, bf16[464,512]{1,0:T(8,128)(2,1)S(1)}, u32[]{:S(2)}, u32[]{:S(2)}) collective-permute-start(bf16[464,512]{1,0:T(8,128)(2,1)} %get-tuple-element.48), channel_id=1, source_target_pairs={{0,16},{8,24},{16,0},{24,8},{1,17},{9,25},{17,1},{25,9},{2,18},{10... | collective-permute-start | bytes 1425416 | tf_op jit(solution)/shard_map/ppermute | solution.py:21
  181.3 13.8 %collective-permute-start.28 = (bf16[464,512]{1,0:T(8,128)(2,1)}, bf16[464,512]{1,0:T(8,128)(2,1)S(1)}, u32[]{:S(2)}, u32[]{:S(2)}) collective-permute-start(bf16[464,512]{1,0:T(8,128)(2,1)} %get-tuple-element.42), channel_id=1, source_target_pairs={{0,32},{32,64},{64,96},{96,0},{1,33},{33,65},{65,97},{97,1},{2,34}... | collective-permute-start | bytes 1425416 | tf_op jit(solution)/shard_map/ppermute | solution.py:21
  183.1 12.3 %collective-permute-start.29 = (bf16[464,512]{1,0:T(8,128)(2,1)}, bf16[464,512]{1,0:T(8,128)(2,1)S(1)}, u32[]{:S(2)}, u32[]{:S(2)}) collective-permute-start(bf16[464,512]{1,0:T(8,128)(2,1)} %get-tuple-element.43), channel_id=1, source_target_pairs={{0,96},{32,0},{64,32},{96,64},{1,97},{33,1},{65,33},{97,65},{2,98}... | collective-permute-start | bytes 1425416 | tf_op jit(solution)/shard_map/ppermute | solution.py:21
  184.6 13.2 %collective-permute-start.31 = (bf16[464,512]{1,0:T(8,128)(2,1)}, bf16[464,512]{1,0:T(8,128)(2,1)S(1)}, u32[]{:S(2)}, u32[]{:S(2)}) collective-permute-start(bf16[464,512]{1,0:T(8,128)(2,1)} %get-tuple-element.46), channel_id=1, source_target_pairs={{0,8},{8,16},{16,24},{24,0},{1,9},{9,17},{17,25},{25,1},{2,10},{10... | collective-permute-start | bytes 1425416 | tf_op jit(solution)/shard_map/ppermute | solution.py:21
  185.5 12.3 %collective-permute-start.32 = (bf16[464,512]{1,0:T(8,128)(2,1)}, bf16[464,512]{1,0:T(8,128)(2,1)S(1)}, u32[]{:S(2)}, u32[]{:S(2)}) collective-permute-start(bf16[464,512]{1,0:T(8,128)(2,1)} %get-tuple-element.47), channel_id=1, source_target_pairs={{0,24},{8,0},{16,8},{24,16},{1,25},{9,1},{17,9},{25,17},{2,26},{10... | collective-permute-start | bytes 1425416 | tf_op jit(solution)/shard_map/ppermute | solution.py:21
  202.4 10.1 %collective-permute-start.41 = (bf16[232,512]{1,0:T(8,128)(2,1)}, bf16[232,512]{1,0:T(8,128)(2,1)S(1)}, u32[]{:S(2)}, u32[]{:S(2)}) collective-permute-start(bf16[232,512]{1,0:T(8,128)(2,1)} %get-tuple-element.50), channel_id=1, source_target_pairs={{0,16},{8,24},{16,0},{24,8},{1,17},{9,25},{17,1},{25,9},{2,18},{10... | collective-permute-start | bytes 712712 | tf_op jit(solution)/shard_map/ppermute | solution.py:21
  204.7 10.3 %collective-permute-start.42 = (bf16[232,512]{1,0:T(8,128)(2,1)}, bf16[232,512]{1,0:T(8,128)(2,1)S(1)}, u32[]{:S(2)}, u32[]{:S(2)}) collective-permute-start(bf16[232,512]{1,0:T(8,128)(2,1)} %get-tuple-element.50), channel_id=1, source_target_pairs={{0,24},{8,0},{16,8},{24,16},{1,25},{9,1},{17,9},{25,17},{2,26},{10... | collective-permute-start | bytes 712712 | tf_op jit(solution)/shard_map/ppermute | solution.py:21
  205.5 10.4 %collective-permute-start.39 = (bf16[232,512]{1,0:T(8,128)(2,1)}, bf16[232,512]{1,0:T(8,128)(2,1)S(1)}, u32[]{:S(2)}, u32[]{:S(2)}) collective-permute-start(bf16[232,512]{1,0:T(8,128)(2,1)} %get-tuple-element.50), channel_id=1, source_target_pairs={{0,8},{8,16},{16,24},{24,0},{1,9},{9,17},{17,25},{25,1},{2,10},{10... | collective-permute-start | bytes 712712 | tf_op jit(solution)/shard_map/ppermute | solution.py:21
  206.7 11.6 %collective-permute-start.36 = (bf16[232,512]{1,0:T(8,128)(2,1)}, bf16[232,512]{1,0:T(8,128)(2,1)S(1)}, u32[]{:S(2)}, u32[]{:S(2)}) collective-permute-start(bf16[232,512]{1,0:T(8,128)(2,1)} %get-tuple-element.49), channel_id=1, source_target_pairs={{0,64},{32,96},{64,0},{96,32},{1,65},{33,97},{65,1},{97,33},{2,66}... | collective-permute-start | bytes 712712 | tf_op jit(solution)/shard_map/ppermute | solution.py:21
  212.5 8.7 %collective-permute-start.37 = (bf16[232,512]{1,0:T(8,128)(2,1)}, bf16[232,512]{1,0:T(8,128)(2,1)S(1)}, u32[]{:S(2)}, u32[]{:S(2)}) collective-permute-start(bf16[232,512]{1,0:T(8,128)(2,1)} %get-tuple-element.49), channel_id=1, source_target_pairs={{0,96},{32,0},{64,32},{96,64},{1,97},{33,1},{65,33},{97,65},{2,98}... | collective-permute-start | bytes 712712 | tf_op jit(solution)/shard_map/ppermute | solution.py:21
  215.0 57.8 %copy-start.13 = (bf16[2,232,512]{2,1,0:T(8,128)(2,1)}, bf16[2,232,512]{2,1,0:T(8,128)(2,1)S(1)}, u32[]{:S(2)}) copy-start(bf16[2,232,512]{2,1,0:T(8,128)(2,1)S(1)} %pad_maximum_fusion.3.refs_3_) | copy-start | bytes 1425412
  215.0 29.6 %collective-permute-start.47 = (bf16[2,232,512]{2,1,0:T(8,128)(2,1)S(1)}, bf16[2,232,512]{2,1,0:T(8,128)(2,1)S(1)}, u32[]{:S(2)}, u32[]{:S(2)}) collective-permute-start(bf16[2,232,512]{2,1,0:T(8,128)(2,1)S(1)} %pad_maximum_fusion.3.refs_3_), channel_id=1, source_target_pairs={{0,96},{32,0},{64,32},{96,64},{1,97},{33,1},{65,33},{97,65},{2,98}... | collective-permute-start | bytes 1425416 | tf_op jit(solution)/shard_map/ppermute | solution.py:21
  216.0 32.3 %collective-permute-start.43 = (bf16[2,232,512]{2,1,0:T(8,128)(2,1)S(1)}, bf16[2,232,512]{2,1,0:T(8,128)(2,1)S(1)}, u32[]{:S(2)}, u32[]{:S(2)}) collective-permute-start(bf16[2,232,512]{2,1,0:T(8,128)(2,1)S(1)} %pad_maximum_fusion.3.refs_3_), channel_id=1, source_target_pairs={{0,32},{32,64},{64,96},{96,0},{1,33},{33,65},{65,97},{97,1},{2,34}... | collective-permute-start | bytes 1425416 | tf_op jit(solution)/shard_map/ppermute | solution.py:21
  218.3 54.4 %copy-start.14 = (bf16[2,232,512]{2,1,0:T(8,128)(2,1)}, bf16[2,232,512]{2,1,0:T(8,128)(2,1)S(1)}, u32[]{:S(2)}) copy-start(bf16[2,232,512]{2,1,0:T(8,128)(2,1)S(1)} %pad_maximum_fusion.2.refs_2_) | copy-start | bytes 1425412
  218.3 29.9 %collective-permute-start.40 = (bf16[2,232,512]{2,1,0:T(8,128)(2,1)S(1)}, bf16[2,232,512]{2,1,0:T(8,128)(2,1)S(1)}, u32[]{:S(2)}, u32[]{:S(2)}) collective-permute-start(bf16[2,232,512]{2,1,0:T(8,128)(2,1)S(1)} %pad_maximum_fusion.2.refs_2_), channel_id=1, source_target_pairs={{0,32},{32,64},{64,96},{96,0},{1,33},{33,65},{65,97},{97,1},{2,34}... | collective-permute-start | bytes 1425416 | tf_op jit(solution)/shard_map/ppermute | solution.py:21
  221.2 22.4 %collective-permute-start.34 = (bf16[232,512]{1,0:T(8,128)(2,1)}, bf16[232,512]{1,0:T(8,128)(2,1)S(1)}, u32[]{:S(2)}, u32[]{:S(2)}) collective-permute-start(bf16[232,512]{1,0:T(8,128)(2,1)} %get-tuple-element.49), channel_id=1, source_target_pairs={{0,32},{32,64},{64,96},{96,0},{1,33},{33,65},{65,97},{97,1},{2,34}... | collective-permute-start | bytes 712712 | tf_op jit(solution)/shard_map/ppermute | solution.py:21
  222.0 50.7 %copy-start.15 = (bf16[2,232,512]{2,1,0:T(8,128)(2,1)}, bf16[2,232,512]{2,1,0:T(8,128)(2,1)S(1)}, u32[]{:S(2)}) copy-start(bf16[2,232,512]{2,1,0:T(8,128)(2,1)S(1)} %pad_maximum_fusion.1.refs_1_) | copy-start | bytes 1425412
  243.6 10.3 %collective-permute-start.46 = (bf16[2,232,512]{2,1,0:T(8,128)(2,1)S(1)}, bf16[2,232,512]{2,1,0:T(8,128)(2,1)S(1)}, u32[]{:S(2)}, u32[]{:S(2)}) collective-permute-start(bf16[2,232,512]{2,1,0:T(8,128)(2,1)S(1)} %pad_maximum_fusion.2.refs_2_), channel_id=1, source_target_pairs={{0,96},{32,0},{64,32},{96,64},{1,97},{33,1},{65,33},{97,65},{2,98}... | collective-permute-start | bytes 1425416 | tf_op jit(solution)/shard_map/ppermute | solution.py:21
  244.6 32.9 %copy-start.17 = (bf16[2,232,512]{2,1,0:T(8,128)(2,1)}, bf16[2,232,512]{2,1,0:T(8,128)(2,1)S(1)}, u32[]{:S(2)}) copy-start(bf16[2,232,512]{2,1,0:T(8,128)(2,1)S(1)} %collective-permute-done.47.refs_7_) | copy-start | bytes 1425412
  244.6 13.8 %collective-permute-start.45 = (bf16[2,232,512]{2,1,0:T(8,128)(2,1)S(1)}, bf16[2,232,512]{2,1,0:T(8,128)(2,1)}, u32[]{:S(2)}, u32[]{:S(2)}) collective-permute-start(bf16[2,232,512]{2,1,0:T(8,128)(2,1)S(1)} %pad_maximum_fusion.1.refs_1_), channel_id=1, source_target_pairs={{0,24},{8,0},{16,8},{24,16},{1,25},{9,1},{17,9},{25,17},{2,26},{10... | collective-permute-start | bytes 1425416 | tf_op jit(solution)/shard_map/ppermute | solution.py:21
  248.3 15.0 %collective-permute-start.38 = (bf16[2,232,512]{2,1,0:T(8,128)(2,1)S(1)}, bf16[2,232,512]{2,1,0:T(8,128)(2,1)S(1)}, u32[]{:S(2)}, u32[]{:S(2)}) collective-permute-start(bf16[2,232,512]{2,1,0:T(8,128)(2,1)S(1)} %pad_maximum_fusion.1.refs_1_), channel_id=1, source_target_pairs={{0,8},{8,16},{16,24},{24,0},{1,9},{9,17},{17,25},{25,1},{2,10},{10... | collective-permute-start | bytes 1425416 | tf_op jit(solution)/shard_map/ppermute | solution.py:21
  248.3 22.4 %collective-permute-start.35 = (bf16[2,232,512]{2,1,0:T(8,128)(2,1)S(1)}, bf16[2,232,512]{2,1,0:T(8,128)(2,1)}, u32[]{:S(2)}, u32[]{:S(2)}) collective-permute-start(bf16[2,232,512]{2,1,0:T(8,128)(2,1)S(1)} %pad_maximum_fusion.refs_0_), channel_id=1, source_target_pairs={{0,8},{8,16},{16,24},{24,0},{1,9},{9,17},{17,25},{25,1},{2,10},{10... | collective-permute-start | bytes 1425416 | tf_op jit(solution)/shard_map/ppermute | solution.py:21
  253.8 23.7 %collective-permute-start.44 = (bf16[2,232,512]{2,1,0:T(8,128)(2,1)S(1)}, bf16[2,232,512]{2,1,0:T(8,128)(2,1)}, u32[]{:S(2)}, u32[]{:S(2)}) collective-permute-start(bf16[2,232,512]{2,1,0:T(8,128)(2,1)S(1)} %pad_maximum_fusion.refs_0_), channel_id=1, source_target_pairs={{0,24},{8,0},{16,8},{24,16},{1,25},{9,1},{17,9},{25,17},{2,26},{10... | collective-permute-start | bytes 1425416 | tf_op jit(solution)/shard_map/ppermute | solution.py:21
  258.4 19.2 %collective-permute-start.51 = (bf16[2,232,512]{2,1,0:T(8,128)(2,1)S(1)}, bf16[2,232,512]{2,1,0:T(8,128)(2,1)}, u32[]{:S(2)}, u32[]{:S(2)}) collective-permute-start(bf16[2,232,512]{2,1,0:T(8,128)(2,1)S(1)} %collective-permute-done.47.refs_7_), channel_id=1, source_target_pairs={{0,96},{32,0},{64,32},{96,64},{1,97},{33,1},{65,33},{97,65},{2,98}... | collective-permute-start | bytes 1425416 | tf_op jit(solution)/shard_map/ppermute | solution.py:21
  263.2 14.4 %collective-permute-start.50 = (bf16[2,232,512]{2,1,0:T(8,128)(2,1)S(1)}, bf16[2,232,512]{2,1,0:T(8,128)(2,1)}, u32[]{:S(2)}, u32[]{:S(2)}) collective-permute-start(bf16[2,232,512]{2,1,0:T(8,128)(2,1)S(1)} %collective-permute-done.40.refs_2_), channel_id=1, source_target_pairs={{0,32},{32,64},{64,96},{96,0},{1,33},{33,65},{65,97},{97,1},{2,34}... | collective-permute-start | bytes 1425416 | tf_op jit(solution)/shard_map/ppermute | solution.py:21
  270.7 10.4 %collective-permute-start.49 = (bf16[2,232,512]{2,1,0:T(8,128)(2,1)}, bf16[2,232,512]{2,1,0:T(8,128)(2,1)}, u32[]{:S(2)}, u32[]{:S(2)}) collective-permute-start(bf16[2,232,512]{2,1,0:T(8,128)(2,1)} %collective-permute-done.45.refs_5_), channel_id=1, source_target_pairs={{0,24},{8,0},{16,8},{24,16},{1,25},{9,1},{17,9},{25,17},{2,26},{10... | collective-permute-start | bytes 1425416 | tf_op jit(solution)/shard_map/ppermute | solution.py:21
  270.7 11.7 %collective-permute-start.48 = (bf16[2,232,512]{2,1,0:T(8,128)(2,1)}, bf16[2,232,512]{2,1,0:T(8,128)(2,1)}, u32[]{:S(2)}, u32[]{:S(2)}) collective-permute-start(bf16[2,232,512]{2,1,0:T(8,128)(2,1)} %collective-permute-done.35.refs_0_), channel_id=1, source_target_pairs={{0,8},{8,16},{16,24},{24,0},{1,9},{9,17},{17,25},{25,1},{2,10},{10... | collective-permute-start | bytes 1425416 | tf_op jit(solution)/shard_map/ppermute | solution.py:21
  290.6 6.5 %collective-permute-start.52 = (bf16[128,512]{1,0:T(8,128)(2,1)}, bf16[128,512]{1,0:T(8,128)(2,1)S(1)}, u32[]{:S(2)}, u32[]{:S(2)}) collective-permute-start(bf16[128,512]{1,0:T(8,128)(2,1)} %get-tuple-element.52), channel_id=1, source_target_pairs={{0,2},{2,4},{4,6},{6,0},{1,3},{3,5},{5,7},{7,1},{8,10},{10,12},{12... | collective-permute-start | bytes 393224 | tf_op jit(solution)/shard_map/ppermute | solution.py:21
  292.5 5.2 %collective-permute-start.53 = (bf16[128,512]{1,0:T(8,128)(2,1)}, bf16[128,512]{1,0:T(8,128)(2,1)S(1)}, u32[]{:S(2)}, u32[]{:S(2)}) collective-permute-start(bf16[128,512]{1,0:T(8,128)(2,1)} %get-tuple-element.53), channel_id=1, source_target_pairs={{0,6},{2,0},{4,2},{6,4},{1,7},{3,1},{5,3},{7,5},{8,14},{10,8},{12,... | collective-permute-start | bytes 393224 | tf_op jit(solution)/shard_map/ppermute | solution.py:21
  293.9 6.7 %collective-permute-start.54 = (bf16[128,512]{1,0:T(8,128)(2,1)}, bf16[128,512]{1,0:T(8,128)(2,1)S(1)}, u32[]{:S(2)}, u32[]{:S(2)}) collective-permute-start(bf16[128,512]{1,0:T(8,128)(2,1)} %get-tuple-element.54), channel_id=1, source_target_pairs={{0,4},{2,6},{4,0},{6,2},{1,5},{3,7},{5,1},{7,3},{8,12},{10,14},{12... | collective-permute-start | bytes 393224 | tf_op jit(solution)/shard_map/ppermute | solution.py:21
  (23 other events, 259.9 us)

commit v3 on v2

--- a/solution.py
+++ b/solution.py
@@ -54,23 +54,23 @@
     return positions + shifted
 
 
-ANY = pl.BlockSpec(memory_space=pl.ANY)
+HBM = pl.BlockSpec(memory_space=pltpu.HBM)
 SMEM = pl.BlockSpec(memory_space=pltpu.SMEM)
 VMEM = pl.BlockSpec(memory_space=pltpu.VMEM)
 
 
-def pieces_kernel(place_ref, gate_ref, up_ref, *refs, axis, base):
+def pieces_kernel(place_ref, gate_ref, up_ref, *refs, wanted):
     outs, sem = refs[:-1], refs[-1]
     copies = []
-    for n, out_ref in enumerate(outs):
-        to = lax.rem(place_ref[axis] + (n + 1) % SIDE, SIDE)
+    for n, (axis, ahead, base) in enumerate(wanted):
+        to = lax.rem(place_ref[axis] + ahead, SIDE)
         for half in range(2):
             first = pl.multiple_of(base + to * BLOCK + half * SUB, 8)
             for kind, ref in enumerate((gate_ref, up_ref)):
                 copies.append(
                     pltpu.make_async_copy(
                         ref.at[pl.ds(first, SUB)],
-                        out_ref.at[half, pl.ds(kind * SUB, SUB)],
+                        outs[n].at[half, pl.ds(kind * SUB, SUB)],
                         sem.at[n, 2 * half + kind],
                     )
                 )
@@ -80,15 +80,20 @@
         copy.wait()
 
 
-def pieces_for(place, gate, up, axis, base):
+def pieces_for(place, gate, up, wanted):
     shape = jax.ShapeDtypeStruct((2, BLOCK, gate.shape[1]), BF16)
     return pl.pallas_call(
-        functools.partial(pieces_kernel, axis=axis, base=base),
-        in_specs=[SMEM] + [ANY] * 2,
-        out_specs=[VMEM] * SIDE,
-        out_shape=[shape] * SIDE,
-        scratch_shapes=[pltpu.SemaphoreType.DMA((SIDE, 4))],
-    )(place, gate, up)
+        functools.partial(pieces_kernel, wanted=wanted),
+        in_specs=[SMEM] + [HBM] * 2,
+        out_specs=[VMEM] * len(wanted),
+        compiler_params=pltpu.CompilerParams(vmem_limit_bytes=10 << 20),
+        out_shape=[shape] * len(wanted),
+        scratch_shapes=[pltpu.SemaphoreType.DMA((len(wanted), 4))],
+    )(place, *in_hbm([gate, up]))
+
+
+def in_hbm(values):
+    return [pltpu.with_memory_space_constraint(value, pltpu.HBM) for value in values]
 
 
 def products_kernel(place_ref, *refs, aheads):
@@ -97,23 +102,15 @@
     features = rows[0].shape[1]
     shares = [(axis, ahead) for ahead in aheads for axis in range(2)]
 
-    def copy(source, target, n, b):
-        return pltpu.make_async_copy(source, target.at[:, pl.ds(b * features, features)], sem.at[n, b])
-
-    def rows_copy(axis, b):
-        return copy(rows[axis * SIDE + b], rows_buf.at[axis], len(shares) + axis, b)
-
     def weight_copy(other, n, b):
         axis, ahead = shares[n]
         at = lax.rem(place_ref[axis] + ahead, SIDE)
         source = weights[(2 * axis + other) * SIDE + b].at[lax.rem(at, 2)]
-        return copy(source, weight_buf.at[n], n, b)
+        target = weight_buf.at[n, :, pl.ds(b * features, features)]
+        return pltpu.make_async_copy(source, target, sem.at[n, b])
 
     for n, (axis, ahead) in enumerate(shares):
         at = lax.rem(place_ref[axis] + ahead, SIDE)
-        if n < 2:
-            for b in range(SIDE):
-                rows_copy(axis, b).start()
 
         @pl.when(at < 2)
         def _(n=n):
@@ -125,10 +122,11 @@
             for b in range(SIDE):
                 weight_copy(1, n, b).start()
 
+    for axis in range(2):
+        for b in range(SIDE):
+            rows_buf[axis, :, b * features : (b + 1) * features] = rows[axis * SIDE + b][...]
     for n, (axis, _) in enumerate(shares):
         for b in range(SIDE):
-            if n < 2:
-                rows_copy(axis, b).wait()
             weight_copy(0, n, b).wait()
         outs[n][...] = lax.dot_general(
             weight_buf[n], rows_buf[axis], (((1,), (1,)), ((), ())), preferred_element_type=F32
@@ -140,8 +138,9 @@
     count = 2 * len(aheads)
     return pl.pallas_call(
         functools.partial(products_kernel, aheads=aheads),
-        in_specs=[SMEM] + [ANY] * (6 * SIDE),
+        in_specs=[SMEM] + [HBM] * (4 * SIDE) + [VMEM] * (2 * SIDE),
         out_specs=[VMEM] * count,
+        compiler_params=pltpu.CompilerParams(vmem_limit_bytes=28 << 20),
         out_shape=[
             jax.ShapeDtypeStruct((BLOCK, tokens), BF16 if ahead else F32)
             for ahead in aheads
@@ -150,9 +149,9 @@
         scratch_shapes=[
             pltpu.VMEM((count, BLOCK, SIDE * features), BF16),
             pltpu.VMEM((2, tokens, SIDE * features), BF16),
-            pltpu.SemaphoreType.DMA((count + 2, SIDE)),
+            pltpu.SemaphoreType.DMA((count, SIDE)),
         ],
-    )(place, *weights, *rows)
+    )(place, *in_hbm(weights[:SIDE]), *weights[SIDE : 2 * SIDE], *in_hbm(weights[2 * SIDE : 3 * SIDE]), *weights[3 * SIDE :], *rows)
 
 
 def hidden_kernel(repeated_ref, *refs):
@@ -174,6 +173,7 @@
         hidden_kernel,
         in_specs=[SMEM] + [VMEM] * len(parts),
         out_specs=[VMEM] * 2,
+        compiler_params=pltpu.CompilerParams(vmem_limit_bytes=16 << 20),
         out_shape=[jax.ShapeDtypeStruct((SUB, parts[0].shape[-1]), BF16)] * 2,
     )(repeated, *parts)
 
@@ -182,7 +182,7 @@
     blocks = 2 * len(which)
     second = own_ref.shape[0] - HALF
     hiddens, refs = refs[: 2 * blocks], refs[2 * blocks :]
-    sums, outs, (weight_buf, hidden_buf, total_ref, sem) = refs[:extra], refs[extra:-4], refs[-4:]
+    sums, outs, (weight_buf, total_ref, sem) = refs[:extra], refs[extra:-3], refs[-3:]
 
     def unit(n, i):
         far_axis = 1 - n % 2
@@ -194,13 +194,8 @@
         first = pl.multiple_of(unit(n, i)[0], 8)
         return pltpu.make_async_copy(core_ref.at[pl.ds(first, SUB)], weight_buf.at[n, i], sem.at[n, i])
 
-    def hidden_copy(n, i):
-        source = hiddens[2 * n + i // 2].at[i % 2]
-        return pltpu.make_async_copy(source, hidden_buf.at[n, i], sem.at[n, SIDE + i])
-
     for n in range(blocks):
         for i in range(SIDE):
-            hidden_copy(n, i).start()
 
             @pl.when(unit(n, i)[1] < 2)
             def _(n=n, i=i):
@@ -212,10 +207,9 @@
 
     for n in range(blocks):
         for i in range(SIDE):
-            hidden_copy(n, i).wait()
             weight_copy(own_ref, n, i).wait()
         term = lax.dot_general(
-            jnp.concatenate([hidden_buf[n, i] for i in range(SIDE)], axis=0),
+            jnp.concatenate([hiddens[2 * n + i // 2][i % 2] for i in range(SIDE)], axis=0),
             jnp.concatenate([weight_buf[n, i] for i in range(SIDE)], axis=0),
             (((0,), (0,)), ((), ())),
             preferred_element_type=F32,
@@ -246,16 +240,16 @@
         out_shape = [jax.ShapeDtypeStruct((tokens, features), F32)]
     outs = pl.pallas_call(
         functools.partial(down_kernel, which=which, extra=len(extra), last=last),
-        in_specs=[SMEM] + [ANY] * (2 + len(hiddens)) + [VMEM] * len(extra),
+        in_specs=[SMEM] + [HBM] * 2 + [VMEM] * (len(hiddens) + len(extra)),
         out_specs=[VMEM] * len(out_shape),
+        compiler_params=pltpu.CompilerParams(vmem_limit_bytes=24 << 20),
         out_shape=out_shape,
         scratch_shapes=[
             pltpu.VMEM((blocks, SIDE, SUB, features), BF16),
-            pltpu.VMEM((blocks, SIDE, SUB, tokens), BF16),
             pltpu.VMEM((tokens, features), F32),
-            pltpu.SemaphoreType.DMA((blocks, 2 * SIDE)),
+            pltpu.SemaphoreType.DMA((blocks, SIDE)),
         ],
-    )(place, own, other, *hiddens, *extra)
+    )(place, *in_hbm([own, other]), *hiddens, *extra)
     return outs if last else outs[0]
 
 
@@ -273,11 +267,16 @@
     blocks, gate_weight, up_weight = lax.optimization_barrier((blocks, gate_weight, up_weight))
     feature_rows = exchange(blocks, ("y", "x")).reshape(-1, features)
 
-    def pieces(axis, base):
-        cut = pieces_for(place, gate_weight.T, up_weight.T, "yx".index(axis), base)
-        return [cut[-1]] + [shift(cut[ahead - 1], axis, ahead) for ahead in range(1, SIDE)]
-
-    own_x, own_y = pieces("x", 0), pieces("y", second)
+    def pieces(wanted):
+        return pieces_for(place, gate_weight.T, up_weight.T, wanted)
+
+    def from_others(axis, base):
+        cut = pieces([("yx".index(axis), ahead, base) for ahead in range(1, SIDE)])
+        return [shift(piece, axis, ahead) for ahead, piece in enumerate(cut, 1)]
+
+    own_x, own_y = from_others("x", 0), from_others("y", second)
+    kept_x, kept_y = pieces([(1, 0, 0), (0, 0, second)])
+    own_x, own_y = [kept_x] + own_x, [kept_y] + own_y
     other_down = shift(down_weight, "core", 1, 2)
     near = around(feature_rows, "z")
     every = jnp.concatenate(near + [shift(r, "core", 1, 2) for r in near], axis=0)

time: 303 us -> 292 us (0.964)
  Pallas kernels: 43.7 us -> 34.8 us
  waiting for transfers between devices: 161 us -> 165 us
  other arithmetic: 4.87 us -> 1.44 us
  local copies, waits for them, and re-layouts: 20.2 us -> 16.9 us
    ppermute x55, waiting for transfers between devices: 151 us -> 155 us  [shift(): lax.ppermute(value, axis, [(i, (i + by) % size) for i in range(size)])]
    pallas_call x2, Pallas kernels: 17.4 us -> 13.5 us  [products(): pl.pallas_call(functools.partial(products_kernel, aheads=aheads), in_spec...]
    pallas_call x2, Pallas kernels: 12.9 us -> 9.43 us  [down_products(): pl.pallas_call(functools.partial(down_kernel, which=which, extra=len(extr...]
    unnamed x69 -> x29, local copies, waits for them, and re-layouts: 13.4 us -> 10.1 us
    pallas_call x2 -> x3, Pallas kernels: 9.77 us -> 10.2 us  [pieces_for(): pl.pallas_call(functools.partial(pieces_kernel, wanted=wanted), in_specs=...]
  transfers between devices with their start and end apart: 56 -> 56, of which waited for: 28 -> 29; matrix products, arithmetic and copies ran while one was open for 6% -> 4% of each run, Pallas kernels for 12% -> 10%
where the time goes in v3:
time: 292 us; the launch traced here: 291 us
  waiting for transfers between devices  165 us (57%)
  starting transfers between devices  72.5 us (25%)
  Pallas kernels  34.8 us (12%)
  local copies, waits for them, and re-layouts  16.9 us (6%)
    ppermute x55, waiting for transfers between devices, shift(): lax.ppermute(value, axis, [(i, (i + by) % size) for i in range(size)])  155 us
    ppermute x55, starting transfers between devices, shift(): lax.ppermute(value, axis, [(i, (i + by) % size) for i in range(size)])  65.3 us
    pallas_call x2, Pallas kernels, products(): pl.pallas_call(functools.partial(products_kernel, aheads=aheads), in_spec...  13.5 us
    pallas_call x3, Pallas kernels, pieces_for(): pl.pallas_call(functools.partial(pieces_kernel, wanted=wanted), in_specs=...  10.2 us
    all_to_all x1, waiting for transfers between devices, exchange(): return lax.all_to_all(value, axis, split_axis=0, concat_axis=0, tiled=True)  10.1 us
    unnamed x29, local copies, waits for them, and re-layouts  10.1 us
    pallas_call x2, Pallas kernels, down_products(): pl.pallas_call(functools.partial(down_kernel, which=which, extra=len(extr...  9.43 us
    all_to_all x1, starting transfers between devices, exchange(): return lax.all_to_all(value, axis, split_axis=0, concat_axis=0, tiled=True)  7.15 us
  transfers between devices with their start and end apart: 56, of which 29 were waited for; matrix products, arithmetic and copies ran while one was open for 4% of the time, Pallas kernels for 10%

profile of v3, /device:TPU:0, one launch (start us, length us, event | category | flops | bytes accessed | tf_op | source)
XLA Modules:
  0.0 290.9 jit_solution(14276351687259906830)
XLA Ops:
  0.0 1.8 copy.13
  1.8 7.1 %all-to-all-start = ((bf16[16,24,512]{2,1,0:T(8,128)(2,1)}), bf16[16,24,512]{2,1,0:T(8,128)(2,1)S(1)}, u32[]{:S(2)}, u32[]{:S(2)}) async-start(bf16[16,24,512]{2,1,0:T(8,128)(2,1)} %bitcast.23), calls=%async_computation | async-start | bytes 786432 | tf_op jit(solution)/shard_map/all_to_all | solution.py:37
  8.9 10.1 %all-to-all-done = bf16[16,24,512]{2,1,0:T(8,128)(2,1)S(1)} async-done(((bf16[16,24,512]{2,1,0:T(8,128)(2,1)}), bf16[16,24,512]{2,1,0:T(8,128)(2,1)S(1)}, u32[]{:S(2)}, u32[]{:S(2)}) %all-to-all-start) | async-done | bytes 393248 | tf_op jit(solution)/shard_map/all_to_all | solution.py:37
  19.0 1.9 collective-permute-start.15
  21.0 3.9 %shard_map.75 = (bf16[2,464,512]{2,1,0:T(8,128)(2,1)}, bf16[2,464,512]{2,1,0:T(8,128)(2,1)}, bf16[2,464,512]{2,1,0:T(8,128)(2,1)S(1)}) custom-call(s32[3]{0:T(128)S(1)} %pad_add_fusion.place_ref, bf16[3696,512]{1,0:T(8,128)(2,1)} %bitcast.26, bf16[3696,512]{1,0:T(8,128)(2,1)} %bitcast.29), custom_call_target="tpu_custom_call" | custom-call | tf_op jit(solution)/shard_map/pallas_call | solution.py:85
  25.0 2.3 collective-permute-start.9
  27.3 1.2 collective-permute-start.10
  28.4 3.6 %collective-permute-start.16 = (bf16[384,512]{1,0:T(8,128)(2,1)S(1)}, bf16[384,512]{1,0:T(8,128)(2,1)S(1)}, u32[]{:S(2)}, u32[]{:S(2)}) collective-permute-start(bf16[384,512]{1,0:T(8,128)(2,1)S(1)} %bitcast.33), channel_id=1, source_target_pairs={{0,4},{2,6},{4,0},{6,2},{1,5},{3,7},{5,1},{7,3},{8,12},{10,14},{12... | collective-permute-start | bytes 1179656 | tf_op jit(solution)/shard_map/ppermute | solution.py:21
  32.3 2.2 collective-permute-start.17
  34.4 6.2 %collective-permute-done.16 = bf16[384,512]{1,0:T(8,128)(2,1)S(1)} collective-permute-done((bf16[384,512]{1,0:T(8,128)(2,1)S(1)}, bf16[384,512]{1,0:T(8,128)(2,1)S(1)}, u32[]{:S(2)}, u32[]{:S(2)}) %collective-permute-start.16) | collective-permute-done | bytes 393248 | tf_op jit(solution)/shard_map/ppermute | solution.py:21
  40.9 6.1 %collective-permute-done.17 = bf16[384,512]{1,0:T(8,128)(2,1)S(1)} collective-permute-done((bf16[384,512]{1,0:T(8,128)(2,1)S(1)}, bf16[384,512]{1,0:T(8,128)(2,1)S(1)}, u32[]{:S(2)}, u32[]{:S(2)}) %collective-permute-start.17) | collective-permute-done | bytes 393248 | tf_op jit(solution)/shard_map/ppermute | solution.py:21
  47.0 4.1 %shard_map.74 = (bf16[2,464,512]{2,1,0:T(8,128)(2,1)}, bf16[2,464,512]{2,1,0:T(8,128)(2,1)}, bf16[2,464,512]{2,1,0:T(8,128)(2,1)}) custom-call(s32[3]{0:T(128)S(1)} %pad_add_fusion.place_ref, bf16[3696,512]{1,0:T(8,128)(2,1)} %bitcast.27, bf16[3696,512]{1,0:T(8,128)(2,1)} %bitcast.30), custom_call_target="tpu_custom_call" | custom-call | tf_op jit(solution)/shard_map/pallas_call | solution.py:85
  51.2 2.2 shard_map.73
  53.8 14.4 %collective-permute-done.8.refs_9_ = bf16[2,464,512]{2,1,0:T(8,128)(2,1)} collective-permute-done((bf16[2,464,512]{2,1,0:T(8,128)(2,1)}, bf16[2,464,512]{2,1,0:T(8,128)(2,1)}, u32[]{:S(2)}, u32[]{:S(2)}) %collective-permute-start.8) | collective-permute-done | bytes 950304 | tf_op jit(solution)/shard_map/ppermute | solution.py:21
  69.5 1.8 constant_dynamic-update-slice_fusion.6
  72.4 2.9 collective-permute-start.3
  79.7 4.3 %gather_fusion = bf16[512,512]{1,0:T(8,128)(2,1)S(1)} fusion(bf16[3072,512]{1,0:T(8,128)(2,1)} %constant_dynamic-update-slice_fusion, s32[1024]{0:T(1024)S(1)} %pad_clamp_fusion), kind=kCustom, calls=%fused_computation | custom fusion | bytes 1050624 | tf_op jit(solution)/shard_map/gather | solution.py:286
  84.0 14.8 %collective-permute-done.1.refs_1_ = bf16[2,464,512]{2,1,0:T(8,128)(2,1)} collective-permute-done((bf16[2,464,512]{2,1,0:T(8,128)(2,1)}, bf16[2,464,512]{2,1,0:T(8,128)(2,1)}, u32[]{:S(2)}, u32[]{:S(2)}) %collective-permute-start.1) | collective-permute-done | bytes 950304 | tf_op jit(solution)/shard_map/ppermute | solution.py:21
  99.9 16.5 %collective-permute-done.3.refs_3_ = bf16[2,464,512]{2,1,0:T(8,128)(2,1)} collective-permute-done((bf16[2,464,512]{2,1,0:T(8,128)(2,1)}, bf16[2,464,512]{2,1,0:T(8,128)(2,1)}, u32[]{:S(2)}, u32[]{:S(2)}) %collective-permute-start.3) | collective-permute-done | bytes 950304 | tf_op jit(solution)/shard_map/ppermute | solution.py:21
  116.4 2.6 collective-permute-start.24
  119.1 5.5 %collective-permute-done.22.refs_17_ = bf16[512,512]{1,0:T(8,128)(2,1)S(1)} collective-permute-done((bf16[512,512]{1,0:T(8,128)(2,1)S(1)}, bf16[512,512]{1,0:T(8,128)(2,1)S(1)}, u32[]{:S(2)}, u32[]{:S(2)}) %collective-permute-start.22) | collective-permute-done | bytes 524320 | tf_op jit(solution)/shard_map/ppermute | solution.py:21
  124.6 2.6 collective-permute-start.26
  127.2 10.7 %collective-permute-done.24.refs_19_ = bf16[512,512]{1,0:T(8,128)(2,1)S(1)} collective-permute-done((bf16[512,512]{1,0:T(8,128)(2,1)S(1)}, bf16[512,512]{1,0:T(8,128)(2,1)S(1)}, u32[]{:S(2)}, u32[]{:S(2)}) %collective-permute-start.24) | collective-permute-done | bytes 524320 | tf_op jit(solution)/shard_map/ppermute | solution.py:21
  137.9 7.0 %collective-permute-done.25.refs_21_ = bf16[512,512]{1,0:T(8,128)(2,1)S(1)} collective-permute-done((bf16[512,512]{1,0:T(8,128)(2,1)S(1)}, bf16[512,512]{1,0:T(8,128)(2,1)S(1)}, u32[]{:S(2)}, u32[]{:S(2)}) %collective-permute-start.25) | collective-permute-done | bytes 524320 | tf_op jit(solution)/shard_map/ppermute | solution.py:21
  145.4 5.6 %collective-permute-done.27.refs_23_ = bf16[512,512]{1,0:T(8,128)(2,1)S(1)} collective-permute-done((bf16[512,512]{1,0:T(8,128)(2,1)S(1)}, bf16[512,512]{1,0:T(8,128)(2,1)S(1)}, u32[]{:S(2)}, u32[]{:S(2)}) %collective-permute-start.27) | collective-permute-done | bytes 524320 | tf_op jit(solution)/shard_map/ppermute | solution.py:21
  151.5 1.5 collective-permute-done.14.refs_15_
  153.0 1.4 collective-permute-done.5.refs_5_
  154.4 1.4 collective-permute-done.6.refs_6_
  155.7 1.4 collective-permute-done.7.refs_7_
  157.1 4.0 %shard_map.77 = (bf16[464,512]{1,0:T(8,128)(2,1)S(1)}, bf16[464,512]{1,0:T(8,128)(2,1)S(1)}) custom-call(s32[3]{0:T(128)S(1)} %pad_add_fusion.place_ref, bf16[2,464,512]{2,1,0:T(8,128)(2,1)} %copy-done, bf16[2,464,512]{2,1,0:T(8,128)(2,1)} %collective-permute-done.1.refs_1_, bf16[2,464,512]{2,1,0:T(8,128)(2,1)} %collective-permute-done.2.refs_2_, ...), custom_call_target="tpu_custom_call" | custom-call | tf_op jit(solution)/shard_map/pallas_call | solution.py:139
  161.1 2.0 collective-permute-start.30
  163.1 1.7 collective-permute-start.33
  164.8 9.4 %shard_map.76 = (bf16[464,512]{1,0:T(8,128)(2,1)}, bf16[464,512]{1,0:T(8,128)(2,1)}, bf16[464,512]{1,0:T(8,128)(2,1)}, bf16[464,512]{1,0:T(8,128)(2,1)}, f32[464,512]{1,0:T(8,128)S(1)}, /*index=5*/f32[464,512]{1,0:T(8,128)S(1)}) custom-call(s32[3]{0:T(128)S(1)} %pad_add_fusion.place_ref, bf16[2,464,512]{2,1,0:T(8,128)(2,1)} %copy-done, ...), custom_call_target="tpu_custom_call" | custom-call | tf_op jit(solution)/shard_map/pallas_call | solution.py:139
  174.3 1.1 collective-permute-start.28
  175.4 2.2 collective-permute-start.29
  180.0 2.4 collective-permute-start.32
  182.4 5.7 %collective-permute-done.28.refs_1_ = bf16[464,512]{1,0:T(8,128)(2,1)S(1)} collective-permute-done((bf16[464,512]{1,0:T(8,128)(2,1)}, bf16[464,512]{1,0:T(8,128)(2,1)S(1)}, u32[]{:S(2)}, u32[]{:S(2)}) %collective-permute-start.28) | collective-permute-done | bytes 475168 | tf_op jit(solution)/shard_map/ppermute | solution.py:21
  188.1 3.5 %collective-permute-done.31.refs_5_ = bf16[464,512]{1,0:T(8,128)(2,1)S(1)} collective-permute-done((bf16[464,512]{1,0:T(8,128)(2,1)}, bf16[464,512]{1,0:T(8,128)(2,1)S(1)}, u32[]{:S(2)}, u32[]{:S(2)}) %collective-permute-start.31) | collective-permute-done | bytes 475168 | tf_op jit(solution)/shard_map/ppermute | solution.py:21
  193.9 1.7 shard_map.78
  195.6 3.1 %collective-permute-start.41 = (bf16[232,512]{1,0:T(8,128)(2,1)S(1)}, bf16[232,512]{1,0:T(8,128)(2,1)S(1)}, u32[]{:S(2)}, u32[]{:S(2)}) collective-permute-start(bf16[232,512]{1,0:T(8,128)(2,1)S(1)} %get-tuple-element.50), channel_id=1, source_target_pairs={{0,16},{8,24},{16,0},{24,8},{1,17},{9,25},{17,1},{25,9},{2,18},{10... | collective-permute-start | bytes 712712 | tf_op jit(solution)/shard_map/ppermute | solution.py:21
  199.5 1.1 collective-permute-start.39
  201.6 3.8 %collective-permute-done.41 = bf16[232,512]{1,0:T(8,128)(2,1)S(1)} collective-permute-done((bf16[232,512]{1,0:T(8,128)(2,1)S(1)}, bf16[232,512]{1,0:T(8,128)(2,1)S(1)}, u32[]{:S(2)}, u32[]{:S(2)}) %collective-permute-start.41) | collective-permute-done | bytes 237600 | tf_op jit(solution)/shard_map/ppermute | solution.py:21
  205.5 1.8 collective-permute-start.37
  207.3 1.4 collective-permute-done.42
  209.4 1.5 collective-permute-start.43
  211.2 2.2 collective-permute-done.37
  213.5 1.3 collective-permute-start.34
  214.8 22.1 %collective-permute-done.34 = bf16[232,512]{1,0:T(8,128)(2,1)S(1)} collective-permute-done((bf16[232,512]{1,0:T(8,128)(2,1)S(1)}, bf16[232,512]{1,0:T(8,128)(2,1)S(1)}, u32[]{:S(2)}, u32[]{:S(2)}) %collective-permute-start.34) | collective-permute-done | bytes 237600 | tf_op jit(solution)/shard_map/ppermute | solution.py:21
  236.9 3.8 %collective-permute-start.45 = (bf16[2,232,512]{2,1,0:T(8,128)(2,1)S(1)}, bf16[2,232,512]{2,1,0:T(8,128)(2,1)S(1)}, u32[]{:S(2)}, u32[]{:S(2)}) collective-permute-start(bf16[2,232,512]{2,1,0:T(8,128)(2,1)S(1)} %pad_maximum_fusion.1.refs_1_), channel_id=1, source_target_pairs={{0,24},{8,0},{16,8},{24,16},{1,25},{9,1},{17,9},{25,17},{2,26},{10... | collective-permute-start | bytes 1425416 | tf_op jit(solution)/shard_map/ppermute | solution.py:21
  241.2 5.8 %collective-permute-done.46.refs_6_ = bf16[2,232,512]{2,1,0:T(8,128)(2,1)S(1)} collective-permute-done((bf16[2,232,512]{2,1,0:T(8,128)(2,1)S(1)}, bf16[2,232,512]{2,1,0:T(8,128)(2,1)S(1)}, u32[]{:S(2)}, u32[]{:S(2)}) %collective-permute-start.46) | collective-permute-done | bytes 475168 | tf_op jit(solution)/shard_map/ppermute | solution.py:21
  247.0 4.8 %collective-permute-start.44 = (bf16[2,232,512]{2,1,0:T(8,128)(2,1)S(1)}, bf16[2,232,512]{2,1,0:T(8,128)(2,1)S(1)}, u32[]{:S(2)}, u32[]{:S(2)}) collective-permute-start(bf16[2,232,512]{2,1,0:T(8,128)(2,1)S(1)} %pad_maximum_fusion.refs_0_), channel_id=1, source_target_pairs={{0,24},{8,0},{16,8},{24,16},{1,25},{9,1},{17,9},{25,17},{2,26},{10... | collective-permute-start | bytes 1425416 | tf_op jit(solution)/shard_map/ppermute | solution.py:21
  251.8 1.5 collective-permute-start.51
  253.3 2.4 collective-permute-done.38.refs_1_
  255.7 2.0 collective-permute-start.50
  257.7 5.3 %collective-permute-done.35.refs_0_ = bf16[2,232,512]{2,1,0:T(8,128)(2,1)S(1)} collective-permute-done((bf16[2,232,512]{2,1,0:T(8,128)(2,1)S(1)}, bf16[2,232,512]{2,1,0:T(8,128)(2,1)S(1)}, u32[]{:S(2)}, u32[]{:S(2)}) %collective-permute-start.35) | collective-permute-done | bytes 475168 | tf_op jit(solution)/shard_map/ppermute | solution.py:21
  263.0 2.0 collective-permute-start.48
  265.0 3.3 %shard_map.79.refs_12_ = f32[512,512]{1,0:T(8,128)S(1)} custom-call(s32[3]{0:T(128)S(1)} %pad_add_fusion.place_ref, bf16[3696,512]{1,0:T(8,128)(2,1)} %own_ref.3, bf16[3696,512]{1,0:T(8,128)(2,1)} %collective-permute-done.other_ref, bf16[2,232,512]{2,1,0:T(8,128)(2,1)S(1)} %pad_maximum_fusion.refs_0_, bf16[2,232,512]{2,1,0:T(8,128)(2,1)S(1)} %pad_maximum_fusion.1.refs_1_, ...), custom_call_target="tpu_custom_call" | custom-call | tf_op jit(solution)/shard_map/pallas_call | solution.py:241
  268.4 4.7 %collective-permute-done.49.refs_9_ = bf16[2,232,512]{2,1,0:T(8,128)(2,1)S(1)} collective-permute-done((bf16[2,232,512]{2,1,0:T(8,128)(2,1)S(1)}, bf16[2,232,512]{2,1,0:T(8,128)(2,1)S(1)}, u32[]{:S(2)}, u32[]{:S(2)}) %collective-permute-start.49) | collective-permute-done | bytes 475168 | tf_op jit(solution)/shard_map/ppermute | solution.py:21
  273.1 1.2 collective-permute-done.48.refs_8_
  274.3 6.1 %shard_map.80 = (f32[128,512]{1,0:T(8,128)S(1)}, bf16[128,512]{1,0:T(8,128)(2,1)S(1)}, bf16[128,512]{1,0:T(8,128)(2,1)S(1)}, bf16[128,512]{1,0:T(8,128)(2,1)S(1)}) custom-call(s32[3]{0:T(128)S(1)} %pad_add_fusion.place_ref, bf16[3696,512]{1,0:T(8,128)(2,1)} %own_ref.3, bf16[3696,512]{1,0:T(8,128)(2,1)} %collective-permute-done.other_ref, ...), custom_call_target="tpu_custom_call" | custom-call | tf_op jit(solution)/shard_map/pallas_call | solution.py:241
  280.4 2.1 collective-permute-start.52
  282.5 1.2 collective-permute-start.53
  283.7 2.4 collective-permute-start.54
  287.4 2.7 collective-permute-done.54
  (100 shorter events, 20.4 us)
Async XLA Ops:
  1.8 17.2 %all-to-all-start = ((bf16[16,24,512]{2,1,0:T(8,128)(2,1)}), bf16[16,24,512]{2,1,0:T(8,128)(2,1)S(1)}, u32[]{:S(2)}, u32[]{:S(2)}) async-start(bf16[16,24,512]{2,1,0:T(8,128)(2,1)} %bitcast.23), calls=%async_computation | async-start | bytes 786432 | tf_op jit(solution)/shard_map/all_to_all | solution.py:37
  19.0 13.2 %collective-permute-start.15 = (bf16[384,512]{1,0:T(8,128)(2,1)S(1)}, bf16[384,512]{1,0:T(8,128)(2,1)}, u32[]{:S(2)}, u32[]{:S(2)}) collective-permute-start(bf16[384,512]{1,0:T(8,128)(2,1)S(1)} %bitcast.32), channel_id=1, source_target_pairs={{0,2},{2,4},{4,6},{6,0},{1,3},{3,5},{5,7},{7,1},{8,10},{10,12},{12... | collective-permute-start | bytes 1179656 | tf_op jit(solution)/shard_map/ppermute | solution.py:21
  21.0 11.0 %copy-start.8 = (s32[128]{0:T(128)S(1)}, s32[128]{0:T(128)}, u32[]{:S(2)}) copy-start(s32[128]{0:T(128)} %param.10) | copy-start | bytes 1540
  21.0 11.0 %copy-start.9 = (s32[128]{0:T(128)S(1)}, s32[128]{0:T(128)}, u32[]{:S(2)}) copy-start(s32[128]{0:T(128)} %param.8) | copy-start | bytes 1540
  21.0 11.2 %copy-start.10 = (s32[128]{0:T(128)S(1)}, s32[128]{0:T(128)}, u32[]{:S(2)}) copy-start(s32[128]{0:T(128)} %param.9) | copy-start | bytes 1540
  24.9 43.3 %collective-permute-start.8 = (bf16[2,464,512]{2,1,0:T(8,128)(2,1)}, bf16[2,464,512]{2,1,0:T(8,128)(2,1)}, u32[]{:S(2)}, u32[]{:S(2)}) collective-permute-start(bf16[2,464,512]{2,1,0:T(8,128)(2,1)} %get-tuple-element.37), channel_id=1, source_target_pairs={{0,32},{32,64},{64,96},{96,0},{1,33},{33,65},{65,97},{97,1},{2,34}... | collective-permute-start | bytes 2850824 | tf_op jit(solution)/shard_map/ppermute | solution.py:21
  25.0 43.3 %collective-permute-start.9 = (bf16[2,464,512]{2,1,0:T(8,128)(2,1)}, bf16[2,464,512]{2,1,0:T(8,128)(2,1)}, u32[]{:S(2)}, u32[]{:S(2)}) collective-permute-start(bf16[2,464,512]{2,1,0:T(8,128)(2,1)} %get-tuple-element.38), channel_id=1, source_target_pairs={{0,64},{32,96},{64,0},{96,32},{1,65},{33,97},{65,1},{97,33},{2,66}... | collective-permute-start | bytes 2850824 | tf_op jit(solution)/shard_map/ppermute | solution.py:21
  27.3 44.8 %collective-permute-start.10 = (bf16[2,464,512]{2,1,0:T(8,128)(2,1)S(1)}, bf16[2,464,512]{2,1,0:T(8,128)(2,1)}, u32[]{:S(2)}, u32[]{:S(2)}) collective-permute-start(bf16[2,464,512]{2,1,0:T(8,128)(2,1)S(1)} %get-tuple-element.39), channel_id=1, source_target_pairs={{0,96},{32,0},{64,32},{96,64},{1,97},{33,1},{65,33},{97,65},{2,98}... | collective-permute-start | bytes 2850824 | tf_op jit(solution)/shard_map/ppermute | solution.py:21
  28.4 12.2 %collective-permute-start.16 = (bf16[384,512]{1,0:T(8,128)(2,1)S(1)}, bf16[384,512]{1,0:T(8,128)(2,1)S(1)}, u32[]{:S(2)}, u32[]{:S(2)}) collective-permute-start(bf16[384,512]{1,0:T(8,128)(2,1)S(1)} %bitcast.33), channel_id=1, source_target_pairs={{0,4},{2,6},{4,0},{6,2},{1,5},{3,7},{5,1},{7,3},{8,12},{10,14},{12... | collective-permute-start | bytes 1179656 | tf_op jit(solution)/shard_map/ppermute | solution.py:21
  32.3 14.7 %collective-permute-start.17 = (bf16[384,512]{1,0:T(8,128)(2,1)S(1)}, bf16[384,512]{1,0:T(8,128)(2,1)S(1)}, u32[]{:S(2)}, u32[]{:S(2)}) collective-permute-start(bf16[384,512]{1,0:T(8,128)(2,1)S(1)} %bitcast.34), channel_id=1, source_target_pairs={{0,6},{2,0},{4,2},{6,4},{1,7},{3,1},{5,3},{7,5},{8,14},{10,8},{12,... | collective-permute-start | bytes 1179656 | tf_op jit(solution)/shard_map/ppermute | solution.py:21
  40.6 6.4 %copy-start.6 = (bf16[384,512]{1,0:T(8,128)(2,1)}, bf16[384,512]{1,0:T(8,128)(2,1)S(1)}, u32[]{:S(2)}) copy-start(bf16[384,512]{1,0:T(8,128)(2,1)S(1)} %collective-permute-done.16) | copy-start | bytes 1179652
  40.6 12.7 %collective-permute-start.18 = (bf16[384,512]{1,0:T(8,128)(2,1)S(1)}, bf16[384,512]{1,0:T(8,128)(2,1)S(1)}, u32[]{:S(2)}, u32[]{:S(2)}) collective-permute-start(bf16[384,512]{1,0:T(8,128)(2,1)S(1)} %bitcast.35), channel_id=1, source_target_pairs={{0,1},{1,0},{2,3},{3,2},{4,5},{5,4},{6,7},{7,6},{8,9},{9,8},{10,11... | collective-permute-start | bytes 1179656 | tf_op jit(solution)/shard_map/ppermute | solution.py:21
  47.0 25.4 %collective-permute-start.19 = (bf16[384,512]{1,0:T(8,128)(2,1)}, bf16[384,512]{1,0:T(8,128)(2,1)S(1)}, u32[]{:S(2)}, u32[]{:S(2)}) collective-permute-start(bf16[384,512]{1,0:T(8,128)(2,1)} %collective-permute-done.15), channel_id=1, source_target_pairs={{0,1},{1,0},{2,3},{3,2},{4,5},{5,4},{6,7},{7,6},{8,9},{9,8},{10,11... | collective-permute-start | bytes 1179656 | tf_op jit(solution)/shard_map/ppermute | solution.py:21
  51.2 17.1 %copy-start.7 = (bf16[384,512]{1,0:T(8,128)(2,1)S(1)}, bf16[384,512]{1,0:T(8,128)(2,1)}, u32[]{:S(2)}) copy-start(bf16[384,512]{1,0:T(8,128)(2,1)} %copy-done.6) | copy-start | bytes 1179652
  53.4 26.3 %copy-start = (bf16[2,464,512]{2,1,0:T(8,128)(2,1)}, bf16[2,464,512]{2,1,0:T(8,128)(2,1)S(1)}, u32[]{:S(2)}) copy-start(bf16[2,464,512]{2,1,0:T(8,128)(2,1)S(1)} %get-tuple-element.32.refs_0_) | copy-start | bytes 2850820
  53.4 26.3 %copy-start.1 = (bf16[2,464,512]{2,1,0:T(8,128)(2,1)}, bf16[2,464,512]{2,1,0:T(8,128)(2,1)S(1)}, u32[]{:S(2)}) copy-start(bf16[2,464,512]{2,1,0:T(8,128)(2,1)S(1)} %get-tuple-element.36.refs_8_) | copy-start | bytes 2850820
  53.4 45.4 %collective-permute-start.1 = (bf16[2,464,512]{2,1,0:T(8,128)(2,1)}, bf16[2,464,512]{2,1,0:T(8,128)(2,1)}, u32[]{:S(2)}, u32[]{:S(2)}) collective-permute-start(bf16[2,464,512]{2,1,0:T(8,128)(2,1)} %get-tuple-element.33), channel_id=1, source_target_pairs={{0,8},{8,16},{16,24},{24,0},{1,9},{9,17},{17,25},{25,1},{2,10},{10... | collective-permute-start | bytes 2850824 | tf_op jit(solution)/shard_map/ppermute | solution.py:21
  68.2 7.8 %collective-permute-start.20 = (bf16[384,512]{1,0:T(8,128)(2,1)S(1)}, bf16[384,512]{1,0:T(8,128)(2,1)S(1)}, u32[]{:S(2)}, u32[]{:S(2)}) collective-permute-start(bf16[384,512]{1,0:T(8,128)(2,1)S(1)} %copy-done.7), channel_id=1, source_target_pairs={{0,1},{1,0},{2,3},{3,2},{4,5},{5,4},{6,7},{7,6},{8,9},{9,8},{10,11... | collective-permute-start | bytes 1179656 | tf_op jit(solution)/shard_map/ppermute | solution.py:21
  68.2 7.8 %collective-permute-start.21 = (bf16[384,512]{1,0:T(8,128)(2,1)S(1)}, bf16[384,512]{1,0:T(8,128)(2,1)S(1)}, u32[]{:S(2)}, u32[]{:S(2)}) collective-permute-start(bf16[384,512]{1,0:T(8,128)(2,1)S(1)} %collective-permute-done.17), channel_id=1, source_target_pairs={{0,1},{1,0},{2,3},{3,2},{4,5},{5,4},{6,7},{7,6},{8,9},{9,8},{10,11... | collective-permute-start | bytes 1179656 | tf_op jit(solution)/shard_map/ppermute | solution.py:21
  72.1 26.7 %collective-permute-start.2 = (bf16[2,464,512]{2,1,0:T(8,128)(2,1)}, bf16[2,464,512]{2,1,0:T(8,128)(2,1)}, u32[]{:S(2)}, u32[]{:S(2)}) collective-permute-start(bf16[2,464,512]{2,1,0:T(8,128)(2,1)} %get-tuple-element.34), channel_id=1, source_target_pairs={{0,16},{8,24},{16,0},{24,8},{1,17},{9,25},{17,1},{25,9},{2,18},{10... | collective-permute-start | bytes 2850824 | tf_op jit(solution)/shard_map/ppermute | solution.py:21
  72.4 44.0 %collective-permute-start.3 = (bf16[2,464,512]{2,1,0:T(8,128)(2,1)}, bf16[2,464,512]{2,1,0:T(8,128)(2,1)}, u32[]{:S(2)}, u32[]{:S(2)}) collective-permute-start(bf16[2,464,512]{2,1,0:T(8,128)(2,1)} %get-tuple-element.35), channel_id=1, source_target_pairs={{0,24},{8,0},{16,8},{24,16},{1,25},{9,1},{17,9},{25,17},{2,26},{10... | collective-permute-start | bytes 2850824 | tf_op jit(solution)/shard_map/ppermute | solution.py:21
  76.1 42.9 %collective-permute-start.11 = (bf16[2,464,512]{2,1,0:T(8,128)(2,1)S(1)}, bf16[2,464,512]{2,1,0:T(8,128)(2,1)S(1)}, u32[]{:S(2)}, u32[]{:S(2)}) collective-permute-start(bf16[2,464,512]{2,1,0:T(8,128)(2,1)S(1)} %get-tuple-element.36.refs_8_), channel_id=1, source_target_pairs={{0,1},{1,0},{2,3},{3,2},{4,5},{5,4},{6,7},{7,6},{8,9},{9,8},{10,11... | collective-permute-start | bytes 2850824 | tf_op jit(solution)/shard_map/ppermute | solution.py:21
  76.1 42.9 %collective-permute-start.4 = (bf16[2,464,512]{2,1,0:T(8,128)(2,1)S(1)}, bf16[2,464,512]{2,1,0:T(8,128)(2,1)}, u32[]{:S(2)}, u32[]{:S(2)}) collective-permute-start(bf16[2,464,512]{2,1,0:T(8,128)(2,1)S(1)} %get-tuple-element.32.refs_0_), channel_id=1, source_target_pairs={{0,1},{1,0},{2,3},{3,2},{4,5},{5,4},{6,7},{7,6},{8,9},{9,8},{10,11... | collective-permute-start | bytes 2850824 | tf_op jit(solution)/shard_map/ppermute | solution.py:21
  98.8 25.8 %collective-permute-start.22 = (bf16[512,512]{1,0:T(8,128)(2,1)S(1)}, bf16[512,512]{1,0:T(8,128)(2,1)S(1)}, u32[]{:S(2)}, u32[]{:S(2)}) collective-permute-start(bf16[512,512]{1,0:T(8,128)(2,1)S(1)} %gather_fusion), channel_id=1, source_target_pairs={{0,8},{8,16},{16,24},{24,0},{1,9},{9,17},{17,25},{25,1},{2,10},{10... | collective-permute-start | bytes 1572872 | tf_op jit(solution)/shard_map/ppermute | solution.py:21
  98.8 25.8 %collective-permute-start.23 = (bf16[512,512]{1,0:T(8,128)(2,1)S(1)}, bf16[512,512]{1,0:T(8,128)(2,1)S(1)}, u32[]{:S(2)}, u32[]{:S(2)}) collective-permute-start(bf16[512,512]{1,0:T(8,128)(2,1)S(1)} %gather_fusion), channel_id=1, source_target_pairs={{0,16},{8,24},{16,0},{24,8},{1,17},{9,25},{17,1},{25,9},{2,18},{10... | collective-permute-start | bytes 1572872 | tf_op jit(solution)/shard_map/ppermute | solution.py:21
  116.4 21.5 %collective-permute-start.24 = (bf16[512,512]{1,0:T(8,128)(2,1)S(1)}, bf16[512,512]{1,0:T(8,128)(2,1)S(1)}, u32[]{:S(2)}, u32[]{:S(2)}) collective-permute-start(bf16[512,512]{1,0:T(8,128)(2,1)S(1)} %gather_fusion), channel_id=1, source_target_pairs={{0,24},{8,0},{16,8},{24,16},{1,25},{9,1},{17,9},{25,17},{2,26},{10... | collective-permute-start | bytes 1572872 | tf_op jit(solution)/shard_map/ppermute | solution.py:21
  119.0 25.9 %collective-permute-start.25 = (bf16[512,512]{1,0:T(8,128)(2,1)S(1)}, bf16[512,512]{1,0:T(8,128)(2,1)S(1)}, u32[]{:S(2)}, u32[]{:S(2)}) collective-permute-start(bf16[512,512]{1,0:T(8,128)(2,1)S(1)} %gather_fusion), channel_id=1, source_target_pairs={{0,32},{32,64},{64,96},{96,0},{1,33},{33,65},{65,97},{97,1},{2,34}... | collective-permute-start | bytes 1572872 | tf_op jit(solution)/shard_map/ppermute | solution.py:21
  119.0 32.0 %collective-permute-start.12 = (bf16[2,464,512]{2,1,0:T(8,128)(2,1)}, bf16[2,464,512]{2,1,0:T(8,128)(2,1)S(1)}, u32[]{:S(2)}, u32[]{:S(2)}) collective-permute-start(bf16[2,464,512]{2,1,0:T(8,128)(2,1)} %collective-permute-done.8.refs_9_), channel_id=1, source_target_pairs={{0,1},{1,0},{2,3},{3,2},{4,5},{5,4},{6,7},{7,6},{8,9},{9,8},{10,11... | collective-permute-start | bytes 2850824 | tf_op jit(solution)/shard_map/ppermute | solution.py:21
  124.6 26.9 %collective-permute-start.13 = (bf16[2,464,512]{2,1,0:T(8,128)(2,1)}, bf16[2,464,512]{2,1,0:T(8,128)(2,1)S(1)}, u32[]{:S(2)}, u32[]{:S(2)}) collective-permute-start(bf16[2,464,512]{2,1,0:T(8,128)(2,1)} %collective-permute-done.9.refs_10_), channel_id=1, source_target_pairs={{0,1},{1,0},{2,3},{3,2},{4,5},{5,4},{6,7},{7,6},{8,9},{9,8},{10,11... | collective-permute-start | bytes 2850824 | tf_op jit(solution)/shard_map/ppermute | solution.py:21
  124.6 20.3 %collective-permute-start.26 = (bf16[512,512]{1,0:T(8,128)(2,1)S(1)}, bf16[512,512]{1,0:T(8,128)(2,1)S(1)}, u32[]{:S(2)}, u32[]{:S(2)}) collective-permute-start(bf16[512,512]{1,0:T(8,128)(2,1)S(1)} %gather_fusion), channel_id=1, source_target_pairs={{0,64},{32,96},{64,0},{96,32},{1,65},{33,97},{65,1},{97,33},{2,66}... | collective-permute-start | bytes 1572872 | tf_op jit(solution)/shard_map/ppermute | solution.py:21
  137.9 13.1 %collective-permute-start.27 = (bf16[512,512]{1,0:T(8,128)(2,1)S(1)}, bf16[512,512]{1,0:T(8,128)(2,1)S(1)}, u32[]{:S(2)}, u32[]{:S(2)}) collective-permute-start(bf16[512,512]{1,0:T(8,128)(2,1)S(1)} %gather_fusion), channel_id=1, source_target_pairs={{0,96},{32,0},{64,32},{96,64},{1,97},{33,1},{65,33},{97,65},{2,98}... | collective-permute-start | bytes 1572872 | tf_op jit(solution)/shard_map/ppermute | solution.py:21
  144.9 118.1 %collective-permute-start = (bf16[3696,512]{1,0:T(8,128)(2,1)}, bf16[3696,512]{1,0:T(8,128)(2,1)}, u32[]{:S(2)}, u32[]{:S(2)}) collective-permute-start(bf16[3696,512]{1,0:T(8,128)(2,1)} %own_ref.3), channel_id=1, source_target_pairs={{0,1},{1,0},{2,3},{3,2},{4,5},{5,4},{6,7},{7,6},{8,9},{9,8},{10,11... | collective-permute-start | bytes 11354120 | tf_op jit(solution)/shard_map/ppermute | solution.py:21
  144.9 8.1 %collective-permute-start.14 = (bf16[2,464,512]{2,1,0:T(8,128)(2,1)}, bf16[2,464,512]{2,1,0:T(8,128)(2,1)S(1)}, u32[]{:S(2)}, u32[]{:S(2)}) collective-permute-start(bf16[2,464,512]{2,1,0:T(8,128)(2,1)} %collective-permute-done.10.refs_11_), channel_id=1, source_target_pairs={{0,1},{1,0},{2,3},{3,2},{4,5},{5,4},{6,7},{7,6},{8,9},{9,8},{10,11... | collective-permute-start | bytes 2850824 | tf_op jit(solution)/shard_map/ppermute | solution.py:21
  150.9 3.4 %collective-permute-start.5 = (bf16[2,464,512]{2,1,0:T(8,128)(2,1)}, bf16[2,464,512]{2,1,0:T(8,128)(2,1)S(1)}, u32[]{:S(2)}, u32[]{:S(2)}) collective-permute-start(bf16[2,464,512]{2,1,0:T(8,128)(2,1)} %collective-permute-done.1.refs_1_), channel_id=1, source_target_pairs={{0,1},{1,0},{2,3},{3,2},{4,5},{5,4},{6,7},{7,6},{8,9},{9,8},{10,11... | collective-permute-start | bytes 2850824 | tf_op jit(solution)/shard_map/ppermute | solution.py:21
  151.0 4.8 %collective-permute-start.6 = (bf16[2,464,512]{2,1,0:T(8,128)(2,1)}, bf16[2,464,512]{2,1,0:T(8,128)(2,1)S(1)}, u32[]{:S(2)}, u32[]{:S(2)}) collective-permute-start(bf16[2,464,512]{2,1,0:T(8,128)(2,1)} %collective-permute-done.2.refs_2_), channel_id=1, source_target_pairs={{0,1},{1,0},{2,3},{3,2},{4,5},{5,4},{6,7},{7,6},{8,9},{9,8},{10,11... | collective-permute-start | bytes 2850824 | tf_op jit(solution)/shard_map/ppermute | solution.py:21
  151.5 5.6 %collective-permute-start.7 = (bf16[2,464,512]{2,1,0:T(8,128)(2,1)}, bf16[2,464,512]{2,1,0:T(8,128)(2,1)S(1)}, u32[]{:S(2)}, u32[]{:S(2)}) collective-permute-start(bf16[2,464,512]{2,1,0:T(8,128)(2,1)} %collective-permute-done.3.refs_3_), channel_id=1, source_target_pairs={{0,1},{1,0},{2,3},{3,2},{4,5},{5,4},{6,7},{7,6},{8,9},{9,8},{10,11... | collective-permute-start | bytes 2850824 | tf_op jit(solution)/shard_map/ppermute | solution.py:21
  161.1 16.5 %collective-permute-start.30 = (bf16[464,512]{1,0:T(8,128)(2,1)S(1)}, bf16[464,512]{1,0:T(8,128)(2,1)S(1)}, u32[]{:S(2)}, u32[]{:S(2)}) collective-permute-start(bf16[464,512]{1,0:T(8,128)(2,1)S(1)} %get-tuple-element.44), channel_id=1, source_target_pairs={{0,64},{32,96},{64,0},{96,32},{1,65},{33,97},{65,1},{97,33},{2,66}... | collective-permute-start | bytes 1425416 | tf_op jit(solution)/shard_map/ppermute | solution.py:21
  163.1 16.1 %collective-permute-start.33 = (bf16[464,512]{1,0:T(8,128)(2,1)S(1)}, bf16[464,512]{1,0:T(8,128)(2,1)S(1)}, u32[]{:S(2)}, u32[]{:S(2)}) collective-permute-start(bf16[464,512]{1,0:T(8,128)(2,1)S(1)} %get-tuple-element.48), channel_id=1, source_target_pairs={{0,16},{8,24},{16,0},{24,8},{1,17},{9,25},{17,1},{25,9},{2,18},{10... | collective-permute-start | bytes 1425416 | tf_op jit(solution)/shard_map/ppermute | solution.py:21
  174.3 13.8 %collective-permute-start.28 = (bf16[464,512]{1,0:T(8,128)(2,1)}, bf16[464,512]{1,0:T(8,128)(2,1)S(1)}, u32[]{:S(2)}, u32[]{:S(2)}) collective-permute-start(bf16[464,512]{1,0:T(8,128)(2,1)} %get-tuple-element.42), channel_id=1, source_target_pairs={{0,32},{32,64},{64,96},{96,0},{1,33},{33,65},{65,97},{97,1},{2,34}... | collective-permute-start | bytes 1425416 | tf_op jit(solution)/shard_map/ppermute | solution.py:21
  175.4 12.8 %collective-permute-start.29 = (bf16[464,512]{1,0:T(8,128)(2,1)}, bf16[464,512]{1,0:T(8,128)(2,1)S(1)}, u32[]{:S(2)}, u32[]{:S(2)}) collective-permute-start(bf16[464,512]{1,0:T(8,128)(2,1)} %get-tuple-element.43), channel_id=1, source_target_pairs={{0,96},{32,0},{64,32},{96,64},{1,97},{33,1},{65,33},{97,65},{2,98}... | collective-permute-start | bytes 1425416 | tf_op jit(solution)/shard_map/ppermute | solution.py:21
  178.4 13.2 %collective-permute-start.31 = (bf16[464,512]{1,0:T(8,128)(2,1)}, bf16[464,512]{1,0:T(8,128)(2,1)S(1)}, u32[]{:S(2)}, u32[]{:S(2)}) collective-permute-start(bf16[464,512]{1,0:T(8,128)(2,1)} %get-tuple-element.46), channel_id=1, source_target_pairs={{0,8},{8,16},{16,24},{24,0},{1,9},{9,17},{17,25},{25,1},{2,10},{10... | collective-permute-start | bytes 1425416 | tf_op jit(solution)/shard_map/ppermute | solution.py:21
  180.0 11.8 %collective-permute-start.32 = (bf16[464,512]{1,0:T(8,128)(2,1)}, bf16[464,512]{1,0:T(8,128)(2,1)}, u32[]{:S(2)}, u32[]{:S(2)}) collective-permute-start(bf16[464,512]{1,0:T(8,128)(2,1)} %get-tuple-element.47), channel_id=1, source_target_pairs={{0,24},{8,0},{16,8},{24,16},{1,25},{9,1},{17,9},{25,17},{2,26},{10... | collective-permute-start | bytes 1425416 | tf_op jit(solution)/shard_map/ppermute | solution.py:21
  191.8 1.0 copy-start.3
  195.6 9.9 %collective-permute-start.41 = (bf16[232,512]{1,0:T(8,128)(2,1)S(1)}, bf16[232,512]{1,0:T(8,128)(2,1)S(1)}, u32[]{:S(2)}, u32[]{:S(2)}) collective-permute-start(bf16[232,512]{1,0:T(8,128)(2,1)S(1)} %get-tuple-element.50), channel_id=1, source_target_pairs={{0,16},{8,24},{16,0},{24,8},{1,17},{9,25},{17,1},{25,9},{2,18},{10... | collective-permute-start | bytes 712712 | tf_op jit(solution)/shard_map/ppermute | solution.py:21
  198.6 10.1 %collective-permute-start.42 = (bf16[232,512]{1,0:T(8,128)(2,1)S(1)}, bf16[232,512]{1,0:T(8,128)(2,1)S(1)}, u32[]{:S(2)}, u32[]{:S(2)}) collective-permute-start(bf16[232,512]{1,0:T(8,128)(2,1)S(1)} %get-tuple-element.50), channel_id=1, source_target_pairs={{0,24},{8,0},{16,8},{24,16},{1,25},{9,1},{17,9},{25,17},{2,26},{10... | collective-permute-start | bytes 712712 | tf_op jit(solution)/shard_map/ppermute | solution.py:21
  199.5 9.9 %collective-permute-start.39 = (bf16[232,512]{1,0:T(8,128)(2,1)S(1)}, bf16[232,512]{1,0:T(8,128)(2,1)S(1)}, u32[]{:S(2)}, u32[]{:S(2)}) collective-permute-start(bf16[232,512]{1,0:T(8,128)(2,1)S(1)} %get-tuple-element.50), channel_id=1, source_target_pairs={{0,8},{8,16},{16,24},{24,0},{1,9},{9,17},{17,25},{25,1},{2,10},{10... | collective-permute-start | bytes 712712 | tf_op jit(solution)/shard_map/ppermute | solution.py:21
  200.7 10.3 %collective-permute-start.36 = (bf16[232,512]{1,0:T(8,128)(2,1)S(1)}, bf16[232,512]{1,0:T(8,128)(2,1)S(1)}, u32[]{:S(2)}, u32[]{:S(2)}) collective-permute-start(bf16[232,512]{1,0:T(8,128)(2,1)S(1)} %get-tuple-element.49), channel_id=1, source_target_pairs={{0,64},{32,96},{64,0},{96,32},{1,65},{33,97},{65,1},{97,33},{2,66}... | collective-permute-start | bytes 712712 | tf_op jit(solution)/shard_map/ppermute | solution.py:21
  205.5 8.0 %collective-permute-start.37 = (bf16[232,512]{1,0:T(8,128)(2,1)S(1)}, bf16[232,512]{1,0:T(8,128)(2,1)S(1)}, u32[]{:S(2)}, u32[]{:S(2)}) collective-permute-start(bf16[232,512]{1,0:T(8,128)(2,1)S(1)} %get-tuple-element.49), channel_id=1, source_target_pairs={{0,96},{32,0},{64,32},{96,64},{1,97},{33,1},{65,33},{97,65},{2,98}... | collective-permute-start | bytes 712712 | tf_op jit(solution)/shard_map/ppermute | solution.py:21
  208.8 28.2 %collective-permute-start.47 = (bf16[2,232,512]{2,1,0:T(8,128)(2,1)S(1)}, bf16[2,232,512]{2,1,0:T(8,128)(2,1)S(1)}, u32[]{:S(2)}, u32[]{:S(2)}) collective-permute-start(bf16[2,232,512]{2,1,0:T(8,128)(2,1)S(1)} %pad_maximum_fusion.3.refs_3_), channel_id=1, source_target_pairs={{0,96},{32,0},{64,32},{96,64},{1,97},{33,1},{65,33},{97,65},{2,98}... | collective-permute-start | bytes 1425416 | tf_op jit(solution)/shard_map/ppermute | solution.py:21
  209.4 31.3 %collective-permute-start.43 = (bf16[2,232,512]{2,1,0:T(8,128)(2,1)S(1)}, bf16[2,232,512]{2,1,0:T(8,128)(2,1)S(1)}, u32[]{:S(2)}, u32[]{:S(2)}) collective-permute-start(bf16[2,232,512]{2,1,0:T(8,128)(2,1)S(1)} %pad_maximum_fusion.3.refs_3_), channel_id=1, source_target_pairs={{0,32},{32,64},{64,96},{96,0},{1,33},{33,65},{65,97},{97,1},{2,34}... | collective-permute-start | bytes 1425416 | tf_op jit(solution)/shard_map/ppermute | solution.py:21
  210.9 29.8 %collective-permute-start.40 = (bf16[2,232,512]{2,1,0:T(8,128)(2,1)S(1)}, bf16[2,232,512]{2,1,0:T(8,128)(2,1)S(1)}, u32[]{:S(2)}, u32[]{:S(2)}) collective-permute-start(bf16[2,232,512]{2,1,0:T(8,128)(2,1)S(1)} %pad_maximum_fusion.2.refs_2_), channel_id=1, source_target_pairs={{0,32},{32,64},{64,96},{96,0},{1,33},{33,65},{65,97},{97,1},{2,34}... | collective-permute-start | bytes 1425416 | tf_op jit(solution)/shard_map/ppermute | solution.py:21
  213.5 23.4 %collective-permute-start.34 = (bf16[232,512]{1,0:T(8,128)(2,1)S(1)}, bf16[232,512]{1,0:T(8,128)(2,1)S(1)}, u32[]{:S(2)}, u32[]{:S(2)}) collective-permute-start(bf16[232,512]{1,0:T(8,128)(2,1)S(1)} %get-tuple-element.49), channel_id=1, source_target_pairs={{0,32},{32,64},{64,96},{96,0},{1,33},{33,65},{65,97},{97,1},{2,34}... | collective-permute-start | bytes 712712 | tf_op jit(solution)/shard_map/ppermute | solution.py:21
  236.9 10.1 %collective-permute-start.46 = (bf16[2,232,512]{2,1,0:T(8,128)(2,1)S(1)}, bf16[2,232,512]{2,1,0:T(8,128)(2,1)S(1)}, u32[]{:S(2)}, u32[]{:S(2)}) collective-permute-start(bf16[2,232,512]{2,1,0:T(8,128)(2,1)S(1)} %pad_maximum_fusion.2.refs_2_), channel_id=1, source_target_pairs={{0,96},{32,0},{64,32},{96,64},{1,97},{33,1},{65,33},{97,65},{2,98}... | collective-permute-start | bytes 1425416 | tf_op jit(solution)/shard_map/ppermute | solution.py:21
  236.9 14.8 %collective-permute-start.45 = (bf16[2,232,512]{2,1,0:T(8,128)(2,1)S(1)}, bf16[2,232,512]{2,1,0:T(8,128)(2,1)S(1)}, u32[]{:S(2)}, u32[]{:S(2)}) collective-permute-start(bf16[2,232,512]{2,1,0:T(8,128)(2,1)S(1)} %pad_maximum_fusion.1.refs_1_), channel_id=1, source_target_pairs={{0,24},{8,0},{16,8},{24,16},{1,25},{9,1},{17,9},{25,17},{2,26},{10... | collective-permute-start | bytes 1425416 | tf_op jit(solution)/shard_map/ppermute | solution.py:21
  240.7 15.0 %collective-permute-start.38 = (bf16[2,232,512]{2,1,0:T(8,128)(2,1)S(1)}, bf16[2,232,512]{2,1,0:T(8,128)(2,1)S(1)}, u32[]{:S(2)}, u32[]{:S(2)}) collective-permute-start(bf16[2,232,512]{2,1,0:T(8,128)(2,1)S(1)} %pad_maximum_fusion.1.refs_1_), channel_id=1, source_target_pairs={{0,8},{8,16},{16,24},{24,0},{1,9},{9,17},{17,25},{25,1},{2,10},{10... | collective-permute-start | bytes 1425416 | tf_op jit(solution)/shard_map/ppermute | solution.py:21
  240.7 22.3 %collective-permute-start.35 = (bf16[2,232,512]{2,1,0:T(8,128)(2,1)S(1)}, bf16[2,232,512]{2,1,0:T(8,128)(2,1)S(1)}, u32[]{:S(2)}, u32[]{:S(2)}) collective-permute-start(bf16[2,232,512]{2,1,0:T(8,128)(2,1)S(1)} %pad_maximum_fusion.refs_0_), channel_id=1, source_target_pairs={{0,8},{8,16},{16,24},{24,0},{1,9},{9,17},{17,25},{25,1},{2,10},{10... | collective-permute-start | bytes 1425416 | tf_op jit(solution)/shard_map/ppermute | solution.py:21
  247.0 21.4 %collective-permute-start.44 = (bf16[2,232,512]{2,1,0:T(8,128)(2,1)S(1)}, bf16[2,232,512]{2,1,0:T(8,128)(2,1)S(1)}, u32[]{:S(2)}, u32[]{:S(2)}) collective-permute-start(bf16[2,232,512]{2,1,0:T(8,128)(2,1)S(1)} %pad_maximum_fusion.refs_0_), channel_id=1, source_target_pairs={{0,24},{8,0},{16,8},{24,16},{1,25},{9,1},{17,9},{25,17},{2,26},{10... | collective-permute-start | bytes 1425416 | tf_op jit(solution)/shard_map/ppermute | solution.py:21
  251.8 16.6 %collective-permute-start.51 = (bf16[2,232,512]{2,1,0:T(8,128)(2,1)S(1)}, bf16[2,232,512]{2,1,0:T(8,128)(2,1)S(1)}, u32[]{:S(2)}, u32[]{:S(2)}) collective-permute-start(bf16[2,232,512]{2,1,0:T(8,128)(2,1)S(1)} %collective-permute-done.47.refs_7_), channel_id=1, source_target_pairs={{0,96},{32,0},{64,32},{96,64},{1,97},{33,1},{65,33},{97,65},{2,98}... | collective-permute-start | bytes 1425416 | tf_op jit(solution)/shard_map/ppermute | solution.py:21
  255.7 12.7 %collective-permute-start.50 = (bf16[2,232,512]{2,1,0:T(8,128)(2,1)S(1)}, bf16[2,232,512]{2,1,0:T(8,128)(2,1)S(1)}, u32[]{:S(2)}, u32[]{:S(2)}) collective-permute-start(bf16[2,232,512]{2,1,0:T(8,128)(2,1)S(1)} %collective-permute-done.40.refs_2_), channel_id=1, source_target_pairs={{0,32},{32,64},{64,96},{96,0},{1,33},{33,65},{65,97},{97,1},{2,34}... | collective-permute-start | bytes 1425416 | tf_op jit(solution)/shard_map/ppermute | solution.py:21
  263.0 10.0 %collective-permute-start.49 = (bf16[2,232,512]{2,1,0:T(8,128)(2,1)S(1)}, bf16[2,232,512]{2,1,0:T(8,128)(2,1)S(1)}, u32[]{:S(2)}, u32[]{:S(2)}) collective-permute-start(bf16[2,232,512]{2,1,0:T(8,128)(2,1)S(1)} %collective-permute-done.45.refs_5_), channel_id=1, source_target_pairs={{0,24},{8,0},{16,8},{24,16},{1,25},{9,1},{17,9},{25,17},{2,26},{10... | collective-permute-start | bytes 1425416 | tf_op jit(solution)/shard_map/ppermute | solution.py:21
  263.0 11.3 %collective-permute-start.48 = (bf16[2,232,512]{2,1,0:T(8,128)(2,1)S(1)}, bf16[2,232,512]{2,1,0:T(8,128)(2,1)S(1)}, u32[]{:S(2)}, u32[]{:S(2)}) collective-permute-start(bf16[2,232,512]{2,1,0:T(8,128)(2,1)S(1)} %collective-permute-done.35.refs_0_), channel_id=1, source_target_pairs={{0,8},{8,16},{16,24},{24,0},{1,9},{9,17},{17,25},{25,1},{2,10},{10... | collective-permute-start | bytes 1425416 | tf_op jit(solution)/shard_map/ppermute | solution.py:21
  280.4 6.2 %collective-permute-start.52 = (bf16[128,512]{1,0:T(8,128)(2,1)S(1)}, bf16[128,512]{1,0:T(8,128)(2,1)S(1)}, u32[]{:S(2)}, u32[]{:S(2)}) collective-permute-start(bf16[128,512]{1,0:T(8,128)(2,1)S(1)} %get-tuple-element.52), channel_id=1, source_target_pairs={{0,2},{2,4},{4,6},{6,0},{1,3},{3,5},{5,7},{7,1},{8,10},{10,12},{12... | collective-permute-start | bytes 393224 | tf_op jit(solution)/shard_map/ppermute | solution.py:21
  282.5 5.0 %collective-permute-start.53 = (bf16[128,512]{1,0:T(8,128)(2,1)S(1)}, bf16[128,512]{1,0:T(8,128)(2,1)S(1)}, u32[]{:S(2)}, u32[]{:S(2)}) collective-permute-start(bf16[128,512]{1,0:T(8,128)(2,1)S(1)} %get-tuple-element.53), channel_id=1, source_target_pairs={{0,6},{2,0},{4,2},{6,4},{1,7},{3,1},{5,3},{7,5},{8,14},{10,8},{12,... | collective-permute-start | bytes 393224 | tf_op jit(solution)/shard_map/ppermute | solution.py:21
  283.7 6.5 %collective-permute-start.54 = (bf16[128,512]{1,0:T(8,128)(2,1)S(1)}, bf16[128,512]{1,0:T(8,128)(2,1)S(1)}, u32[]{:S(2)}, u32[]{:S(2)}) collective-permute-start(bf16[128,512]{1,0:T(8,128)(2,1)S(1)} %get-tuple-element.54), channel_id=1, source_target_pairs={{0,4},{2,6},{4,0},{6,2},{1,5},{3,7},{5,1},{7,3},{8,12},{10,14},{12... | collective-permute-start | bytes 393224 | tf_op jit(solution)/shard_map/ppermute | solution.py:21
  (3 other events, 2.6 us)
